TPU v7x, 32 devices: a whole 2x2x4 slice. The times are simulated.
32 devices in a mesh: seq: 16 (over z, y, core), tp: 2 (over x).
Axes of the slice: x: 2, y: 2, z: 4, core: 2. Of those that a mesh axis runs over, the one named last changes fastest.
Arguments:
- queries: bfloat16 [16384, 2048], P('seq', 'tp'), may hold values from -6 to 6
- keys: bfloat16 [16384, 2048], P('seq', 'tp'), may hold values from -6 to 6
- values: bfloat16 [16384, 2048], P('seq', 'tp'), may hold values from -6 to 6
- saved_output: bfloat16 [16384, 2048], P('seq', 'tp'), may hold values from -2 to 2
- grad_output: bfloat16 [16384, 2048], P('seq', 'tp'), may hold values from -6 to 6
- log_norm: float32 [16, 16384], P('tp', 'seq'), as said below
- global_keys: bfloat16 [16, 128, 2048], P('seq', None, 'tp'), may hold values from -6 to 6
- global_values: bfloat16 [16, 128, 2048], P('seq', None, 'tp'), may hold values from -6 to 6
- flow_links: int32 [128, 3], replicated, may hold values from 0 to 127, as said below
- glob_owner: int32 [128], replicated, may hold values from 0 to 15
Outputs:
- grad_queries: bfloat16 [16384, 2048], P('seq', 'tp')
- grad_keys: bfloat16 [16384, 2048], P('seq', 'tp')
- grad_values: bfloat16 [16384, 2048], P('seq', 'tp')
- grad_global_keys: bfloat16 [128, 2048], P(None, 'tp')
- grad_global_values: bfloat16 [128, 2048], P(None, 'tp')
Inputs may be any that keep to these rules, and one draw needn't show every extreme that they name: `flow_links`: the 24 entries of the query blocks of one index of seq name blocks held by any one index of seq at most 2 times, and on every index some holder is named exactly 2 times. `log_norm`: each entry lies within 1 of log(896) + 0.5.
All inputs are finite; a program needn't handle non-finite values.
Results may differ from a plain program's by a relative error of at most 0.0068.
Values may be sent and summed in bfloat16 or wider, within the bound.
No kernel may reach another device: no remote copies, remote signals or barrier semaphores. Data moves between devices by JAX's collectives and lax.ppermute only.
A program may use at most 256 MiB of HBM per device.

v0:
```python
import jax
import jax.numpy as jnp
from jax import lax
from jax.sharding import PartitionSpec as P

HD = 128
BLK = 128
R = 3
G = 128


def extended(block, sides, width):
    for axis, dim in sides:
        count = lax.axis_size(axis)
        forward = [(i, i + 1) for i in range(count - 1)]
        forward.append((count - 1, 0))
        backward = [(target, source) for source, target in forward]
        low = lax.ppermute(
            lax.slice_in_dim(block, block.shape[dim] - width, None, axis=dim), axis, forward
        )
        high = lax.ppermute(lax.slice_in_dim(block, 0, width, axis=dim), axis, backward)
        block = jnp.concatenate([low, block, high], axis=dim)
    return block


def pair_terms(query_rows, grad_rows, norm_rows, delta_rows, key_rows, value_rows, factor, weight):
    scores = (
        jnp.einsum(
            "...qhd,...khd->...hqk", query_rows, key_rows, preferred_element_type=jnp.float32
        )
        * factor
    )
    attend = jnp.exp(scores - norm_rows[..., None])
    if weight is not None:
        attend = attend * weight
    grad_attend = jnp.einsum(
        "...qhd,...khd->...hqk", grad_rows, value_rows, preferred_element_type=jnp.float32
    )
    grad_scores = attend * (grad_attend - delta_rows[..., None])
    attend_low = attend.astype(jnp.bfloat16)
    scores_low = grad_scores.astype(jnp.bfloat16)
    grad_q = factor * jnp.einsum(
        "...hqk,...khd->...qhd", scores_low, key_rows, preferred_element_type=jnp.float32
    )
    grad_k = factor * jnp.einsum(
        "...hqk,...qhd->...khd", scores_low, query_rows, preferred_element_type=jnp.float32
    )
    grad_v = jnp.einsum(
        "...hqk,...qhd->...khd", attend_low, grad_rows, preferred_element_type=jnp.float32
    )
    return (grad_q, grad_k, grad_v)


def slot_view(flow_links, cycle_size, blocks):
    per_device = flow_links.reshape(cycle_size, -1)
    entries = per_device.shape[1]
    target = per_device // blocks
    inside = per_device % blocks
    order = jnp.arange(entries, dtype=jnp.int32)
    earlier = order[None, :] < order[:, None]
    same = target[:, :, None] == target[:, None, :]
    rank = jnp.sum(jnp.logical_and(same, earlier[None]), axis=2)
    query_of = order // R
    return (target, inside, rank, query_of)


def block_onehot(indices, valid, blocks):
    columns = jnp.arange(blocks, dtype=jnp.int32)
    hits = jnp.logical_and(
        indices.reshape(-1)[:, None] == columns[None, :], valid.reshape(-1)[:, None]
    )
    return hits.astype(jnp.bfloat16)


def add_to_blocks(onehot, terms):
    flat = terms.reshape(onehot.shape[0], -1)
    return jnp.einsum("sb,sf->bf", onehot, flat, preferred_element_type=jnp.float32)


def body(
    queries,
    keys,
    values,
    saved_output,
    grad_output,
    log_norm,
    global_keys,
    global_values,
    flow_links,
    glob_owner,
):
    cycle_size = lax.axis_size("seq")
    my_index = lax.axis_index("seq")
    tokens_here, features = queries.shape
    heads_here = features // HD
    blocks = tokens_here // BLK
    factor = HD ** (-0.5)
    entries = blocks * R
    capacity = max(2, (entries + cycle_size - 1) // cycle_size)
    shape_blocks = (blocks, BLK, heads_here, HD)
    query_blocks = queries.reshape(shape_blocks)
    grad_blocks = grad_output.reshape(shape_blocks)
    key_blocks = keys.reshape(shape_blocks)
    value_blocks = values.reshape(shape_blocks)
    product = grad_output.astype(jnp.float32) * saved_output.astype(jnp.float32)
    delta_blocks = jnp.transpose(jnp.sum(product.reshape(shape_blocks), axis=3), (0, 2, 1))
    norm_blocks = jnp.transpose(log_norm.reshape(heads_here, blocks, BLK), (1, 0, 2))
    owned = (glob_owner == my_index)[:, None]
    own_glob_keys = jnp.where(owned, global_keys[0].astype(jnp.float32), 0.0)
    own_glob_vals = jnp.where(owned, global_values[0].astype(jnp.float32), 0.0)
    glob_sum_keys, glob_sum_vals = (
        lax.psum(own_glob_keys.astype(jnp.bfloat16), "seq").astype(jnp.float32),
        lax.psum(own_glob_vals.astype(jnp.bfloat16), "seq").astype(jnp.float32),
    )
    glob_key_now = glob_sum_keys.astype(jnp.bfloat16).reshape(G, heads_here, HD)
    glob_val_now = glob_sum_vals.astype(jnp.bfloat16).reshape(G, heads_here, HD)
    glob_scores = (
        jnp.einsum("bqhd,khd->bhqk", query_blocks, glob_key_now, preferred_element_type=jnp.float32)
        * factor
    )
    glob_attend = jnp.exp(glob_scores - norm_blocks[..., None])
    glob_grad_attend = jnp.einsum(
        "bqhd,khd->bhqk", grad_blocks, glob_val_now, preferred_element_type=jnp.float32
    )
    glob_grad_scores = glob_attend * (glob_grad_attend - delta_blocks[..., None])
    glob_attend_low = glob_attend.astype(jnp.bfloat16)
    glob_scores_low = glob_grad_scores.astype(jnp.bfloat16)
    dq_glob = factor * jnp.einsum(
        "bhqk,khd->bqhd", glob_scores_low, glob_key_now, preferred_element_type=jnp.float32
    )
    dk_glob_part = factor * jnp.einsum(
        "bhqk,bqhd->khd", glob_scores_low, query_blocks, preferred_element_type=jnp.float32
    )
    dv_glob_part = jnp.einsum(
        "bhqk,bqhd->khd", glob_attend_low, grad_blocks, preferred_element_type=jnp.float32
    )
    dk_glob, dv_glob = lax.psum((dk_glob_part, dv_glob_part), "seq")
    wide = extended(jnp.stack([keys, values]), (("seq", 1),), BLK)
    wide_keys = wide[0].reshape(blocks + 2, BLK, heads_here, HD)
    wide_vals = wide[1].reshape(blocks + 2, BLK, heads_here, HD)
    win_keys = jnp.concatenate([wide_keys[:-2], wide_keys[1:-1], wide_keys[2:]], axis=1)
    win_vals = jnp.concatenate([wide_vals[:-2], wide_vals[1:-1], wide_vals[2:]], axis=1)
    dq_win, dk_win, dv_win = pair_terms(
        query_blocks, grad_blocks, norm_blocks, delta_blocks, win_keys, win_vals, factor, None
    )

    def fold(terms):
        parts = terms.reshape(blocks, 3, BLK, heads_here, HD)
        zero = jnp.zeros((1, BLK, heads_here, HD), jnp.float32)
        first = jnp.concatenate([parts[:, 0], zero, zero], axis=0)
        middle = jnp.concatenate([zero, parts[:, 1], zero], axis=0)
        last = jnp.concatenate([zero, zero, parts[:, 2]], axis=0)
        return first + middle + last

    acc_keys = fold(dk_win)
    acc_vals = fold(dv_win)
    rim_keys = jnp.concatenate([acc_keys[0], acc_keys[-1]], axis=0).reshape(2 * BLK, features)
    rim_vals = jnp.concatenate([acc_vals[0], acc_vals[-1]], axis=0).reshape(2 * BLK, features)
    returned = extended(jnp.stack([rim_keys, rim_vals]), (("seq", 1),), BLK)
    own_keys = acc_keys[1:-1].reshape(blocks, BLK, features)
    own_vals = acc_vals[1:-1].reshape(blocks, BLK, features)
    own_keys = own_keys.at[0].add(returned[0, :BLK]).at[blocks - 1].add(returned[0, 3 * BLK :])
    own_vals = own_vals.at[0].add(returned[1, :BLK]).at[blocks - 1].add(returned[1, 3 * BLK :])
    target, inside, rank, query_of = slot_view(flow_links, cycle_size, blocks)
    devices = jnp.arange(cycle_size, dtype=jnp.int32)
    slots = jnp.arange(capacity, dtype=jnp.int32)
    mine_target = target[my_index]
    mine_rank = rank[my_index]
    serve_pick = jnp.logical_and(
        (target == my_index)[:, None, :], rank[:, None, :] == slots[None, :, None]
    )
    serve_valid = jnp.any(serve_pick, axis=2)
    serve_key = jnp.sum(jnp.where(serve_pick, inside[:, None, :], 0), axis=2)
    serve_hot = block_onehot(serve_key, serve_valid, blocks)
    slot_shape = (cycle_size, capacity, BLK, heads_here, HD)
    ask_pick = jnp.logical_and(
        mine_target[None, None, :] == devices[:, None, None],
        mine_rank[None, None, :] == slots[None, :, None],
    )
    ask_valid = jnp.any(ask_pick, axis=2)
    ask_query = jnp.sum(jnp.where(ask_pick, query_of[None, None, :], 0), axis=2)
    ask_hot = block_onehot(ask_query, ask_valid, blocks)
    rows_out = jnp.stack(
        [
            queries.reshape(blocks, BLK, features)[ask_query],
            grad_output.reshape(blocks, BLK, features)[ask_query],
        ],
        axis=2,
    )
    stats_out = jnp.stack([norm_blocks[ask_query], delta_blocks[ask_query]], axis=2)
    rows_in = lax.all_to_all(rows_out, "seq", split_axis=0, concat_axis=0, tiled=True)
    stats_in = lax.all_to_all(stats_out, "seq", split_axis=0, concat_axis=0, tiled=True)
    weight = serve_valid.astype(jnp.float32)[:, :, None, None, None]
    dq_link, dk_link, dv_link = pair_terms(
        rows_in[:, :, 0].reshape(slot_shape),
        rows_in[:, :, 1].reshape(slot_shape),
        stats_in[:, :, 0],
        stats_in[:, :, 1],
        key_blocks[serve_key],
        value_blocks[serve_key],
        factor,
        weight,
    )
    local_terms = jnp.stack(
        [
            dk_link.astype(jnp.bfloat16).reshape(cycle_size, capacity, BLK, features),
            dv_link.astype(jnp.bfloat16).reshape(cycle_size, capacity, BLK, features),
        ],
        axis=2,
    )
    kv_added = add_to_blocks(serve_hot, local_terms).reshape(blocks, 2, BLK, features)
    dq_back = lax.all_to_all(
        dq_link.astype(jnp.bfloat16), "seq", split_axis=0, concat_axis=0, tiled=True
    )
    dq_added = add_to_blocks(ask_hot, dq_back)
    total_q = (dq_win + dq_glob).reshape(blocks, BLK * features) + dq_added
    grad_queries = total_q.astype(jnp.bfloat16).reshape(tokens_here, features)
    grad_keys = (own_keys + kv_added[:, 0]).astype(jnp.bfloat16).reshape(tokens_here, features)
    grad_values = (own_vals + kv_added[:, 1]).astype(jnp.bfloat16).reshape(tokens_here, features)
    grad_global_keys = dk_glob.astype(jnp.bfloat16).reshape(G, features)
    grad_global_values = dv_glob.astype(jnp.bfloat16).reshape(G, features)
    return (grad_queries, grad_keys, grad_values, grad_global_keys, grad_global_values)


def solution(mesh):
    return jax.shard_map(
        body,
        mesh=mesh,
        in_specs=(
            P("seq", "tp"),
            P("seq", "tp"),
            P("seq", "tp"),
            P("seq", "tp"),
            P("seq", "tp"),
            P("tp", "seq"),
            P("seq", None, "tp"),
            P("seq", None, "tp"),
            P(),
            P(),
        ),
        out_specs=(P("seq", "tp"), P("seq", "tp"), P("seq", "tp"), P(None, "tp"), P(None, "tp")),
        check_vma=False,
    )
```

profile of v0, /device:TPU:15, one launch (start us, length us, event | category | flops | bytes accessed | tf_op | source)
XLA Modules:
  0.0 1026.2 jit_solution(11833871854781932651)
XLA Ops:
  31.6 12.3 %copy.258 = bf16[16,2,1,128,1024]{3,4,1,2,0:T(8,128)(2,1)} copy(bf16[16,2,1,128,1024]{4,3,1,0,2:T(8,128)(2,1)} %bitcast.248) | data formatting | bytes 16777216 | tf_op jit(solution)/shard_map/stack | solution.py:183
  50.5 12.2 %copy.257 = bf16[16,2,1,128,1024]{3,4,1,2,0:T(8,128)(2,1)} copy(bf16[16,2,1,128,1024]{4,3,1,0,2:T(8,128)(2,1)} %bitcast.246) | data formatting | bytes 16777216 | tf_op jit(solution)/shard_map/stack | solution.py:183
  62.7 13.8 %pad_maximum_fusion = bf16[16,2,2,128,1024]{3,4,1,2,0:T(8,128)(2,1)} fusion(bf16[16,2,1,128,1024]{3,4,1,2,0:T(8,128)(2,1)} %copy.258, bf16[16,2,1,128,1024]{3,4,1,2,0:T(8,128)(2,1)} %copy.257), kind=kLoop, calls=%fused_computation.8 | loop fusion | flops 8388608 | bytes 33554432 | tf_op jit(solution)/shard_map/stack | solution.py:183
  118.0 12.8 %copy.267 = bf16[16,2,128,8,128]{2,4,3,1,0:T(8,128)(2,1)} copy(bf16[16,2,128,8,128]{4,3,2,1,0:T(8,128)(2,1)} %bitcast.247) | data formatting | bytes 16777216 | tf_op jit(solution)/shard_map/gather | solution.py:199
  130.8 305.5 %all-reduce.9.cloned.1.call-done = (bf16[128,8,128]{2,0,1:T(8,128)(2,1)}, bf16[128,8,128]{2,0,1:T(8,128)(2,1)}) async-done(((bf16[128,8,128]{2,0,1:T(8,128)(2,1)}, bf16[128,8,128]{2,0,1:T(8,128)(2,1)}), (bf16[128,8,128]{2,0,1:T(8,128)(2,1)}, bf16[128,8,128]{2,0,1:T(8,128)(2,1)})) %all-reduce.9.cloned.1.call-update) | async-done | bytes 524304 | tf_op jit(solution)/shard_map/psum | solution.py:112
  444.5 75.9 %all-reduce.10 = (bf16[128,8,128]{2,0,1:T(8,128)(2,1)}, bf16[128,8,128]{2,0,1:T(8,128)(2,1)S(1)}) all-reduce(f32[128,8,128]{2,0,1:T(8,128)} %fusion.70, f32[128,8,128]{2,0,1:T(8,128)S(1)} %fusion.62), channel_id=1, replica_groups=mesh['seq'=16,'tp'=2] {'seq'}, use_global_device_ids=true, to_apply=%region_8.9 | all-reduce | flops 262144 | bytes 1572864 | tf_op jit(solution)/shard_map/psum | solution.py:137
  538.0 11.6 %fusion.96 = (bf16[16,2,1,128,1024]{3,4,1,2,0:T(8,128)(2,1)}, bf16[16,2,1,128,1024]{3,4,1,2,0:T(8,128)(2,1)}) fusion(bf16[16,2,2,128,1024]{3,4,1,2,0:T(8,128)(2,1)} %all-to-all-done), kind=kLoop, calls=%fused_computation.159 | loop fusion | bytes 33554432 | tf_op jit(solution)/shard_map/slice | solution.py:196
  549.6 14.4 %fusion.101 = f32[16,2,8,128,128]{4,3,2,1,0:T(8,128)} fusion(bf16[16,2,128,8,128]{2,4,3,1,0:T(8,128)(2,1)} %bitcast.220, bf16[16,2,128,8,128]{2,4,3,1,0:T(8,128)(2,1)} %copy.267), kind=kOutput, calls=%fused_computation.164 | convolution fusion | flops 1073741824 | bytes 33554432 | tf_op jit(solution)/shard_map/...qhd,...khd->...hqk/dot_general | solution.py:28
  564.0 18.1 %multiply_convert_fusion.2 = bf16[16,2,8,128,128]{4,3,2,1,0:T(8,128)(2,1)S(1)} fusion(f32[16,2,8,128,128]{4,3,2,1,0:T(8,128)} %fusion.101, f32[16,2,8,128]{3,2,1,0:T(8,128)S(1)} %get-tuple-element.112, f32[16,2]{1,0:T(8,128)S(1)} %copy.263, f32[16,2,8,128]{3,2,1,0:T(8,128)S(1)} %get-tuple-element.111, bf16[16,2,128,8,128]{2,4,3,1,0:T(8,128)(2,1)} %bitcast.239, ...), kind=kOutput, calls=%fused_computation.14 | convolution fusion | flops 1098907648 | bytes 42205312 | tf_op jit(solution)/shard_map/...qhd,...khd->...hqk/dot_general | solution.py:36
  585.4 10.3 fusion.7
  595.6 20.5 %all-to-all-start.2 = ((bf16[16,2,128,8,128]{2,4,3,1,0:T(8,128)(2,1)}), bf16[16,2,128,8,128]{2,4,3,1,0:T(8,128)(2,1)}, u32[]{:S(2)}, u32[]{:S(2)}) async-start(bf16[16,2,128,8,128]{2,4,3,1,0:T(8,128)(2,1)} %fusion.7), calls=%async_computation.2 | async-start | bytes 16777216 | tf_op jit(solution)/shard_map/all_to_all | solution.py:212
  620.3 9.3 fusion.57
  629.6 11.3 %fusion.16 = f32[8,8,384,128]{3,2,1,0:T(8,128)} fusion(f32[8,8,384,128]{3,2,1,0:T(8,128)} %fusion.57, f32[8,8,128]{2,1,0:T(8,128)S(1)} %bitcast.282, bf16[8,128,8,128]{3,2,1,0:T(8,128)(2,1)S(1)} %bitcast.260), kind=kOutput, calls=%fused_computation.32 | convolution fusion | flops 814743552 | bytes 27295744 | tf_op jit(solution)/shard_map/...hqk,...qhd->...khd/dot_general | solution.py:48
  640.9 9.9 slice_bitcast_fusion.4
  650.8 9.4 multiply_convert_fusion.3
  660.2 9.1 broadcast_multiply_fusion
  669.4 9.9 slice_bitcast_fusion.7
  680.1 11.8 %fusion.31 = (f32[10,128,8,128]{3,1,2,0:T(8,128)S(1)}, f32[10,128,8,128]{3,1,2,0:T(8,128)}) fusion(f32[1,128,8,128]{3,1,2,0:T(8,128)} %broadcast.296, f32[8,128,8,128]{3,1,2,0:T(8,128)} %get-tuple-element.83, f32[8,128,8,128]{3,1,2,0:T(8,128)} %get-tuple-element.82, f32[8,128,8,128]{3,1,2,0:T(8,128)S(1)} %copy-done.11, ...), kind=kLoop, calls=%fused_computation.45 | loop fusion | flops 10485760 | bytes 36175872 | tf_op jit(solution)/shard_map/add | solution.py:153
  735.3 72.6 %collective-permute-done.2 = f32[2,128,1024]{2,0,1:T(2,128)} collective-permute-done((f32[2,128,1024]{2,0,1:T(2,128)}, f32[2,128,1024]{2,0,1:T(2,128)}, u32[]{:S(2)}, u32[]{:S(2)}) %collective-permute-start.2) | collective-permute-done | bytes 1048608 | tf_op jit(solution)/shard_map/ppermute | solution.py:18
  810.9 11.0 %scatter-add.16 = f32[8,128,1024]{2,0,1:T(8,128)} dynamic-update-slice(f32[8,128,1024]{2,0,1:T(8,128)} %bitcast.251, f32[1,128,1024]{2,0,1:T(1,128)S(1)} %get-tuple-element.107, s32[]{:T(128)} %constant.146.clone.1, s32[]{:T(128)} %constant.146.clone.1, s32[]{:T(128)} %constant.146.clone.1) | dynamic-update-slice | bytes 1048580 | tf_op jit(solution)/shard_map/scatter-add | solution.py:163
  821.9 10.9 %scatter-add.14 = f32[8,128,1024]{2,0,1:T(8,128)} dynamic-update-slice(f32[8,128,1024]{2,0,1:T(8,128)} %bitcast.250, f32[1,128,1024]{2,0,1:T(1,128)S(1)} %get-tuple-element.108, s32[]{:T(128)} %constant.146.clone.1, s32[]{:T(128)} %constant.146.clone.1, s32[]{:T(128)} %constant.146.clone.1) | dynamic-update-slice | bytes 1048580 | tf_op jit(solution)/shard_map/scatter-add | solution.py:162
  838.4 11.0 %scatter-add.19 = f32[8,128,1024]{2,0,1:T(8,128)} dynamic-update-slice(f32[8,128,1024]{2,0,1:T(8,128)} %scatter-add.16, f32[1,128,1024]{2,0,1:T(1,128)S(1)} %get-tuple-element.105, s32[]{:T(128)} %constant.147.clone.1, s32[]{:T(128)} %constant.146.clone.1, s32[]{:T(128)} %constant.146.clone.1) | dynamic-update-slice | bytes 1048580 | tf_op jit(solution)/shard_map/scatter-add | solution.py:163
  849.4 10.9 %scatter-add.15 = f32[8,128,1024]{2,0,1:T(8,128)} dynamic-update-slice(f32[8,128,1024]{2,0,1:T(8,128)} %scatter-add.14, f32[1,128,1024]{2,0,1:T(1,128)S(1)} %get-tuple-element.106, s32[]{:T(128)} %constant.147.clone.1, s32[]{:T(128)} %constant.146.clone.1, s32[]{:T(128)} %constant.146.clone.1) | dynamic-update-slice | bytes 1048580 | tf_op jit(solution)/shard_map/scatter-add | solution.py:162
  860.4 13.0 %fusion.13 = bf16[16,2,8,128,128]{4,3,2,1,0:T(8,128)(2,1)} fusion(bf16[16,2,128,8,128]{2,4,3,1,0:T(8,128)(2,1)} %bitcast.240, f32[16,2,8,128,128]{4,3,2,1,0:T(8,128)} %fusion.101, f32[16,2]{1,0:T(8,128)S(1)} %copy.263, f32[16,2,8,128]{3,2,1,0:T(8,128)S(1)} %get-tuple-element.111), kind=kOutput, calls=%fused_computation.31 | convolution fusion | flops 1094713344 | bytes 33685632 | tf_op jit(solution)/shard_map/...hqk,...qhd->...khd/dot_general | solution.py:48
  873.4 12.3 %copy.284 = bf16[16,2,1,128,1024]{4,3,2,1,0:T(8,128)(2,1)} copy(bf16[16,2,1,128,1024]{3,4,1,0,2:T(8,128)(2,1)} %bitcast.237) | data formatting | bytes 16777216 | tf_op jit(solution)/shard_map/stack;reshape | solution.py:204
  885.7 11.4 %multiply_convert_fusion = bf16[16,2,8,128,128]{4,3,2,1,0:T(8,128)(2,1)} fusion(bf16[16,2,128,8,128]{2,4,3,1,0:T(8,128)(2,1)} %bitcast.221, bf16[16,2,8,128,128]{4,3,2,1,0:T(8,128)(2,1)} %copy-done.2), kind=kOutput, calls=%fused_computation.12 | convolution fusion | flops 1082130432 | bytes 25165824 | tf_op jit(solution)/shard_map/...hqk,...qhd->...khd/dot_general | solution.py:45
  897.1 12.2 %copy.283 = bf16[16,2,1,128,1024]{4,3,2,1,0:T(8,128)(2,1)} copy(bf16[16,2,1,128,1024]{3,4,1,0,2:T(8,128)(2,1)} %bitcast.238) | data formatting | bytes 16777216 | tf_op jit(solution)/shard_map/stack;reshape | solution.py:204
  909.3 13.7 %pad_maximum_fusion.1 = bf16[16,2,2,128,1024]{4,3,2,1,0:T(8,128)(2,1)} fusion(bf16[16,2,1,128,1024]{4,3,2,1,0:T(8,128)(2,1)} %copy.284, bf16[16,2,1,128,1024]{4,3,2,1,0:T(8,128)(2,1)} %copy.283), kind=kLoop, calls=%fused_computation.9 | loop fusion | flops 8388608 | bytes 33554432 | tf_op jit(solution)/shard_map/stack | solution.py:204
  923.1 14.9 %reshape.432 = bf16[32,262144]{1,0:T(8,128)(2,1)} reshape(bf16[16,2,2,128,1024]{4,3,2,1,0:T(8,128)(2,1)} %pad_maximum_fusion.1) | data formatting | bytes 33554432 | tf_op jit(solution)/shard_map/reshape | solution.py:76
  938.0 18.7 %copy.323 = bf16[4,8,256,1024]{3,2,1,0:T(8,128)(2,1)} copy(bf16[4,8,256,1024]{3,1,2,0:T(8,128)(2,1)} %bitcast.230) | data formatting | bytes 33554432
  956.7 17.0 %fusion.1 = f32[8,2,128,1024]{3,0,2,1:T(8,128)S(1)} fusion(bf16[2,128,1024,32]{2,1,0,3:T(8,128)(2,1)} %bitcast.229, s32[32]{0:T(128)S(1)} %copy-done.25, pred[32]{0:T(512)(128)(4,1)S(1)} %copy-done.24), kind=kOutput, calls=%fused_computation.10 | convolution fusion | flops 134218240 | bytes 25165984 | tf_op jit(solution)/shard_map/sb,sf->bf/dot_general | solution.py:77
  987.5 12.7 %copy.268 = bf16[16,2,128,8,128]{4,3,2,1,0:T(8,128)(2,1)} copy(bf16[16,2,128,8,128]{2,4,3,1,0:T(8,128)(2,1)} %all-to-all-done.2) | data formatting | bytes 16777216 | tf_op jit(solution)/shard_map/all_to_all | solution.py:212
  (182 shorter events, 190.9 us)
Async XLA Ops:
  13.4 13.2 %copy-start = (bf16[1024,1024]{1,0:T(8,128)(2,1)S(1)}, bf16[1024,1024]{1,0:T(8,128)(2,1)}, u32[]{:S(2)}) copy-start(bf16[1024,1024]{1,0:T(8,128)(2,1)} %param.22) | copy-start | bytes 6291460
  20.0 56.5 %all-to-all-start.1 = ((f32[16,2,2,8,128]{4,3,1,2,0:T(8,128)}), f32[16,2,2,8,128]{4,3,1,2,0:T(8,128)S(1)}, u32[]{:S(2)}, u32[]{:S(2)}) async-start(f32[16,2,2,8,128]{4,3,1,2,0:T(8,128)} %pad_maximum_fusion.12), calls=%async_computation.1 | async-start | bytes 524288 | tf_op jit(solution)/shard_map/all_to_all | solution.py:192
  76.5 6.3 copy-start.23
  76.5 8.9 copy-start.28
  76.5 461.5 %all-to-all-start = ((bf16[16,2,2,128,1024]{3,4,1,2,0:T(8,128)(2,1)}), bf16[16,2,2,128,1024]{3,4,1,2,0:T(8,128)(2,1)}, u32[]{:S(2)}, u32[]{:S(2)}) async-start(bf16[16,2,2,128,1024]{3,4,1,2,0:T(8,128)(2,1)} %pad_maximum_fusion), calls=%async_computation | async-start | bytes 33554432 | tf_op jit(solution)/shard_map/all_to_all | solution.py:191
  82.7 353.6 %all-reduce.9.cloned.1.call-start = ((), (), s32[]{:S(2)}) async-start(), calls=%async_computation.3 | async-start | bytes 1048576 | tf_op jit(solution)/shard_map/psum | solution.py:112
  92.1 431.4 %collective-permute-start.1 = (bf16[2,128,1024]{2,1,0:T(8,128)(2,1)}, bf16[2,128,1024]{2,1,0:T(8,128)(2,1)}, u32[]{:S(2)}, u32[]{:S(2)}) collective-permute-start(bf16[2,128,1024]{2,1,0:T(8,128)(2,1)} %get-tuple-element.101), channel_id=1, source_target_pairs={{2,0},{4,2},{6,4},{8,6},{10,8},{12,10},{14,12},{16,14},{18,16},{20... | collective-permute-start | bytes 1572872 | tf_op jit(solution)/shard_map/ppermute | solution.py:21
  92.5 431.0 %collective-permute-start = (bf16[2,128,1024]{2,1,0:T(8,128)(2,1)}, bf16[2,128,1024]{2,1,0:T(8,128)(2,1)}, u32[]{:S(2)}, u32[]{:S(2)}) collective-permute-start(bf16[2,128,1024]{2,1,0:T(8,128)(2,1)} %get-tuple-element.102), channel_id=1, source_target_pairs={{0,2},{2,4},{4,6},{6,8},{8,10},{10,12},{12,14},{14,16},{16,18},{18... | collective-permute-start | bytes 1572872 | tf_op jit(solution)/shard_map/ppermute | solution.py:18
  101.2 3.3 copy-start.5
  582.1 3.3 copy-start.2
  595.6 391.8 %all-to-all-start.2 = ((bf16[16,2,128,8,128]{2,4,3,1,0:T(8,128)(2,1)}), bf16[16,2,128,8,128]{2,4,3,1,0:T(8,128)(2,1)}, u32[]{:S(2)}, u32[]{:S(2)}) async-start(bf16[16,2,128,8,128]{2,4,3,1,0:T(8,128)(2,1)} %fusion.7), calls=%async_computation.2 | async-start | bytes 16777216 | tf_op jit(solution)/shard_map/all_to_all | solution.py:212
  616.2 4.1 copy-start.4
  620.3 9.3 copy-start.10
  640.9 10.0 copy-start.19
  669.3 10.7 %copy-start.11 = (f32[8,128,8,128]{3,1,2,0:T(8,128)S(1)}, f32[8,128,8,128]{3,1,2,0:T(8,128)}, u32[]{:S(2)}) copy-start(f32[8,128,8,128]{3,1,2,0:T(8,128)} %get-tuple-element.81) | copy-start | bytes 12582916
  669.3 34.2 %slice-start.2 = ((s8[6291456]{0:T(1024)(128)(4,1)}), s8[2097152]{0:T(1024)(128)(4,1)S(1)}, s32[]{:S(2)}) async-start(s8[6291456]{0:T(1024)(128)(4,1)} %bitcast.244), calls=%async_computation.6 | async-start | bytes 4194304
  680.1 23.5 %slice-start.3 = ((s8[6291456]{0:T(1024)(128)(4,1)}), s8[4194304]{0:T(1024)(128)(4,1)S(1)}, s32[]{:S(2)}) async-start(s8[6291456]{0:T(1024)(128)(4,1)} %bitcast.244), calls=%async_computation.7 | async-start | bytes 8388608
  691.8 3.8 copy-start.6
  695.6 7.9 slice-start
  696.9 6.7 slice-start.1
  700.9 132.0 %collective-permute-start.3 = (f32[2,128,1024]{2,0,1:T(2,128)}, f32[2,128,1024]{2,0,1:T(2,128)}, u32[]{:S(2)}, u32[]{:S(2)}) collective-permute-start(f32[2,128,1024]{2,0,1:T(2,128)} %get-tuple-element.103), channel_id=1, source_target_pairs={{2,0},{4,2},{6,4},{8,6},{10,8},{12,10},{14,12},{16,14},{18,16},{20... | collective-permute-start | bytes 3145736 | tf_op jit(solution)/shard_map/ppermute | solution.py:21
  701.2 106.7 %collective-permute-start.2 = (f32[2,128,1024]{2,0,1:T(2,128)}, f32[2,128,1024]{2,0,1:T(2,128)}, u32[]{:S(2)}, u32[]{:S(2)}) collective-permute-start(f32[2,128,1024]{2,0,1:T(2,128)} %get-tuple-element.104), channel_id=1, source_target_pairs={{0,2},{2,4},{4,6},{6,8},{8,10},{10,12},{12,14},{14,16},{16,18},{18... | collective-permute-start | bytes 3145736 | tf_op jit(solution)/shard_map/ppermute | solution.py:18
  710.2 4.8 copy-start.16
  710.2 4.8 copy-start.21
  723.5 6.8 copy-start.12
  730.3 4.4 copy-start.18
  730.3 4.7 copy-start.17
  938.0 18.7 %copy-start.24 = (pred[32]{0:T(512)(128)(4,1)S(1)}, pred[32]{0:T(512)(128)(4,1)}, u32[]{:S(2)}) copy-start(pred[32]{0:T(512)(128)(4,1)} %and.122) | copy-start | bytes 100
  938.0 18.7 %copy-start.25 = (s32[32]{0:T(128)S(1)}, s32[32]{0:T(128)}, u32[]{:S(2)}) copy-start(s32[32]{0:T(128)} %eq.133) | copy-start | bytes 388
  980.8 4.2 copy-start.13
  1000.2 8.9 copy-start.26
  1000.2 8.9 copy-start.27
  (9 other events, 18.4 us)
Sparse Core Ops, SparseCore 0:
  90.0 346.2 all-reduce.8
where the time goes:
time: 1040 us; the launch traced here: 1030 us
  waiting for transfers between devices  378 us (36%)
  local copies, waits for them, and re-layouts  304 us (29%)
  matrix products  143 us (14%)
  blocking collectives  75.9 us (7%)
  other arithmetic  71.9 us (7%)
  starting transfers between devices  39.1 us (4%)
  between operations  14.7 us (1%)
    psum x1, waiting for transfers between devices, body(): lax.psum(own_glob_keys.astype(jnp.bfloat16), 'seq').astype(jnp.float32)  306 us
    psum x1, blocking collectives, body(): dk_glob, dv_glob = lax.psum((dk_glob_part, dv_glob_part), 'seq')  75.9 us
    ppermute x2, waiting for transfers between devices, extended(): lax.ppermute(lax.slice_in_dim(block, block.shape[dim] - width, None, axis...  72.6 us
    unnamed x83, local copies, waits for them, and re-layouts  43.3 us
    dot_general x2, matrix products, pair_terms(): jnp.einsum('...qhd,...khd->...hqk', grad_rows, value_rows, preferred_elem...  27.5 us
    dot_general x2, matrix products, add_to_blocks(): jnp.einsum('sb,sf->bf', onehot, flat, preferred_element_type=jnp.float32)  24.8 us
    another operation x2, local copies, waits for them, and re-layouts, body(): jnp.stack([dk_link.astype(jnp.bfloat16).reshape(cycle_size, capacity, BLK...  24.5 us
    another operation x2, local copies, waits for them, and re-layouts, body(): jnp.stack([queries.reshape(blocks, BLK, features)[ask_query], grad_output...  24.5 us
  transfers between devices with their start and end apart: 8, of which 2 were waited for; matrix products, arithmetic and copies ran while one was open for 40% of the time, Pallas kernels for 0%

commit v1 on v0

v1 whole, which is shorter than its diff:
```python
import functools
import math

import jax
import jax.numpy as jnp
from jax import lax
from jax.experimental import pallas as pl
from jax.experimental.pallas import tpu as pltpu
from jax.sharding import PartitionSpec as P

HD = 128
BLK = 128
R = 3
G = 128
W = 3
FACTOR = HD ** (-0.5)
LOG2E = math.log2(math.e)
STAGE = 4


def pair_kernel(left_ref, right_ref, out_ref):
    heads = out_ref.shape[0]
    for head in range(heads):
        cols = slice(head * HD, (head + 1) * HD)
        out_ref[head, 0, :, :HD] = left_ref[:, cols]
        out_ref[head, 0, :, HD:] = right_ref[:, cols]


def pair_heads(left, right, share):
    tokens, features = left.shape
    heads = features // HD
    part = tokens // share
    rows = min(256, part)
    steps = part // rows
    out = pl.pallas_call(
        pair_kernel,
        grid=(share, steps),
        in_specs=[pl.BlockSpec((rows, features), lambda s, t: (s * steps + t, 0))] * 2,
        out_specs=pl.BlockSpec((heads, 1, rows, 2 * HD), lambda s, t: (0, s, t, 0)),
        out_shape=jax.ShapeDtypeStruct((heads, share, part, 2 * HD), left.dtype),
        cost_estimate=pl.CostEstimate(
            flops=0, bytes_accessed=4 * tokens * features * 2, transcendentals=0
        ),
    )(left, right)
    return out.reshape(heads * share, part, 2 * HD)


def unpair_kernel(in_ref, *out_refs):
    heads = in_ref.shape[0]
    for head in range(heads):
        cols = slice(head * HD, (head + 1) * HD)
        for which, out_ref in enumerate(out_refs):
            out_ref[:, cols] = in_ref[head, 0, :, which * HD : (which + 1) * HD]


def unpair_heads(mixed, share):
    parts, part, width = mixed.shape
    heads = parts // share
    count = width // HD
    rows = min(256, part)
    steps = part // rows
    shape = jax.ShapeDtypeStruct((share * part, heads * HD), mixed.dtype)
    return pl.pallas_call(
        unpair_kernel,
        grid=(share, steps),
        in_specs=[pl.BlockSpec((heads, 1, rows, width), lambda s, t: (0, s, t, 0))],
        out_specs=[pl.BlockSpec((rows, heads * HD), lambda s, t: (s * steps + t, 0))] * count,
        out_shape=[shape] * count,
        cost_estimate=pl.CostEstimate(
            flops=0, bytes_accessed=4 * parts * part * width, transcendentals=0
        ),
    )(mixed.reshape(heads, share, part, width))


def attention_kernel(
    table_ref, stats_ref, pair_ref, kv_ref, glob_ref, dq_ref, dkv_ref, dglob_ref, acc, stage, sems
):
    count, tile, _ = pair_ref.shape
    total = acc.shape[0]
    kinds = (W + R) * (BLK // tile)

    def clear(block, carry):
        acc[block] = jnp.zeros((tile, 2 * HD), jnp.float32)
        return carry

    lax.fori_loop(0, total, clear, 0)
    dglob_ref[...] = jnp.zeros_like(dglob_ref)
    zero = jnp.zeros((tile, HD), jnp.bfloat16)

    def one_block(block, carry):
        pair = pair_ref[block]
        mixed = jnp.concatenate(
            [
                jnp.concatenate([pair[:, :HD], zero], axis=1),
                jnp.concatenate([zero, pair[:, HD:]], axis=1),
            ],
            axis=0,
        )
        stats = stats_ref[block]
        norm = stats[0:1] * LOG2E
        delta = stats[1:2]
        places = [table_ref[block * kinds + kind] for kind in range(kinds)]
        rows = jnp.concatenate([kv_ref[place] for place in places] + [glob_ref[...]], axis=0)
        both = lax.dot_general(
            rows, mixed, (((1,), (1,)), ((), ())), preferred_element_type=jnp.float32
        )
        attend = jnp.exp2(both[:, :tile] * (FACTOR * LOG2E) - norm)
        grad_scores = attend * (both[:, tile:] - delta)
        attend_low = attend.astype(jnp.bfloat16)
        scores_low = grad_scores.astype(jnp.bfloat16)
        grad_kv = jnp.dot(
            jnp.concatenate([scores_low, attend_low], axis=1),
            mixed,
            preferred_element_type=jnp.float32,
        )
        for kind, place in enumerate(places):
            acc[place] += grad_kv[kind * tile : (kind + 1) * tile]
        dglob_ref[...] += grad_kv[kinds * tile :]
        grad_q = lax.dot_general(
            scores_low, rows[:, :HD], (((0,), (0,)), ((), ())), preferred_element_type=jnp.float32
        )
        dq_ref[block] = (grad_q * FACTOR).astype(jnp.bfloat16)
        return carry

    lax.fori_loop(0, count, one_block, 0)
    dglob_ref[:, :HD] = dglob_ref[:, :HD] * FACTOR

    def copy_out(step, slot):
        return pltpu.make_async_copy(
            stage.at[slot], dkv_ref.at[pl.ds(step * STAGE, STAGE)], sems.at[slot]
        )

    steps = total // STAGE
    for step in range(steps):
        slot = step % 2
        if step >= 2:
            copy_out(step - 2, slot).wait()
        part = acc[step * STAGE : (step + 1) * STAGE]
        stage[slot, :, :, :HD] = (part[:, :, :HD] * FACTOR).astype(jnp.bfloat16)
        stage[slot, :, :, HD:] = part[:, :, HD:].astype(jnp.bfloat16)
        copy_out(step, slot).start()
    for step in range(max(0, steps - 2), steps):
        copy_out(step, step % 2).wait()


def attention(table, stats, pairs, kv, glob):
    count, tile, _ = pairs.shape
    total = kv.shape[0]
    vmem = pl.BlockSpec(memory_space=pltpu.VMEM)
    return pl.pallas_call(
        attention_kernel,
        in_specs=[pl.BlockSpec(memory_space=pltpu.SMEM), vmem, vmem, vmem, vmem],
        out_specs=[vmem, pl.BlockSpec(memory_space=pl.ANY), vmem],
        out_shape=[
            jax.ShapeDtypeStruct((count, tile, HD), jnp.bfloat16),
            jax.ShapeDtypeStruct((total, tile, 2 * HD), jnp.bfloat16),
            jax.ShapeDtypeStruct((G, 2 * HD), jnp.float32),
        ],
        scratch_shapes=[
            pltpu.VMEM((total, tile, 2 * HD), jnp.float32),
            pltpu.VMEM((2, STAGE, tile, 2 * HD), jnp.bfloat16),
            pltpu.SemaphoreType.DMA((2,)),
        ],
        compiler_params=pltpu.CompilerParams(vmem_limit_bytes=60 * 1024 * 1024),
        cost_estimate=pl.CostEstimate(
            flops=count * (W + R + 1) * 10 * tile * BLK * HD,
            bytes_accessed=(total * 8 + count * 6) * tile * HD,
            transcendentals=count * (W + R + 1) * tile * BLK,
        ),
    )(table, stats, pairs, kv, glob)


def exchange(array):
    return lax.all_to_all(array, "seq", split_axis=0, concat_axis=0, tiled=True)


def to_mate(array, step, share):
    size = lax.axis_size("seq")
    return lax.ppermute(
        array, "seq", [(i, i - i % share + (i + step) % share) for i in range(size)]
    )


def body(
    queries,
    keys,
    values,
    saved_output,
    grad_output,
    log_norm,
    global_keys,
    global_values,
    flow_links,
    glob_owner,
):
    size = lax.axis_size("seq")
    tokens, features = queries.shape
    heads = features // HD
    blocks = tokens // BLK
    share = size // heads
    part = tokens // share
    tile = min(BLK, part)
    sub = part // tile
    pieces = BLK // tile
    count = size * sub
    mine = lax.axis_index("seq") % share

    kv_own = exchange(pair_heads(keys, values, share))
    glob_pair = jnp.concatenate(
        [global_keys.reshape(G, heads, HD), global_values.reshape(G, heads, HD)], axis=2
    )
    glob_out = jnp.repeat(jnp.transpose(glob_pair, (1, 0, 2)), share, axis=0)
    glob_in = exchange(glob_out)
    product = grad_output.astype(jnp.float32) * saved_output.astype(jnp.float32)
    delta = jnp.sum(product.reshape(tokens, heads, HD), axis=2).T
    stats_out = jnp.stack(
        [log_norm.reshape(size, part), delta.reshape(size, part)], axis=1
    )
    stats_in = exchange(stats_out)
    pairs = exchange(pair_heads(queries, grad_output, share))

    owners = jnp.arange(size, dtype=jnp.int32)[:, None] == glob_owner[None, :]
    glob_now = jnp.sum(
        jnp.where(owners[:, :, None], glob_in.astype(jnp.float32), 0.0), axis=0
    ).astype(jnp.bfloat16)
    stats = jnp.transpose(stats_in.reshape(size, 2, sub, tile), (0, 2, 1, 3)).reshape(
        count, 2, tile
    )
    kv = jnp.concatenate(
        [kv_own] + [to_mate(kv_own, share - step, share) for step in range(1, share)], axis=0
    ).reshape(share * count, tile, 2 * HD)

    order = jnp.arange(count, dtype=jnp.int32)
    my_blocks = (order // sub) * blocks + (mine * sub + order % sub) // pieces
    near = my_blocks[:, None] + jnp.arange(-1, 2, dtype=jnp.int32)[None, :]
    wanted = jnp.concatenate(
        [(near + size * blocks) % (size * blocks), flow_links[my_blocks]], axis=1
    )
    within = (wanted % blocks)[:, :, None] * pieces + jnp.arange(pieces, dtype=jnp.int32)
    offset = (within // sub - mine + share) % share
    table = offset * count + (wanted // blocks)[:, :, None] * sub + within % sub

    dq, dkv, dglob = attention(
        table.reshape(-1).astype(jnp.int32),
        stats,
        pairs.reshape(count, tile, 2 * HD),
        kv,
        glob_now,
    )
    dq_back = exchange(dq.reshape(size, part, HD))
    dkv = dkv.reshape(share, size, part, 2 * HD)
    dkv_sum = dkv[0].astype(jnp.float32)
    for step in range(1, share):
        dkv_sum = dkv_sum + to_mate(dkv[step], step, share).astype(jnp.float32)
    dkv_back = exchange(dkv_sum.astype(jnp.bfloat16))
    glob_parts = lax.all_gather(dglob, "seq", axis=0, tiled=False)
    glob_sum = jnp.sum(glob_parts.reshape(heads, share, G, 2, HD), axis=1)
    glob_grads = jnp.transpose(glob_sum, (2, 1, 0, 3)).reshape(2, G, features).astype(jnp.bfloat16)

    (grad_queries,) = unpair_heads(dq_back, share)
    grad_keys, grad_values = unpair_heads(dkv_back, share)
    return (grad_queries, grad_keys, grad_values, glob_grads[0], glob_grads[1])


def solution(mesh):
    return jax.shard_map(
        body,
        mesh=mesh,
        in_specs=(
            P("seq", "tp"),
            P("seq", "tp"),
            P("seq", "tp"),
            P("seq", "tp"),
            P("seq", "tp"),
            P("tp", "seq"),
            P("seq", None, "tp"),
            P("seq", None, "tp"),
            P(),
            P(),
        ),
        out_specs=(P("seq", "tp"), P("seq", "tp"), P("seq", "tp"), P(None, "tp"), P(None, "tp")),
        check_vma=False,
    )
```

time: 1040 us -> 499 us (0.48); the launches traced: 1030 us -> 498 us
  local copies, waits for them, and re-layouts: 304 us -> 19.7 us
  matrix products: 143 us -> 0 us
  Pallas kernels: 0 us -> 78.8 us
  blocking collectives: 75.9 us -> 0 us
  waiting for transfers between devices: 378 us -> 326 us
  other arithmetic: 71.9 us -> 25.2 us
    psum x1 -> x0, waiting for transfers between devices: 306 us -> none  [body(): lax.psum(own_glob_keys.astype(jnp.bfloat16), 'seq').astype(jnp.float32)]
    all_to_all x3 -> x6, waiting for transfers between devices: 0.01 us -> 236 us  [exchange(): return lax.all_to_all(array, 'seq', split_axis=0, concat_axis=0, tiled=True)]
    dot_general x17 -> x0, matrix products: 143 us -> none  [the longest x2 27.5 us: pair_terms(): jnp.einsum('...qhd,...khd->...hqk', grad_rows, value_rows, preferred_elem...]
    all_gather x0 -> x1, waiting for transfers between devices: none -> 84.2 us  [body(): glob_parts = lax.all_gather(dglob, 'seq', axis=0, tiled=False)]
    pallas_call x0 -> x5, Pallas kernels: none -> 78.8 us  [the longest x1 59.7 us: attention(): pl.pallas_call(attention_kernel, in_specs=[pl.BlockSpec(memory_space=pltp...]
    psum x1 -> x0, blocking collectives: 75.9 us -> none  [body(): dk_glob, dv_glob = lax.psum((dk_glob_part, dv_glob_part), 'seq')]
    ppermute x4 -> x2, waiting for transfers between devices: 72.6 us -> 6.16 us  [to_mate(): lax.ppermute(array, 'seq', [(i, i - i % share + (i + step) % share) for i...]
    another operation x9 -> x3, local copies, waits for them, and re-layouts: 56.5 us -> 1.45 us  [body(): jnp.stack([log_norm.reshape(size, part), delta.reshape(size, part)], axis=1)]
  transfers between devices with their start and end apart: 8 -> 9, of which waited for: 2 -> 9; matrix products, arithmetic and copies ran while one was open for 40% -> 5% of each run, Pallas kernels for 0% -> 3%
where the time goes in v1:
time: 499 us; the launch traced here: 498 us
  waiting for transfers between devices  326 us (65%)
  Pallas kernels  78.8 us (16%)
  starting transfers between devices  33.4 us (7%)
  other arithmetic  25.2 us (5%)
  local copies, waits for them, and re-layouts  19.7 us (4%)
  between operations  14.2 us (3%)
    all_to_all x6, waiting for transfers between devices, exchange(): return lax.all_to_all(array, 'seq', split_axis=0, concat_axis=0, tiled=True)  236 us
    all_gather x1, waiting for transfers between devices, body(): glob_parts = lax.all_gather(dglob, 'seq', axis=0, tiled=False)  84.2 us
    pallas_call x1, Pallas kernels, attention(): pl.pallas_call(attention_kernel, in_specs=[pl.BlockSpec(memory_space=pltp...  59.7 us
    all_to_all x6, starting transfers between devices, exchange(): return lax.all_to_all(array, 'seq', split_axis=0, concat_axis=0, tiled=True)  32.6 us
  transfers between devices with their start and end apart: 9, of which 9 were waited for; matrix products, arithmetic and copies ran while one was open for 5% of the time, Pallas kernels for 3%

profile of v1, /device:TPU:15, one launch (start us, length us, event | category | flops | bytes accessed | tf_op | source)
XLA Modules:
  0.0 497.9 jit_solution(4224096160216261376)
XLA Ops:
  7.9 3.1 multiply_bitcast_fusion
  11.1 3.0 copy.54
  14.0 3.4 reduce_sum.27
  18.3 6.6 %all-to-all-start = ((f32[16,2,512]{2,1,0:T(2,128)}), f32[16,2,512]{2,1,0:T(2,128)S(1)}, u32[]{:S(2)}, u32[]{:S(2)}) async-start(f32[16,2,512]{2,1,0:T(2,128)} %copy.48), calls=%async_computation | async-start | bytes 131072 | tf_op jit(solution)/shard_map/all_to_all | solution.py:174
  25.2 4.0 all-to-all-done
  29.1 1.1 broadcast_in_dim.15
  30.2 6.2 %all-to-all-start.3 = ((bf16[16,128,256]{2,1,0:T(8,128)(2,1)}), bf16[16,128,256]{2,1,0:T(8,128)(2,1)S(1)}, u32[]{:S(2)}, u32[]{:S(2)}) async-start(bf16[16,128,256]{2,1,0:T(8,128)(2,1)} %bitcast.9), calls=%async_computation.3 | async-start | bytes 2097152 | tf_op jit(solution)/shard_map/all_to_all | solution.py:174
  36.4 5.0 shard_map.138
  41.4 19.9 %all-to-all-done.3 = bf16[16,128,256]{2,1,0:T(8,128)(2,1)S(1)} async-done(((bf16[16,128,256]{2,1,0:T(8,128)(2,1)}), bf16[16,128,256]{2,1,0:T(8,128)(2,1)S(1)}, u32[]{:S(2)}, u32[]{:S(2)}) %all-to-all-start.3) | async-done | bytes 1048608 | tf_op jit(solution)/shard_map/all_to_all | solution.py:174
  61.3 4.9 all-to-all-start.2
  66.2 4.9 shard_map.137
  71.2 87.5 %all-to-all-done.2 = bf16[16,512,256]{2,1,0:T(8,128)(2,1)} async-done(((bf16[16,512,256]{2,1,0:T(8,128)(2,1)}), bf16[16,512,256]{2,1,0:T(8,128)(2,1)}, u32[]{:S(2)}, u32[]{:S(2)}) %all-to-all-start.2) | async-done | bytes 4194336 | tf_op jit(solution)/shard_map/all_to_all | solution.py:174
  158.7 5.0 %all-to-all-start.1 = ((bf16[16,512,256]{2,1,0:T(8,128)(2,1)}), bf16[16,512,256]{2,1,0:T(8,128)(2,1)}, u32[]{:S(2)}, u32[]{:S(2)}) async-start(bf16[16,512,256]{2,1,0:T(8,128)(2,1)} %bitcast.36), calls=%async_computation.1 | async-start | bytes 8388608 | tf_op jit(solution)/shard_map/all_to_all | solution.py:174
  166.5 1.1 select_reduce_fusion.glob_ref
  167.6 3.9 collective-permute-done
  171.5 7.4 %pad_maximum_fusion = bf16[32,512,256]{2,1,0:T(8,128)(2,1)} fusion(bf16[16,512,256]{2,1,0:T(8,128)(2,1)} %collective-permute-done, bf16[16,512,256]{2,1,0:T(8,128)(2,1)} %all-to-all-done.2), kind=kLoop, calls=%fused_computation.1 | loop fusion | flops 4194304 | bytes 16777216 | tf_op jit(solution)/shard_map/concatenate | solution.py:229
  178.9 77.3 %all-to-all-done.1 = bf16[16,512,256]{2,1,0:T(8,128)(2,1)} async-done(((bf16[16,512,256]{2,1,0:T(8,128)(2,1)}), bf16[16,512,256]{2,1,0:T(8,128)(2,1)}, u32[]{:S(2)}, u32[]{:S(2)}) %all-to-all-start.1) | async-done | bytes 4194336 | tf_op jit(solution)/shard_map/all_to_all | solution.py:174
  256.2 59.7 %shard_map.139 = (bf16[64,128,128]{2,1,0:T(8,128)(2,1)}, bf16[128,128,256]{2,1,0:T(8,128)(2,1)}, f32[128,256]{1,0:T(8,128)}) custom-call(s32[384]{0:T(512)} %fusion.7.table_ref, f32[64,2,128]{2,1,0:T(2,128)} %bitcast.52, bf16[64,128,256]{2,1,0:T(8,128)(2,1)} %bitcast.5.pair_ref, bf16[128,128,256]{2,1,0:T(8,128)(2,1)} %bitcast.40, ...), custom_call_target="tpu_custom_call" | custom-call | flops 9395240960 | bytes 23068672 | tf_op jit(solution)/shard_map/pallas_call | solution.py:150
  315.9 6.0 %fusion.19 = (bf16[64,128,256]{2,1,0:T(8,128)(2,1)}, bf16[64,128,256]{2,1,0:T(8,128)(2,1)}) fusion(bf16[128,128,256]{2,1,0:T(8,128)(2,1)} %get-tuple-element.11), kind=kLoop, calls=%fused_computation.61 | loop fusion | bytes 16777216 | tf_op jit(solution)/shard_map/slice | solution.py:252
  322.1 5.0 %all-to-all-start.4 = ((bf16[16,512,128]{2,1,0:T(8,128)(2,1)}), bf16[16,512,128]{2,1,0:T(8,128)(2,1)S(1)}, u32[]{:S(2)}, u32[]{:S(2)}) async-start(bf16[16,512,128]{2,1,0:T(8,128)(2,1)} %bitcast.44), calls=%async_computation.4 | async-start | bytes 4194304 | tf_op jit(solution)/shard_map/all_to_all | solution.py:174
  327.1 2.3 collective-permute-done.1
  329.4 6.7 %fusion = bf16[16,512,256]{2,1,0:T(8,128)(2,1)} fusion(bf16[16,512,256]{2,1,0:T(8,128)(2,1)} %collective-permute-done.1, bf16[16,512,256]{2,1,0:T(8,128)(2,1)} %bitcast.37), kind=kLoop, calls=%fused_computation.3 | loop fusion | flops 8388608 | bytes 12582912 | tf_op jit(solution)/shard_map/convert_element_type | solution.py:255
  336.2 38.4 %all-to-all-done.4 = bf16[16,512,128]{2,1,0:T(8,128)(2,1)S(1)} async-done(((bf16[16,512,128]{2,1,0:T(8,128)(2,1)}), bf16[16,512,128]{2,1,0:T(8,128)(2,1)S(1)}, u32[]{:S(2)}, u32[]{:S(2)}) %all-to-all-start.4) | async-done | bytes 2097184 | tf_op jit(solution)/shard_map/all_to_all | solution.py:174
  374.5 1.3 copy-done
  375.9 4.9 all-to-all-start.5
  381.5 84.2 %all-gather.3.cloned.1.call-done = f32[2048,256]{1,0:T(8,128)} async-done(((f32[128,256]{1,0:T(8,128)}), f32[2048,256]{1,0:T(8,128)}) %all-gather.3.cloned.1.call-update) | async-done | bytes 2097168 | tf_op jit(solution)/shard_map/all_gather | solution.py:256
  465.7 2.3 reshape.259
  468.0 1.9 reduce_sum.29
  469.9 4.0 shard_map.140
  473.9 0.9 fusion.20
  477.3 8.5 %all-to-all-done.5 = bf16[16,512,256]{2,1,0:T(8,128)(2,1)} async-done(((bf16[16,512,256]{2,1,0:T(8,128)(2,1)}), bf16[16,512,256]{2,1,0:T(8,128)(2,1)}, u32[]{:S(2)}, u32[]{:S(2)}) %all-to-all-start.5) | async-done | bytes 4194336 | tf_op jit(solution)/shard_map/all_to_all | solution.py:174
  485.9 5.2 %shard_map.141 = (bf16[1024,1024]{1,0:T(8,128)(2,1)}, bf16[1024,1024]{1,0:T(8,128)(2,1)}) custom-call(bf16[8,2,512,256]{3,2,1,0:T(8,128)(2,1)} %bitcast.14.in_ref), custom_call_target="tpu_custom_call" | custom-call | bytes 8388608 | tf_op jit(solution)/shard_map/pallas_call | solution.py:63
  (39 shorter events, 8.0 us)
Async XLA Ops:
  14.0 10.9 %copy-start.1 = (bf16[1,128,1024]{2,1,0:T(8,128)(2,1)S(1)}, bf16[1,128,1024]{2,1,0:T(8,128)(2,1)}, u32[]{:S(2)}) copy-start(bf16[1,128,1024]{2,1,0:T(8,128)(2,1)} %param.16) | copy-start | bytes 786436
  14.0 10.9 %copy-start.2 = (bf16[1,128,1024]{2,1,0:T(8,128)(2,1)S(1)}, bf16[1,128,1024]{2,1,0:T(8,128)(2,1)}, u32[]{:S(2)}) copy-start(bf16[1,128,1024]{2,1,0:T(8,128)(2,1)} %param.17) | copy-start | bytes 786436
  18.3 10.8 %all-to-all-start = ((f32[16,2,512]{2,1,0:T(2,128)}), f32[16,2,512]{2,1,0:T(2,128)S(1)}, u32[]{:S(2)}, u32[]{:S(2)}) async-start(f32[16,2,512]{2,1,0:T(2,128)} %copy.48), calls=%async_computation | async-start | bytes 131072 | tf_op jit(solution)/shard_map/all_to_all | solution.py:174
  30.2 31.1 %all-to-all-start.3 = ((bf16[16,128,256]{2,1,0:T(8,128)(2,1)}), bf16[16,128,256]{2,1,0:T(8,128)(2,1)S(1)}, u32[]{:S(2)}, u32[]{:S(2)}) async-start(bf16[16,128,256]{2,1,0:T(8,128)(2,1)} %bitcast.9), calls=%async_computation.3 | async-start | bytes 2097152 | tf_op jit(solution)/shard_map/all_to_all | solution.py:174
  61.3 97.4 %all-to-all-start.2 = ((bf16[16,512,256]{2,1,0:T(8,128)(2,1)}), bf16[16,512,256]{2,1,0:T(8,128)(2,1)}, u32[]{:S(2)}, u32[]{:S(2)}) async-start(bf16[16,512,256]{2,1,0:T(8,128)(2,1)} %bitcast.38), calls=%async_computation.2 | async-start | bytes 8388608 | tf_op jit(solution)/shard_map/all_to_all | solution.py:174
  158.7 5.4 %copy-start.3 = (s32[128,3]{0,1:T(4,128)S(1)}, s32[128,3]{0,1:T(4,128)}, u32[]{:S(2)}) copy-start(s32[128,3]{0,1:T(4,128)} %param.18) | copy-start | bytes 4612
  158.7 6.5 %copy-start.4 = (s32[128]{0:T(128)S(1)}, s32[128]{0:T(128)}, u32[]{:S(2)}) copy-start(s32[128]{0:T(128)} %param.19) | copy-start | bytes 1540
  158.7 97.5 %all-to-all-start.1 = ((bf16[16,512,256]{2,1,0:T(8,128)(2,1)}), bf16[16,512,256]{2,1,0:T(8,128)(2,1)}, u32[]{:S(2)}, u32[]{:S(2)}) async-start(bf16[16,512,256]{2,1,0:T(8,128)(2,1)} %bitcast.36), calls=%async_computation.1 | async-start | bytes 8388608 | tf_op jit(solution)/shard_map/all_to_all | solution.py:174
  163.7 7.7 %collective-permute-start = (bf16[16,512,256]{2,1,0:T(8,128)(2,1)}, bf16[16,512,256]{2,1,0:T(8,128)(2,1)}, u32[]{:S(2)}, u32[]{:S(2)}) collective-permute-start(bf16[16,512,256]{2,1,0:T(8,128)(2,1)} %all-to-all-done.2), channel_id=1, source_target_pairs={{0,2},{2,0},{4,6},{6,4},{8,10},{10,8},{12,14},{14,12},{16,18},{18,... | collective-permute-start | bytes 12582920 | tf_op jit(solution)/shard_map/ppermute | solution.py:179
  321.9 7.5 %collective-permute-start.1 = (bf16[16,512,256]{2,1,0:T(8,128)(2,1)}, bf16[16,512,256]{2,1,0:T(8,128)(2,1)}, u32[]{:S(2)}, u32[]{:S(2)}) collective-permute-start(bf16[16,512,256]{2,1,0:T(8,128)(2,1)} %bitcast.13), channel_id=1, source_target_pairs={{0,2},{2,0},{4,6},{6,4},{8,10},{10,8},{12,14},{14,12},{16,18},{18,... | collective-permute-start | bytes 12582920 | tf_op jit(solution)/shard_map/ppermute | solution.py:179
  322.1 52.4 %all-to-all-start.4 = ((bf16[16,512,128]{2,1,0:T(8,128)(2,1)}), bf16[16,512,128]{2,1,0:T(8,128)(2,1)S(1)}, u32[]{:S(2)}, u32[]{:S(2)}) async-start(bf16[16,512,128]{2,1,0:T(8,128)(2,1)} %bitcast.44), calls=%async_computation.4 | async-start | bytes 4194304 | tf_op jit(solution)/shard_map/all_to_all | solution.py:174
  374.5 1.3 copy-start
  375.9 110.0 %all-to-all-start.5 = ((bf16[16,512,256]{2,1,0:T(8,128)(2,1)}), bf16[16,512,256]{2,1,0:T(8,128)(2,1)}, u32[]{:S(2)}, u32[]{:S(2)}) async-start(bf16[16,512,256]{2,1,0:T(8,128)(2,1)} %fusion), calls=%async_computation.5 | async-start | bytes 8388608 | tf_op jit(solution)/shard_map/all_to_all | solution.py:174
  380.8 84.9 %all-gather.3.cloned.1.call-start = ((), (), s32[]{:S(2)}) async-start(), calls=%async_computation.6 | async-start | bytes 2228224 | tf_op jit(solution)/shard_map/all_gather | solution.py:256
Sparse Core Ops, SparseCore 0:
  384.3 81.2 all-gather.2

commit v2 on v1

--- a/solution.py
+++ b/solution.py
@@ -181,7 +181,7 @@
     )
 
 
-def body(
+def body_shared(
     queries,
     keys,
     values,
@@ -262,6 +262,400 @@
     return (grad_queries, grad_keys, grad_values, glob_grads[0], glob_grads[1])
 
 
+CHUNKS = ((0, 1), (4, 4), (2, 2), (1, 1))
+PAD = 8
+VMEM_LIMIT = 60 * 1024 * 1024
+
+
+def split_two(row):
+    high = row.astype(jnp.bfloat16).astype(jnp.float32)
+    return jnp.concatenate([high, row - high], axis=1)
+
+
+def pack_queries_kernel(query_ref, grad_ref, saved_ref, norm_ref, out_ref):
+    rows = query_ref.shape[0]
+    for head in range(out_ref.shape[0]):
+        cols = slice(head * HD, (head + 1) * HD)
+        grad = grad_ref[:, cols]
+        out_ref[head, :rows, :HD] = query_ref[:, cols]
+        out_ref[head, :rows, HD:] = grad
+        product = grad.astype(jnp.float32) * saved_ref[:, cols].astype(jnp.float32)
+        delta = jnp.sum(product.T, axis=0, keepdims=True)
+        norm = norm_ref[head : head + 1, :]
+        stats = []
+        for block in range(rows // BLK):
+            lanes = slice(block * BLK, (block + 1) * BLK)
+            stats += [split_two(norm[:, lanes]), split_two(delta[:, lanes])]
+        if len(stats) < PAD:
+            stats.append(jnp.zeros((PAD - len(stats), 2 * HD), jnp.float32))
+        out_ref[head, rows:, :] = jnp.concatenate(stats, axis=0).astype(jnp.bfloat16)
+
+
+def pack_queries(queries, grad_output, saved_output, log_norm, first, blocks):
+    features = queries.shape[1]
+    heads = features // HD
+    rows = blocks * BLK
+    spec = pl.BlockSpec((rows, features), lambda i: (first // blocks, 0))
+    shape = (heads, rows + PAD, 2 * HD)
+    return pl.pallas_call(
+        pack_queries_kernel,
+        grid=(1,),
+        in_specs=[spec] * 3 + [pl.BlockSpec((heads, rows), lambda i: (0, first // blocks))],
+        out_specs=pl.BlockSpec(shape, lambda i: (0, 0, 0)),
+        out_shape=jax.ShapeDtypeStruct(shape, jnp.bfloat16),
+        compiler_params=pltpu.CompilerParams(vmem_limit_bytes=VMEM_LIMIT),
+        cost_estimate=pl.CostEstimate(
+            flops=0, bytes_accessed=rows * features * 10, transcendentals=0
+        ),
+    )(queries, grad_output, saved_output, log_norm)
+
+
+def pack_keys_kernel(key_ref, value_ref, glob_key_ref, glob_value_ref, out_ref):
+    rows = key_ref.shape[0]
+    for head in range(out_ref.shape[0]):
+        cols = slice(head * HD, (head + 1) * HD)
+        out_ref[head, :rows, :HD] = key_ref[:, cols]
+        out_ref[head, :rows, HD:] = value_ref[:, cols]
+        out_ref[head, rows:, :HD] = glob_key_ref[:, cols]
+        out_ref[head, rows:, HD:] = glob_value_ref[:, cols]
+
+
+def pack_keys(keys, values, glob_keys, glob_values):
+    tokens, features = keys.shape
+    heads = features // HD
+    vmem = pl.BlockSpec(memory_space=pltpu.VMEM)
+    return pl.pallas_call(
+        pack_keys_kernel,
+        in_specs=[vmem] * 4,
+        out_specs=vmem,
+        out_shape=jax.ShapeDtypeStruct((heads, tokens + G, 2 * HD), jnp.bfloat16),
+        compiler_params=pltpu.CompilerParams(vmem_limit_bytes=VMEM_LIMIT),
+        cost_estimate=pl.CostEstimate(
+            flops=0, bytes_accessed=(tokens + G) * features * 8, transcendentals=0
+        ),
+    )(keys, values, glob_keys, glob_values)
+
+
+def pair_grads(pair, stats, rows, valid):
+    zero = jnp.zeros((BLK, HD), jnp.bfloat16)
+    mixed = jnp.concatenate(
+        [
+            jnp.concatenate([pair[:, :HD], zero], axis=1),
+            jnp.concatenate([zero, pair[:, HD:]], axis=1),
+        ],
+        axis=0,
+    )
+    norm = (stats[0:1, :HD] + stats[0:1, HD:]) * LOG2E
+    delta = stats[1:2, :HD] + stats[1:2, HD:]
+    rows = jnp.concatenate(rows, axis=0) if len(rows) > 1 else rows[0]
+    both = lax.dot_general(
+        rows, mixed, (((1,), (1,)), ((), ())), preferred_element_type=jnp.float32
+    )
+    attend = jnp.exp2(both[:, :HD] * (FACTOR * LOG2E) - norm)
+    parts = []
+    for kind, known in enumerate(valid):
+        part = attend[kind * BLK : (kind + 1) * BLK]
+        parts.append(part if known is None else jnp.where(known, part, 0.0))
+    attend = jnp.concatenate(parts, axis=0) if len(parts) > 1 else parts[0]
+    grad_scores = attend * (both[:, HD:] - delta)
+    scores_low = grad_scores.astype(jnp.bfloat16)
+    grad_kv = jnp.dot(
+        jnp.concatenate([scores_low, attend.astype(jnp.bfloat16)], axis=1),
+        mixed,
+        preferred_element_type=jnp.float32,
+    )
+    grad_q = lax.dot_general(
+        scores_low, rows[:, :HD], (((0,), (0,)), ((), ())), preferred_element_type=jnp.float32
+    )
+    return grad_kv, grad_q * FACTOR
+
+
+def key_rows(kv_ref, place, blocks):
+    source = place // blocks
+    start = pl.multiple_of((place % blocks) * BLK, BLK)
+    return kv_ref[source, pl.ds(start, BLK), :]
+
+
+def own_kernel(table_ref, *refs):
+    chunk_refs, (kv_ref, glob_ref) = refs[: len(CHUNKS)], refs[len(CHUNKS) : len(CHUNKS) + 2]
+    dq_refs, (dkv_ref, dglob_ref) = refs[len(CHUNKS) + 2 : -2], refs[-2:]
+    sources = kv_ref.shape[0]
+    blocks = dkv_ref.shape[0] // sources
+    kinds = W + R
+
+    def clear(block, carry):
+        dkv_ref[block] = jnp.zeros((BLK, 2 * HD), jnp.float32)
+        return carry
+
+    lax.fori_loop(0, dkv_ref.shape[0], clear, 0)
+    dglob_ref[...] = jnp.zeros_like(dglob_ref)
+    for (first, size), pair_ref, dq_ref in zip(CHUNKS, chunk_refs, dq_refs):
+
+        def one_source(source, carry, first=first, size=size, pair_ref=pair_ref, dq_ref=dq_ref):
+            stats = pair_ref[source, size * BLK :, :].astype(jnp.float32)
+            for inner in range(size):
+                lines = slice(inner * BLK, (inner + 1) * BLK)
+                entry = (source * blocks + first + inner) * kinds
+                wanted = [table_ref[entry + kind] for kind in range(kinds)]
+                places = [jnp.maximum(place, 0) for place in wanted]
+                rows = [key_rows(kv_ref, place, blocks) for place in places]
+                grad_kv, grad_q = pair_grads(
+                    pair_ref[source, lines, :],
+                    stats[2 * inner : 2 * inner + 2],
+                    rows + [glob_ref[...]],
+                    [place >= 0 for place in wanted] + [None],
+                )
+                for kind, place in enumerate(places):
+                    dkv_ref[place] += grad_kv[kind * BLK : (kind + 1) * BLK]
+                dglob_ref[...] += grad_kv[kinds * BLK :]
+                dq_ref[source, lines, :] = grad_q
+            return carry
+
+        lax.fori_loop(0, sources, one_source, 0)
+    dglob_ref[:, :HD] = dglob_ref[:, :HD] * FACTOR
+
+
+def own_pairs(table, chunks, kv, glob):
+    sources = kv.shape[0]
+    blocks = (kv.shape[1] - G) // BLK
+    vmem = pl.BlockSpec(memory_space=pltpu.VMEM)
+    smem = pl.BlockSpec(memory_space=pltpu.SMEM)
+    units = sources * blocks * (W + R + 1)
+    return pl.pallas_call(
+        own_kernel,
+        in_specs=[smem] + [vmem] * (len(chunks) + 2),
+        out_specs=[vmem] * (len(chunks) + 2),
+        out_shape=[
+            jax.ShapeDtypeStruct((sources, size * BLK, HD), jnp.float32) for _, size in CHUNKS
+        ]
+        + [
+            jax.ShapeDtypeStruct((sources * blocks, BLK, 2 * HD), jnp.float32),
+            jax.ShapeDtypeStruct((G, 2 * HD), jnp.float32),
+        ],
+        compiler_params=pltpu.CompilerParams(vmem_limit_bytes=VMEM_LIMIT),
+        cost_estimate=pl.CostEstimate(flops=0, bytes_accessed=1024, transcendentals=0),
+    )(table, *chunks, kv, glob)
+
+
+def cross_kernel(first, size, last, table_ref, pair_ref, kv_ref, sum_ref, dq_ref, dkv_ref):
+    sources = kv_ref.shape[0]
+    total = sum_ref.shape[0]
+    blocks = total // sources
+
+    def one_source(source, carry):
+        stats = pair_ref[source, size * BLK :, :].astype(jnp.float32)
+        for inner in range(size):
+            lines = slice(inner * BLK, (inner + 1) * BLK)
+            entry = (source * blocks + first + inner) * R
+            wanted = [table_ref[entry + kind] for kind in range(R)]
+            places = [jnp.maximum(place, 0) for place in wanted]
+            grad_kv, grad_q = pair_grads(
+                pair_ref[source, lines, :],
+                stats[2 * inner : 2 * inner + 2],
+                [key_rows(kv_ref, place, blocks) for place in places],
+                [place >= 0 for place in wanted],
+            )
+            for kind, place in enumerate(places):
+                sum_ref[place] += grad_kv[kind * BLK : (kind + 1) * BLK]
+            dq_ref[source, lines, :] = grad_q.astype(jnp.bfloat16)
+        return carry
+
+    lax.fori_loop(0, sources, one_source, 0)
+    rims = []
+    if first == 0:
+        rims.append((0, 0, total - 1))
+    if first + size == blocks:
+        rims.append((sources - 1, size - 1, 0))
+    for source, inner, place in rims:
+        lines = slice(inner * BLK, (inner + 1) * BLK)
+        stats = pair_ref[source, size * BLK :, :].astype(jnp.float32)
+        grad_kv, grad_q = pair_grads(
+            pair_ref[source, lines, :],
+            stats[2 * inner : 2 * inner + 2],
+            [key_rows(kv_ref, place, blocks)],
+            [None],
+        )
+        sum_ref[place] += grad_kv
+        dq_ref[source, lines, :] = (
+            dq_ref[source, lines, :].astype(jnp.float32) + grad_q
+        ).astype(jnp.bfloat16)
+    if last:
+
+        def round_block(block, carry):
+            start = pl.multiple_of((block % blocks) * BLK, BLK)
+            value = sum_ref[block]
+            dkv_ref[block // blocks, pl.ds(start, BLK), :] = jnp.concatenate(
+                [value[:, :HD] * FACTOR, value[:, HD:]], axis=1
+            ).astype(jnp.bfloat16)
+            return carry
+
+        lax.fori_loop(0, total, round_block, 0)
+
+
+def cross_middle_kernel(first, size, table_ref, pair_ref, kv_ref, in_ref, dq_ref, sum_ref):
+    def carry_over(block, carry):
+        sum_ref[block] = in_ref[block]
+        return carry
+
+    lax.fori_loop(0, sum_ref.shape[0], carry_over, 0)
+    cross_kernel(first, size, False, table_ref, pair_ref, kv_ref, sum_ref, dq_ref, None)
+
+
+def cross_last_kernel(first, size, table_ref, pair_ref, kv_ref, in_ref, dq_ref, dkv_ref, sum_ref):
+    def carry_over(block, carry):
+        sum_ref[block] = in_ref[block]
+        return carry
+
+    lax.fori_loop(0, sum_ref.shape[0], carry_over, 0)
+    cross_kernel(first, size, True, table_ref, pair_ref, kv_ref, sum_ref, dq_ref, dkv_ref)
+
+
+def cross_pairs(table, pairs, kv, sums, first, size, last):
+    sources = kv.shape[0]
+    blocks = (kv.shape[1] - G) // BLK
+    vmem = pl.BlockSpec(memory_space=pltpu.VMEM)
+    smem = pl.BlockSpec(memory_space=pltpu.SMEM)
+    units = sources * size * R
+    dq_shape = jax.ShapeDtypeStruct((sources, size * BLK, HD), jnp.bfloat16)
+    if last:
+        kernel = functools.partial(cross_last_kernel, first, size)
+        sum_shape = jax.ShapeDtypeStruct((sources, blocks * BLK, 2 * HD), jnp.bfloat16)
+        scratch = [pltpu.VMEM(sums.shape, jnp.float32)]
+    else:
+        kernel = functools.partial(cross_middle_kernel, first, size)
+        sum_shape = jax.ShapeDtypeStruct(sums.shape, jnp.float32)
+        scratch = []
+    return pl.pallas_call(
+        kernel,
+        in_specs=[smem, vmem, vmem, vmem],
+        out_specs=[vmem, vmem],
+        out_shape=[dq_shape, sum_shape],
+        scratch_shapes=scratch,
+        compiler_params=pltpu.CompilerParams(vmem_limit_bytes=VMEM_LIMIT),
+        cost_estimate=pl.CostEstimate(flops=0, bytes_accessed=1024, transcendentals=0),
+    )(table, pairs, kv, sums)
+
+
+def unpack_kernel(groups, *refs):
+    in_refs, out_ref = refs[:-1], refs[-1]
+    for in_ref, places in zip(in_refs, groups):
+        start = 0
+        for first, size in places:
+            for head in range(in_ref.shape[0]):
+                out_ref[first * BLK : (first + size) * BLK, head * HD : (head + 1) * HD] = in_ref[
+                    head, start : start + size * BLK, :
+                ]
+            start += size * BLK
+
+
+def unpack_queries(arrays, groups):
+    heads = arrays[0].shape[0]
+    tokens = sum(array.shape[1] for array in arrays)
+    vmem = pl.BlockSpec(memory_space=pltpu.VMEM)
+    return pl.pallas_call(
+        functools.partial(unpack_kernel, groups),
+        in_specs=[vmem] * len(arrays),
+        out_specs=vmem,
+        out_shape=jax.ShapeDtypeStruct((tokens, heads * HD), jnp.bfloat16),
+        compiler_params=pltpu.CompilerParams(vmem_limit_bytes=VMEM_LIMIT),
+        cost_estimate=pl.CostEstimate(
+            flops=0, bytes_accessed=tokens * heads * HD * 4, transcendentals=0
+        ),
+    )(*arrays)
+
+
+def body_halves(
+    queries,
+    keys,
+    values,
+    saved_output,
+    grad_output,
+    log_norm,
+    global_keys,
+    global_values,
+    flow_links,
+    glob_owner,
+):
+    size = lax.axis_size("seq")
+    my_index = lax.axis_index("seq")
+    tokens, features = queries.shape
+    heads = features // HD
+    blocks = tokens // BLK
+    count = heads * blocks
+    half = my_index // heads
+    groups = [list(range(heads)), list(range(heads, size))]
+
+    def within(array):
+        return lax.all_to_all(
+            array, "seq", split_axis=0, concat_axis=0, tiled=True, axis_index_groups=groups
+        )
+
+    def across(array):
+        return lax.ppermute(array, "seq", [(i, (i + heads) % size) for i in range(size)])
+
+    chunks, crossed = [], []
+    for first, number in CHUNKS:
+        packed = pack_queries(queries, grad_output, saved_output, log_norm, first, number)
+        if chunks:
+            packed, chunks[-1] = lax.optimization_barrier((packed, chunks[-1]))
+        chunk = within(packed)
+        chunks.append(chunk)
+        crossed.append(across(chunk))
+    owned = (glob_owner == my_index)[:, None]
+    packed = pack_keys(
+        keys,
+        values,
+        jnp.where(owned, global_keys[0], jnp.bfloat16(0)),
+        jnp.where(owned, global_values[0], jnp.bfloat16(0)),
+    )
+    packed, chunks[-1] = lax.optimization_barrier((packed, chunks[-1]))
+    kv = within(packed)
+    glob_half = jnp.sum(kv[:, tokens:, :].astype(jnp.float32), axis=0).astype(jnp.bfloat16)
+    glob_now = (glob_half.astype(jnp.float32) + across(glob_half).astype(jnp.float32)).astype(
+        jnp.bfloat16
+    )
+
+    def places(wanted):
+        here = wanted - half * count
+        return jnp.where((here >= 0) & (here < count), here, -1).reshape(-1).astype(jnp.int32)
+
+    links = flow_links.reshape(2, count, R)
+    my_links = lax.dynamic_index_in_dim(links, half, axis=0, keepdims=False)
+    other_links = lax.dynamic_index_in_dim(links, 1 - half, axis=0, keepdims=False)
+    mine = half * count + jnp.arange(count, dtype=jnp.int32)
+    near = (mine[:, None] + jnp.arange(-1, 2, dtype=jnp.int32) + 2 * count) % (2 * count)
+    own_table = places(jnp.concatenate([near, my_links], axis=1))
+    cross_table = places(other_links)
+
+    *own_dq, sums, dglob = own_pairs(own_table, chunks, kv, glob_now)
+    glob_parts = lax.all_gather(dglob, "seq", axis=0, tiled=False)
+    totals = []
+    for step, (first, number) in enumerate(CHUNKS):
+        dq, sums = cross_pairs(
+            cross_table, crossed[step], kv, sums, first, number, step == len(CHUNKS) - 1
+        )
+        totals.append(
+            (own_dq[step] + across(dq).astype(jnp.float32)).astype(jnp.bfloat16)
+        )
+    sums = within(sums)
+    totals[-1], sums = lax.optimization_barrier((totals[-1], sums))
+    grad_keys, grad_values = unpair_heads(sums, 1)
+    early = within(jnp.concatenate(totals[:-1], axis=1))
+    late = within(totals[-1])
+    grad_queries = unpack_queries((early, late), (CHUNKS[:-1], CHUNKS[-1:]))
+    glob_sum = jnp.sum(glob_parts.reshape(2, heads, G, 2, HD), axis=0)
+    glob_grads = jnp.transpose(glob_sum, (2, 1, 0, 3)).reshape(2, G, features).astype(jnp.bfloat16)
+    return (grad_queries, grad_keys, grad_values, glob_grads[0], glob_grads[1])
+
+
+def body(queries, *rest):
+    heads = queries.shape[1] // HD
+    blocks = queries.shape[0] // BLK
+    if lax.axis_size("seq") == 2 * heads and blocks == sum(number for _, number in CHUNKS):
+        return body_halves(queries, *rest)
+    return body_shared(queries, *rest)
+
+
 def solution(mesh):
     return jax.shard_map(
         body,

time: 499 us -> 558 us (1.12)
  Pallas kernels: 78.8 us -> 131 us
  starting transfers between devices: 33.4 us -> 53.5 us
  other arithmetic: 25.2 us -> 12.9 us
  local copies, waits for them, and re-layouts: 19.7 us -> 7.8 us
  waiting for transfers between devices: 326 us -> 336 us
    ppermute x2 -> x9, waiting for transfers between devices: 6.16 us -> 205 us  [across(): lax.ppermute(array, 'seq', [(i, (i + heads) % size) for i in range(size)])]
    all_to_all x6 -> x8, waiting for transfers between devices: 236 us -> 132 us  [within(): lax.all_to_all(array, 'seq', split_axis=0, concat_axis=0, tiled=True, axi...]
    all_gather x1, waiting for transfers between devices: 84.2 us -> 0.01 us  [body_halves(): glob_parts = lax.all_gather(dglob, 'seq', axis=0, tiled=False)]
    pallas_call x3 -> x11, Pallas kernels: 69.6 us -> 126 us  [the longest x4 62.2 us: cross_pairs(): pl.pallas_call(kernel, in_specs=[smem, vmem, vmem, vmem], out_specs=[vmem...]
    all_to_all x6 -> x8, starting transfers between devices: 32.6 us -> 44.1 us  [within(): lax.all_to_all(array, 'seq', split_axis=0, concat_axis=0, tiled=True, axi...]
    ppermute x2 -> x9, starting transfers between devices: 0.58 us -> 9.44 us  [across(): lax.ppermute(array, 'seq', [(i, (i + heads) % size) for i in range(size)])]
    concatenate x3 -> x1, other arithmetic: 8.17 us -> 1.36 us  [body_halves(): early = within(jnp.concatenate(totals[:-1], axis=1))]
    slice x5 -> x3, local copies, waits for them, and re-layouts: 7.68 us -> 1.7 us  [body_halves(): return (grad_queries, grad_keys, grad_values, glob_grads[0], glob_grads[1])]
  transfers between devices with their start and end apart: 9 -> 18, of which waited for: 9 -> 7; matrix products, arithmetic and copies ran while one was open for 5% -> 3% of each run, Pallas kernels for 3% -> 20%
where the time goes in v2:
time: 558 us; the launch traced here: 556 us
  waiting for transfers between devices  336 us (60%)
  Pallas kernels  131 us (23%)
  starting transfers between devices  53.5 us (10%)
  between operations  14.2 us (3%)
  other arithmetic  12.9 us (2%)
  local copies, waits for them, and re-layouts  7.8 us (1%)
    ppermute x9, waiting for transfers between devices, across(): lax.ppermute(array, 'seq', [(i, (i + heads) % size) for i in range(size)])  205 us
    all_to_all x8, waiting for transfers between devices, within(): lax.all_to_all(array, 'seq', split_axis=0, concat_axis=0, tiled=True, axi...  132 us
    pallas_call x4, Pallas kernels, cross_pairs(): pl.pallas_call(kernel, in_specs=[smem, vmem, vmem, vmem], out_specs=[vmem...  62.2 us
    all_to_all x8, starting transfers between devices, within(): lax.all_to_all(array, 'seq', split_axis=0, concat_axis=0, tiled=True, axi...  44.1 us
    pallas_call x1, Pallas kernels, own_pairs(): pl.pallas_call(own_kernel, in_specs=[smem] + [vmem] * (len(chunks) + 2),...  44 us
  transfers between devices with their start and end apart: 18, of which 7 were waited for; matrix products, arithmetic and copies ran while one was open for 3% of the time, Pallas kernels for 20%

profile of v2, /device:TPU:15, one launch (start us, length us, event | category | flops | bytes accessed | tf_op | source)
XLA Modules:
  0.0 556.1 jit_solution(12806965283197709603)
XLA Ops:
  7.2 2.1 shard_map.138
  9.3 4.5 all-to-all-start
  13.8 4.0 shard_map.137
  17.8 3.2 all-to-all-done.refs_0_
  21.9 5.5 all-to-all-start.1
  27.4 2.7 shard_map.139
  30.1 21.3 %all-to-all-done.1.refs_1_ = bf16[8,520,256]{2,1,0:T(8,128)(2,1)S(1)} async-done(((bf16[8,520,256]{2,1,0:T(8,128)(2,1)}), bf16[8,520,256]{2,1,0:T(8,128)(2,1)S(1)}, u32[]{:S(2)}, u32[]{:S(2)}) %all-to-all-start.1) | async-done | bytes 2129952 | tf_op jit(solution)/shard_map/all_to_all | solution.py:589
  51.4 5.5 all-to-all-start.2
  56.9 2.2 shard_map.140
  59.1 10.6 %all-to-all-done.2.refs_2_ = bf16[8,264,256]{2,1,0:T(8,128)(2,1)S(1)} async-done(((bf16[8,264,256]{2,1,0:T(8,128)(2,1)}), bf16[8,264,256]{2,1,0:T(8,128)(2,1)S(1)}, u32[]{:S(2)}, u32[]{:S(2)}) %all-to-all-start.2) | async-done | bytes 1081376 | tf_op jit(solution)/shard_map/all_to_all | solution.py:589
  69.7 6.1 %all-to-all-start.3 = ((bf16[8,136,256]{2,1,0:T(8,128)(2,1)}), bf16[8,136,256]{2,1,0:T(8,128)(2,1)}, u32[]{:S(2)}, u32[]{:S(2)}) async-start(bf16[8,136,256]{2,1,0:T(8,128)(2,1)} %shard_map.140), calls=%async_computation.3 | async-start | bytes 1114112 | tf_op jit(solution)/shard_map/all_to_all | solution.py:589
  75.8 1.8 bitcast_select_fusion
  77.7 5.5 shard_map.141
  83.2 6.4 %all-to-all-start.4 = ((bf16[8,1152,256]{2,1,0:T(8,128)(2,1)}), bf16[8,1152,256]{2,1,0:T(8,128)(2,1)}, u32[]{:S(2)}, u32[]{:S(2)}) async-start(bf16[8,1152,256]{2,1,0:T(8,128)(2,1)} %shard_map.141), calls=%async_computation.4 | async-start | bytes 9437184 | tf_op jit(solution)/shard_map/all_to_all | solution.py:589
  89.6 2.3 collective-permute-start.3
  93.3 2.3 collective-permute-start.1
  95.7 96.5 %all-to-all-done.4.refs_4_.kv_ref = bf16[8,1152,256]{2,1,0:T(8,128)(2,1)} async-done(((bf16[8,1152,256]{2,1,0:T(8,128)(2,1)}), bf16[8,1152,256]{2,1,0:T(8,128)(2,1)}, u32[]{:S(2)}, u32[]{:S(2)}) %all-to-all-start.4) | async-done | bytes 4718624 | tf_op jit(solution)/shard_map/all_to_all | solution.py:589
  194.1 85.8 %collective-permute-done = bf16[128,256]{1,0:T(8,128)(2,1)S(1)} collective-permute-done((bf16[128,256]{1,0:T(8,128)(2,1)S(1)}, bf16[128,256]{1,0:T(8,128)(2,1)S(1)}, u32[]{:S(2)}, u32[]{:S(2)}) %collective-permute-start) | collective-permute-done | bytes 65568 | tf_op jit(solution)/shard_map/ppermute | solution.py:594
  280.6 44.0 %shard_map.142 = (f32[8,128,128]{2,1,0:T(8,128)}, f32[8,512,128]{2,1,0:T(8,128)}, f32[8,256,128]{2,1,0:T(8,128)}, f32[8,128,128]{2,1,0:T(8,128)}, f32[64,128,256]{2,1,0:T(8,128)}, /*index=5*/f32[128,256]{1,0:T(8,128)}) custom-call(s32[384]{0:T(512)} %and_select_fusion.1.table_ref, bf16[8,136,256]{2,1,0:T(8,128)(2,1)} %copy-done.3, ...), custom_call_target="tpu_custom_call" | custom-call | bytes 1024 | tf_op jit(solution)/shard_map/pallas_call | solution.py:424
  324.5 13.2 %shard_map.143 = (bf16[8,128,128]{2,1,0:T(8,128)(2,1)}, f32[64,128,256]{2,1,0:T(8,128)}) custom-call(s32[192]{0:T(256)} %and_select_fusion.table_ref, bf16[8,136,256]{2,1,0:T(8,128)(2,1)} %collective-permute-done.1.pair_ref, bf16[8,1152,256]{2,1,0:T(8,128)(2,1)} %all-to-all-done.4.refs_4_.kv_ref, f32[64,128,256]{2,1,0:T(8,128)} %get-tuple-element.40.in_ref), custom_call_target="tpu_custom_call" | custom-call | bytes 1024 | tf_op jit(solution)/shard_map/pallas_call | solution.py:528
  337.8 21.2 %shard_map.144 = (bf16[8,512,128]{2,1,0:T(8,128)(2,1)}, f32[64,128,256]{2,1,0:T(8,128)}) custom-call(s32[192]{0:T(256)} %and_select_fusion.table_ref, bf16[8,520,256]{2,1,0:T(8,128)(2,1)} %collective-permute-done.3.pair_ref, bf16[8,1152,256]{2,1,0:T(8,128)(2,1)} %all-to-all-done.4.refs_4_.kv_ref, f32[64,128,256]{2,1,0:T(8,128)} %get-tuple-element.43.in_ref), custom_call_target="tpu_custom_call" | custom-call | bytes 1024 | tf_op jit(solution)/shard_map/pallas_call | solution.py:528
  358.9 15.3 %shard_map.145 = (bf16[8,256,128]{2,1,0:T(8,128)(2,1)}, f32[64,128,256]{2,1,0:T(8,128)}) custom-call(s32[192]{0:T(256)} %and_select_fusion.table_ref, bf16[8,264,256]{2,1,0:T(8,128)(2,1)} %collective-permute-done.5.pair_ref, bf16[8,1152,256]{2,1,0:T(8,128)(2,1)} %all-to-all-done.4.refs_4_.kv_ref, f32[64,128,256]{2,1,0:T(8,128)} %get-tuple-element.46.in_ref), custom_call_target="tpu_custom_call" | custom-call | bytes 1024 | tf_op jit(solution)/shard_map/pallas_call | solution.py:528
  374.3 12.4 %shard_map.146 = (bf16[8,128,128]{2,1,0:T(8,128)(2,1)}, bf16[8,1024,256]{2,1,0:T(8,128)(2,1)}) custom-call(s32[192]{0:T(256)} %and_select_fusion.table_ref, bf16[8,136,256]{2,1,0:T(8,128)(2,1)} %collective-permute-done.7.pair_ref, bf16[8,1152,256]{2,1,0:T(8,128)(2,1)} %all-to-all-done.4.refs_4_.kv_ref, f32[64,128,256]{2,1,0:T(8,128)} %get-tuple-element.49.in_ref), custom_call_target="tpu_custom_call" | custom-call | bytes 1024 | tf_op jit(solution)/shard_map/pallas_call | solution.py:528
  386.7 6.5 %all-to-all-start.6 = ((bf16[8,1024,256]{2,1,0:T(8,128)(2,1)}), bf16[8,1024,256]{2,1,0:T(8,128)(2,1)}, u32[]{:S(2)}, u32[]{:S(2)}) async-start(bf16[8,1024,256]{2,1,0:T(8,128)(2,1)} %get-tuple-element.51), calls=%async_computation.6 | async-start | bytes 8388608 | tf_op jit(solution)/shard_map/all_to_all | solution.py:589
  397.4 86.7 %collective-permute-done.2 = bf16[8,128,128]{2,1,0:T(8,128)(2,1)S(1)} collective-permute-done((bf16[8,128,128]{2,1,0:T(8,128)(2,1)}, bf16[8,128,128]{2,1,0:T(8,128)(2,1)S(1)}, u32[]{:S(2)}, u32[]{:S(2)}) %collective-permute-start.2) | collective-permute-done | bytes 262176 | tf_op jit(solution)/shard_map/ppermute | solution.py:594
  489.2 5.1 all-to-all-start.5
  494.7 32.1 %collective-permute-done.8 = bf16[8,128,128]{2,1,0:T(8,128)(2,1)S(1)} collective-permute-done((bf16[8,128,128]{2,1,0:T(8,128)(2,1)S(1)}, bf16[8,128,128]{2,1,0:T(8,128)(2,1)S(1)}, u32[]{:S(2)}, u32[]{:S(2)}) %collective-permute-start.8) | collective-permute-done | bytes 262176 | tf_op jit(solution)/shard_map/ppermute | solution.py:594
  527.6 4.4 all-to-all-start.7
  532.0 2.3 reshape.44
  534.3 2.2 reduce_sum.22
  539.9 5.2 shard_map.148
  545.8 3.4 shard_map.147
  (71 shorter events, 19.2 us)
Async XLA Ops:
  9.3 11.7 %all-to-all-start = ((bf16[8,136,256]{2,1,0:T(8,128)(2,1)}), bf16[8,136,256]{2,1,0:T(8,128)(2,1)S(1)}, u32[]{:S(2)}, u32[]{:S(2)}) async-start(bf16[8,136,256]{2,1,0:T(8,128)(2,1)} %shard_map.138), calls=%async_computation | async-start | bytes 1114112 | tf_op jit(solution)/shard_map/all_to_all | solution.py:589
  21.0 0.8 copy-start.3
  21.9 29.6 %all-to-all-start.1 = ((bf16[8,520,256]{2,1,0:T(8,128)(2,1)}), bf16[8,520,256]{2,1,0:T(8,128)(2,1)S(1)}, u32[]{:S(2)}, u32[]{:S(2)}) async-start(bf16[8,520,256]{2,1,0:T(8,128)(2,1)} %shard_map.137), calls=%async_computation.1 | async-start | bytes 4259840 | tf_op jit(solution)/shard_map/all_to_all | solution.py:589
  51.4 38.2 %copy-start = (bf16[8,520,256]{2,1,0:T(8,128)(2,1)}, bf16[8,520,256]{2,1,0:T(8,128)(2,1)S(1)}, u32[]{:S(2)}) copy-start(bf16[8,520,256]{2,1,0:T(8,128)(2,1)S(1)} %all-to-all-done.1.refs_1_) | copy-start | bytes 6389764
  51.4 18.3 %all-to-all-start.2 = ((bf16[8,264,256]{2,1,0:T(8,128)(2,1)}), bf16[8,264,256]{2,1,0:T(8,128)(2,1)S(1)}, u32[]{:S(2)}, u32[]{:S(2)}) async-start(bf16[8,264,256]{2,1,0:T(8,128)(2,1)} %shard_map.139), calls=%async_computation.2 | async-start | bytes 2162688 | tf_op jit(solution)/shard_map/all_to_all | solution.py:589
  56.9 18.9 %copy-start.11 = (s32[128]{0:T(128)S(1)}, s32[128]{0:T(128)}, u32[]{:S(2)}) copy-start(s32[128]{0:T(128)} %param.19) | copy-start | bytes 1540
  56.9 18.9 %copy-start.8 = (bf16[1,128,1024]{2,1,0:T(8,128)(2,1)S(1)}, bf16[1,128,1024]{2,1,0:T(8,128)(2,1)}, u32[]{:S(2)}) copy-start(bf16[1,128,1024]{2,1,0:T(8,128)(2,1)} %param.17) | copy-start | bytes 786436
  69.7 22.4 %copy-start.2 = (bf16[8,264,256]{2,1,0:T(8,128)(2,1)}, bf16[8,264,256]{2,1,0:T(8,128)(2,1)S(1)}, u32[]{:S(2)}) copy-start(bf16[8,264,256]{2,1,0:T(8,128)(2,1)S(1)} %all-to-all-done.2.refs_2_) | copy-start | bytes 3244036
  69.7 13.5 %all-to-all-start.3 = ((bf16[8,136,256]{2,1,0:T(8,128)(2,1)}), bf16[8,136,256]{2,1,0:T(8,128)(2,1)}, u32[]{:S(2)}, u32[]{:S(2)}) async-start(bf16[8,136,256]{2,1,0:T(8,128)(2,1)} %shard_map.140), calls=%async_computation.3 | async-start | bytes 1114112 | tf_op jit(solution)/shard_map/all_to_all | solution.py:589
  83.2 8.8 %copy-start.9 = (s32[128,3]{0,1:T(4,128)S(1)}, s32[128,3]{0,1:T(4,128)}, u32[]{:S(2)}) copy-start(s32[128,3]{0,1:T(4,128)} %param.18) | copy-start | bytes 4612
  83.2 109.0 %all-to-all-start.4 = ((bf16[8,1152,256]{2,1,0:T(8,128)(2,1)}), bf16[8,1152,256]{2,1,0:T(8,128)(2,1)}, u32[]{:S(2)}, u32[]{:S(2)}) async-start(bf16[8,1152,256]{2,1,0:T(8,128)(2,1)} %shard_map.141), calls=%async_computation.4 | async-start | bytes 9437184 | tf_op jit(solution)/shard_map/all_to_all | solution.py:589
  89.6 248.1 %collective-permute-start.3 = (bf16[8,520,256]{2,1,0:T(8,128)(2,1)S(1)}, bf16[8,520,256]{2,1,0:T(8,128)(2,1)}, u32[]{:S(2)}, u32[]{:S(2)}) collective-permute-start(bf16[8,520,256]{2,1,0:T(8,128)(2,1)S(1)} %all-to-all-done.1.refs_1_), channel_id=1, source_target_pairs={{0,16},{2,18},{4,20},{6,22},{8,24},{10,26},{12,28},{14,30},{16,0},... | collective-permute-start | bytes 6389768 | tf_op jit(solution)/shard_map/ppermute | solution.py:594
  92.2 266.8 %collective-permute-start.5 = (bf16[8,264,256]{2,1,0:T(8,128)(2,1)S(1)}, bf16[8,264,256]{2,1,0:T(8,128)(2,1)}, u32[]{:S(2)}, u32[]{:S(2)}) collective-permute-start(bf16[8,264,256]{2,1,0:T(8,128)(2,1)S(1)} %all-to-all-done.2.refs_2_), channel_id=1, source_target_pairs={{0,16},{2,18},{4,20},{6,22},{8,24},{10,26},{12,28},{14,30},{16,0},... | collective-permute-start | bytes 3244040 | tf_op jit(solution)/shard_map/ppermute | solution.py:594
  93.3 231.2 %collective-permute-start.1 = (bf16[8,136,256]{2,1,0:T(8,128)(2,1)}, bf16[8,136,256]{2,1,0:T(8,128)(2,1)}, u32[]{:S(2)}, u32[]{:S(2)}) collective-permute-start(bf16[8,136,256]{2,1,0:T(8,128)(2,1)} %copy-done.3), channel_id=1, source_target_pairs={{0,16},{2,18},{4,20},{6,22},{8,24},{10,26},{12,28},{14,30},{16,0},... | collective-permute-start | bytes 1671176 | tf_op jit(solution)/shard_map/ppermute | solution.py:594
  95.7 278.6 %collective-permute-start.7 = (bf16[8,136,256]{2,1,0:T(8,128)(2,1)}, bf16[8,136,256]{2,1,0:T(8,128)(2,1)}, u32[]{:S(2)}, u32[]{:S(2)}) collective-permute-start(bf16[8,136,256]{2,1,0:T(8,128)(2,1)} %all-to-all-done.3.refs_3_), channel_id=1, source_target_pairs={{0,16},{2,18},{4,20},{6,22},{8,24},{10,26},{12,28},{14,30},{16,0},... | collective-permute-start | bytes 1671176 | tf_op jit(solution)/shard_map/ppermute | solution.py:594
  193.3 86.6 %collective-permute-start = (bf16[128,256]{1,0:T(8,128)(2,1)S(1)}, bf16[128,256]{1,0:T(8,128)(2,1)S(1)}, u32[]{:S(2)}, u32[]{:S(2)}) collective-permute-start(bf16[128,256]{1,0:T(8,128)(2,1)S(1)} %slice_reduce_fusion), channel_id=1, source_target_pairs={{0,16},{2,18},{4,20},{6,22},{8,24},{10,26},{12,28},{14,30},{16,0},... | collective-permute-start | bytes 196616 | tf_op jit(solution)/shard_map/ppermute | solution.py:594
  386.7 98.5 %copy-start.6 = (f32[8,256,128]{2,1,0:T(8,128)S(1)}, f32[8,256,128]{2,1,0:T(8,128)}, u32[]{:S(2)}) copy-start(f32[8,256,128]{2,1,0:T(8,128)} %get-tuple-element.45) | copy-start | bytes 3145732
  386.7 102.5 %all-to-all-start.6 = ((bf16[8,1024,256]{2,1,0:T(8,128)(2,1)}), bf16[8,1024,256]{2,1,0:T(8,128)(2,1)}, u32[]{:S(2)}, u32[]{:S(2)}) async-start(bf16[8,1024,256]{2,1,0:T(8,128)(2,1)} %get-tuple-element.51), calls=%async_computation.6 | async-start | bytes 8388608 | tf_op jit(solution)/shard_map/all_to_all | solution.py:589
  393.2 93.2 %copy-start.4 = (f32[8,512,128]{2,1,0:T(8,128)S(1)}, f32[8,512,128]{2,1,0:T(8,128)}, u32[]{:S(2)}) copy-start(f32[8,512,128]{2,1,0:T(8,128)} %get-tuple-element.42) | copy-start | bytes 6291460
  393.2 138.8 %all-gather.3.cloned.1.call-start = ((), (), s32[]{:S(2)}) async-start(), calls=%async_computation.8 | async-start | bytes 2228224 | tf_op jit(solution)/shard_map/all_gather | solution.py:631
  393.2 93.2 %collective-permute-start.4 = (bf16[8,512,128]{2,1,0:T(8,128)(2,1)}, bf16[8,512,128]{2,1,0:T(8,128)(2,1)}, u32[]{:S(2)}, u32[]{:S(2)}) collective-permute-start(bf16[8,512,128]{2,1,0:T(8,128)(2,1)} %get-tuple-element.44), channel_id=1, source_target_pairs={{0,16},{2,18},{4,20},{6,22},{8,24},{10,26},{12,28},{14,30},{16,0},... | collective-permute-start | bytes 3145736 | tf_op jit(solution)/shard_map/ppermute | solution.py:594
  395.0 90.2 %collective-permute-start.6 = (bf16[8,256,128]{2,1,0:T(8,128)(2,1)}, bf16[8,256,128]{2,1,0:T(8,128)(2,1)}, u32[]{:S(2)}, u32[]{:S(2)}) collective-permute-start(bf16[8,256,128]{2,1,0:T(8,128)(2,1)} %get-tuple-element.47), channel_id=1, source_target_pairs={{0,16},{2,18},{4,20},{6,22},{8,24},{10,26},{12,28},{14,30},{16,0},... | collective-permute-start | bytes 1572872 | tf_op jit(solution)/shard_map/ppermute | solution.py:594
  395.7 88.5 %collective-permute-start.2 = (bf16[8,128,128]{2,1,0:T(8,128)(2,1)}, bf16[8,128,128]{2,1,0:T(8,128)(2,1)S(1)}, u32[]{:S(2)}, u32[]{:S(2)}) collective-permute-start(bf16[8,128,128]{2,1,0:T(8,128)(2,1)} %get-tuple-element.41), channel_id=1, source_target_pairs={{0,16},{2,18},{4,20},{6,22},{8,24},{10,26},{12,28},{14,30},{16,0},... | collective-permute-start | bytes 786440 | tf_op jit(solution)/shard_map/ppermute | solution.py:594
  489.2 5.1 copy-start.10
  489.2 37.6 %copy-start.7 = (f32[8,128,128]{2,1,0:T(8,128)S(1)}, f32[8,128,128]{2,1,0:T(8,128)}, u32[]{:S(2)}) copy-start(f32[8,128,128]{2,1,0:T(8,128)} %get-tuple-element.48) | copy-start | bytes 1572868
  489.2 38.4 %all-to-all-start.5 = ((bf16[8,896,128]{2,1,0:T(8,128)(2,1)}), bf16[8,896,128]{2,1,0:T(8,128)(2,1)S(1)}, u32[]{:S(2)}, u32[]{:S(2)}) async-start(bf16[8,896,128]{2,1,0:T(8,128)(2,1)} %pad_maximum_fusion), calls=%async_computation.5 | async-start | bytes 3670016 | tf_op jit(solution)/shard_map/all_to_all | solution.py:589
  494.4 32.5 %collective-permute-start.8 = (bf16[8,128,128]{2,1,0:T(8,128)(2,1)S(1)}, bf16[8,128,128]{2,1,0:T(8,128)(2,1)S(1)}, u32[]{:S(2)}, u32[]{:S(2)}) collective-permute-start(bf16[8,128,128]{2,1,0:T(8,128)(2,1)S(1)} %copy-done.10), channel_id=1, source_target_pairs={{0,16},{2,18},{4,20},{6,22},{8,24},{10,26},{12,28},{14,30},{16,0},... | collective-permute-start | bytes 786440 | tf_op jit(solution)/shard_map/ppermute | solution.py:594
  527.6 4.4 copy-start.1
  527.6 17.5 %all-to-all-start.7 = ((bf16[8,128,128]{2,1,0:T(8,128)(2,1)}), bf16[8,128,128]{2,1,0:T(8,128)(2,1)S(1)}, u32[]{:S(2)}, u32[]{:S(2)}) async-start(bf16[8,128,128]{2,1,0:T(8,128)(2,1)} %add_convert_fusion.2), calls=%async_computation.7 | async-start | bytes 524288 | tf_op jit(solution)/shard_map/all_to_all | solution.py:589
  545.1 0.7 copy-start.5
Sparse Core Ops, SparseCore 0:
  397.6 115.6 all-gather.2

commit v3 on v1

--- a/solution.py
+++ b/solution.py
@@ -181,7 +181,7 @@
     )
 
 
-def body(
+def body_shared(
     queries,
     keys,
     values,
@@ -262,6 +262,333 @@
     return (grad_queries, grad_keys, grad_values, glob_grads[0], glob_grads[1])
 
 
+PAD = 8
+CHUNKS = 2
+VMEM_LIMIT = 60 * 1024 * 1024
+
+
+def split_two(row):
+    high = row.astype(jnp.bfloat16).astype(jnp.float32)
+    return jnp.concatenate([high, row - high], axis=1)
+
+
+def pack_kernel(query_ref, grad_ref, saved_ref, norm_ref, *refs):
+    *kv_refs, out_ref = refs
+    rows = query_ref.shape[0]
+    base = out_ref.shape[2] - rows - PAD
+    for head in range(out_ref.shape[0]):
+        cols = slice(head * HD, (head + 1) * HD)
+        for which, kv_ref in enumerate(kv_refs):
+            out_ref[head, 0, :base, which * HD : (which + 1) * HD] = kv_ref[:, cols]
+        grad = grad_ref[:, cols]
+        out_ref[head, 0, base : base + rows, :HD] = query_ref[:, cols]
+        out_ref[head, 0, base : base + rows, HD:] = grad
+        product = grad.astype(jnp.float32) * saved_ref[:, cols].astype(jnp.float32)
+        delta = jnp.sum(product.T, axis=0, keepdims=True)
+        norm = norm_ref[head : head + 1, :]
+        stats = []
+        for block in range(rows // BLK):
+            lanes = slice(block * BLK, (block + 1) * BLK)
+            stats += [split_two(norm[:, lanes]), split_two(delta[:, lanes])]
+        stats.append(jnp.zeros((PAD - len(stats), 2 * HD), jnp.float32))
+        out_ref[head, 0, base + rows :, :] = jnp.concatenate(stats, axis=0).astype(jnp.bfloat16)
+
+
+def pack(queries, grad_output, saved_output, log_norm, chunk, share, *kv):
+    tokens, features = queries.shape
+    heads = features // HD
+    part = tokens // share
+    rows = part // CHUNKS
+    base = part if kv else 0
+    height = base + rows + PAD
+    spec = pl.BlockSpec((rows, features), lambda s: (s * CHUNKS + chunk, 0))
+    out = pl.pallas_call(
+        pack_kernel,
+        grid=(share,),
+        in_specs=[spec] * 3
+        + [pl.BlockSpec((heads, rows), lambda s: (0, s * CHUNKS + chunk))]
+        + [pl.BlockSpec((part, features), lambda s: (s, 0))] * len(kv),
+        out_specs=pl.BlockSpec((heads, 1, height, 2 * HD), lambda s: (0, s, 0, 0)),
+        out_shape=jax.ShapeDtypeStruct((heads, share, height, 2 * HD), jnp.bfloat16),
+        compiler_params=pltpu.CompilerParams(vmem_limit_bytes=VMEM_LIMIT),
+        cost_estimate=pl.CostEstimate(
+            flops=0, bytes_accessed=share * height * features * 8, transcendentals=0
+        ),
+    )(queries, grad_output, saved_output, log_norm, *kv)
+    return out.reshape(heads * share, height, 2 * HD)
+
+
+def pair_grads(pair, stats, rows):
+    zero = jnp.zeros((BLK, HD), jnp.bfloat16)
+    mixed = jnp.concatenate(
+        [
+            jnp.concatenate([pair[:, :HD], zero], axis=1),
+            jnp.concatenate([zero, pair[:, HD:]], axis=1),
+        ],
+        axis=0,
+    )
+    norm = (stats[0:1, :HD] + stats[0:1, HD:]) * LOG2E
+    delta = stats[1:2, :HD] + stats[1:2, HD:]
+    rows = jnp.concatenate(rows, axis=0)
+    both = lax.dot_general(
+        rows, mixed, (((1,), (1,)), ((), ())), preferred_element_type=jnp.float32
+    )
+    attend = jnp.exp2(both[:, :HD] * (FACTOR * LOG2E) - norm)
+    grad_scores = attend * (both[:, HD:] - delta)
+    scores_low = grad_scores.astype(jnp.bfloat16)
+    grad_kv = jnp.dot(
+        jnp.concatenate([scores_low, attend.astype(jnp.bfloat16)], axis=1),
+        mixed,
+        preferred_element_type=jnp.float32,
+    )
+    grad_q = lax.dot_general(
+        scores_low, rows[:, :HD], (((0,), (0,)), ((), ())), preferred_element_type=jnp.float32
+    )
+    return grad_kv, grad_q * FACTOR
+
+
+def chunk_kernel(last, base, table_ref, glob_ref, own_ref, mate_ref, pair_ref, *refs):
+    if last:
+        before_ref, glob_before_ref, dq_ref, keep_ref, give_ref, dglob_ref = refs[:6]
+        kv, pairs, acc, sems, before, stage, out_sems = refs[6:]
+    else:
+        dq_ref, sum_ref, dglob_ref, kv, pairs, acc, sems = refs
+    sources = pairs.shape[0]
+    blocks = (pairs.shape[1] - PAD) // BLK
+    sub = kv.shape[1] // BLK
+    total = acc.shape[0]
+    kinds = W + R
+    copies = [
+        pltpu.make_async_copy(
+            own_ref.at[:, pl.ds(0, sub * BLK), :], kv.at[pl.ds(0, sources)], sems.at[0]
+        ),
+        pltpu.make_async_copy(
+            mate_ref.at[:, pl.ds(0, sub * BLK), :], kv.at[pl.ds(sources, sources)], sems.at[1]
+        ),
+        pltpu.make_async_copy(
+            pair_ref.at[:, pl.ds(base, pairs.shape[1]), :], pairs, sems.at[2]
+        ),
+    ]
+    for copy in copies:
+        copy.start()
+    if last:
+        earlier = pltpu.make_async_copy(before_ref, before, sems.at[3])
+        earlier.start()
+        dglob_ref[...] = glob_before_ref[...]
+    else:
+        dglob_ref[...] = jnp.zeros_like(dglob_ref)
+
+    def clear(block, carry):
+        acc[block] = jnp.zeros((BLK, 2 * HD), jnp.float32)
+        return carry
+
+    lax.fori_loop(0, total, clear, 0)
+    for copy in copies:
+        copy.wait()
+
+    def one_source(source, carry):
+        stats = pairs[source, blocks * BLK :, :].astype(jnp.float32)
+        for inner in range(blocks):
+            lines = slice(inner * BLK, (inner + 1) * BLK)
+            entry = (source * blocks + inner) * kinds
+            places = [table_ref[entry + kind] for kind in range(kinds)]
+            rows = [
+                kv[place // sub, pl.ds(pl.multiple_of((place % sub) * BLK, BLK), BLK), :]
+                for place in places
+            ]
+            grad_kv, grad_q = pair_grads(
+                pairs[source, lines, :], stats[2 * inner : 2 * inner + 2], rows + [glob_ref[...]]
+            )
+            for kind, place in enumerate(places):
+                acc[place] += grad_kv[kind * BLK : (kind + 1) * BLK]
+            dglob_ref[...] += grad_kv[kinds * BLK :]
+            dq_ref[source, lines, :] = grad_q.astype(jnp.bfloat16)
+        return carry
+
+    lax.fori_loop(0, sources, one_source, 0)
+    if not last:
+        leave = pltpu.make_async_copy(acc, sum_ref, sems.at[3])
+        leave.start()
+        leave.wait()
+        return
+    dglob_ref[:, :HD] = dglob_ref[:, :HD] * FACTOR
+    earlier.wait()
+
+    def copy_out(group):
+        slot = group % 2
+        out = keep_ref.at[group] if group < sources else give_ref.at[group - sources]
+        return pltpu.make_async_copy(stage.at[slot], out, out_sems.at[slot])
+
+    groups = total // sub
+    for group in range(groups):
+        if group >= 2:
+            copy_out(group - 2).wait()
+        for inner in range(sub):
+            value = acc[group * sub + inner] + before[group * sub + inner]
+            lines = slice(inner * BLK, (inner + 1) * BLK)
+            stage[group % 2, lines, :HD] = (value[:, :HD] * FACTOR).astype(jnp.bfloat16)
+            stage[group % 2, lines, HD:] = value[:, HD:].astype(jnp.bfloat16)
+        copy_out(group).start()
+    for group in range(max(0, groups - 2), groups):
+        copy_out(group).wait()
+
+
+def chunk_call(table, glob, own, mate, pairs, base, part, before=None):
+    sources = own.shape[0]
+    rows = pairs.shape[1] - base - PAD
+    total = 2 * sources * (part // BLK)
+    last = before is not None
+    vmem = pl.BlockSpec(memory_space=pltpu.VMEM)
+    smem = pl.BlockSpec(memory_space=pltpu.SMEM)
+    hbm = pl.BlockSpec(memory_space=pl.ANY)
+    sums = jax.ShapeDtypeStruct((total, BLK, 2 * HD), jnp.float32)
+    rounded = jax.ShapeDtypeStruct((sources, part, 2 * HD), jnp.bfloat16)
+    scratch = [
+        pltpu.VMEM((2 * sources, part, 2 * HD), jnp.bfloat16),
+        pltpu.VMEM((sources, rows + PAD, 2 * HD), jnp.bfloat16),
+        pltpu.VMEM(sums.shape, jnp.float32),
+        pltpu.SemaphoreType.DMA((4,)),
+    ]
+    if last:
+        scratch += [
+            pltpu.VMEM(sums.shape, jnp.float32),
+            pltpu.VMEM((2, part, 2 * HD), jnp.bfloat16),
+            pltpu.SemaphoreType.DMA((2,)),
+        ]
+    units = sources * (rows // BLK) * (W + R + 1)
+    return pl.pallas_call(
+        functools.partial(chunk_kernel, last, base),
+        in_specs=[smem, vmem, hbm, hbm, hbm] + [hbm, vmem] * last,
+        out_specs=[vmem] + [hbm] * (2 if last else 1) + [vmem],
+        out_shape=[jax.ShapeDtypeStruct((sources, rows, HD), jnp.bfloat16)]
+        + ([rounded] * 2 if last else [sums])
+        + [
+            jax.ShapeDtypeStruct((G, 2 * HD), jnp.float32),
+        ],
+        scratch_shapes=scratch,
+        compiler_params=pltpu.CompilerParams(vmem_limit_bytes=VMEM_LIMIT),
+        cost_estimate=pl.CostEstimate(
+            flops=units * 16 * BLK * BLK * HD,
+            bytes_accessed=total * BLK * HD * 16,
+            transcendentals=units * BLK * BLK,
+        ),
+    )(table, glob, own, mate, pairs, *(before or ()))
+
+
+def unpack_kernel(share, *refs):
+    *in_refs, out_ref = refs
+    rows = in_refs[0].shape[1]
+    for chunk, in_ref in enumerate(in_refs):
+        for index in range(in_ref.shape[0]):
+            start = ((index % share) * CHUNKS + chunk) * rows
+            head = index // share
+            out_ref[start : start + rows, head * HD : (head + 1) * HD] = in_ref[index]
+
+
+def unpack_queries(arrays, share):
+    size, rows, _ = arrays[0].shape
+    vmem = pl.BlockSpec(memory_space=pltpu.VMEM)
+    shape = (share * CHUNKS * rows, size // share * HD)
+    return pl.pallas_call(
+        functools.partial(unpack_kernel, share),
+        in_specs=[vmem] * len(arrays),
+        out_specs=vmem,
+        out_shape=jax.ShapeDtypeStruct(shape, jnp.bfloat16),
+        compiler_params=pltpu.CompilerParams(vmem_limit_bytes=VMEM_LIMIT),
+        cost_estimate=pl.CostEstimate(
+            flops=0, bytes_accessed=shape[0] * shape[1] * 4, transcendentals=0
+        ),
+    )(*arrays)
+
+
+def body_chunks(
+    queries,
+    keys,
+    values,
+    saved_output,
+    grad_output,
+    log_norm,
+    global_keys,
+    global_values,
+    flow_links,
+    glob_owner,
+):
+    size = lax.axis_size("seq")
+    my_index = lax.axis_index("seq")
+    tokens, features = queries.shape
+    heads = features // HD
+    blocks = tokens // BLK
+    share = size // heads
+    part = tokens // share
+    sub = part // BLK
+    mine = my_index % share
+
+    owned = (glob_owner == my_index)[:, None, None]
+    glob_pair = jnp.concatenate(
+        [global_keys.reshape(G, heads, HD), global_values.reshape(G, heads, HD)], axis=2
+    )
+    glob_out = jnp.transpose(jnp.where(owned, glob_pair, jnp.bfloat16(0)), (1, 0, 2))
+    glob_half = lax.psum_scatter(
+        glob_out.reshape(size, G // share, 2 * HD), "seq", scatter_dimension=0, tiled=False
+    )
+    first = exchange(
+        pack(queries, grad_output, saved_output, log_norm, 0, share, keys, values)
+    )
+    packed = pack(queries, grad_output, saved_output, log_norm, 1, share)
+    packed, first, glob_half = lax.optimization_barrier((packed, first, glob_half))
+    second = exchange(packed)
+    mate = to_mate(first, 1, share)
+    glob_mate = to_mate(glob_half, 1, share)
+    glob_now = jnp.where(
+        mine == 0,
+        jnp.concatenate([glob_half, glob_mate], axis=0),
+        jnp.concatenate([glob_mate, glob_half], axis=0),
+    )
+
+    count = size * sub
+    order = jnp.arange(count, dtype=jnp.int32)
+    my_blocks = (order // sub) * blocks + mine * sub + order % sub
+    near = my_blocks[:, None] + jnp.arange(-1, 2, dtype=jnp.int32)[None, :]
+    links = lax.dynamic_index_in_dim(
+        flow_links.reshape(size, share, sub, R), mine, axis=1, keepdims=False
+    ).reshape(count, R)
+    wanted = jnp.concatenate([(near + size * blocks) % (size * blocks), links], axis=1)
+    within = wanted % blocks
+    offset = (within // sub - mine + share) % share
+    table = (offset * count + (wanted // blocks) * sub + within % sub).astype(jnp.int32)
+    tables = table.reshape(size, CHUNKS, -1)
+
+    dq_first, sums, dglob = chunk_call(
+        tables[:, 0].reshape(-1), glob_now, first, mate, first, part, part
+    )
+    dq_second, keep, give, dglob = chunk_call(
+        tables[:, 1].reshape(-1), glob_now, first, mate, second, 0, part, (sums, dglob)
+    )
+    back_first = exchange(dq_first)
+    dq_second, keep, give, dglob, back_first = lax.optimization_barrier(
+        (dq_second, keep, give, dglob, back_first)
+    )
+    back_second = exchange(dq_second)
+    dkv_sum = (keep.astype(jnp.float32) + to_mate(give, 1, share).astype(jnp.float32)).astype(
+        jnp.bfloat16
+    )
+    dkv_sum, back_second = lax.optimization_barrier((dkv_sum, back_second))
+    grad_keys, grad_values = unpair_heads(exchange(dkv_sum), share)
+    grad_queries = unpack_queries((back_first, back_second), share)
+    glob_parts = lax.all_gather(dglob, "seq", axis=0, tiled=False)
+    glob_sum = jnp.sum(glob_parts.reshape(heads, share, G, 2, HD), axis=1)
+    glob_grads = jnp.transpose(glob_sum, (2, 1, 0, 3)).reshape(2, G, features).astype(jnp.bfloat16)
+    return (grad_queries, grad_keys, grad_values, glob_grads[0], glob_grads[1])
+
+
+def body(queries, *rest):
+    tokens, features = queries.shape
+    share = lax.axis_size("seq") // (features // HD)
+    if share == 2 and tokens % (share * CHUNKS * BLK) == 0:
+        return body_chunks(queries, *rest)
+    return body_shared(queries, *rest)
+
+
 def solution(mesh):
     return jax.shard_map(
         body,

time: 499 us -> 413 us (0.83)
  waiting for transfers between devices: 326 us -> 266 us
  other arithmetic: 25.2 us -> 10.5 us
  local copies, waits for them, and re-layouts: 19.7 us -> 8.65 us
  Pallas kernels: 78.8 us -> 84.4 us
    all_to_all x6 -> x5, waiting for transfers between devices: 236 us -> 68.7 us  [exchange(): return lax.all_to_all(array, 'seq', split_axis=0, concat_axis=0, tiled=True)]
    reduce_scatter x0 -> x1, waiting for transfers between devices: none -> 108 us  [body_chunks(): lax.psum_scatter(glob_out.reshape(size, G // share, 2 * HD), 'seq', scatt...]
    pallas_call x3 -> x5, Pallas kernels: 69.6 us -> 79.2 us  [the longest x2 66.6 us: chunk_call(): pl.pallas_call(functools.partial(chunk_kernel, last, base), in_specs=[sme...]
    concatenate x3 -> x1, other arithmetic: 8.17 us -> 0.01 us  [body_chunks(): jnp.concatenate([(near + size * blocks) % (size * blocks), links], axis=1)]
    slice x5 -> x4, local copies, waits for them, and re-layouts: 7.68 us -> 1.74 us  [the longest x3 1.7 us: body_chunks(): return (grad_queries, grad_keys, grad_values, glob_grads[0], glob_grads[1])]
    all_to_all x6 -> x5, starting transfers between devices: 32.6 us -> 27.3 us  [exchange(): return lax.all_to_all(array, 'seq', split_axis=0, concat_axis=0, tiled=True)]
  transfers between devices with their start and end apart: 9 -> 10, of which waited for: 9 -> 8; matrix products, arithmetic and copies ran while one was open for 5% -> 4% of each run, Pallas kernels for 3% -> 18%
where the time goes in v3:
time: 413 us; the launch traced here: 412 us
  waiting for transfers between devices  266 us (64%)
  Pallas kernels  84.4 us (20%)
  starting transfers between devices  28.6 us (7%)
  between operations  14.3 us (3%)
  other arithmetic  10.5 us (3%)
  local copies, waits for them, and re-layouts  8.65 us (2%)
    reduce_scatter x1, waiting for transfers between devices, body_chunks(): lax.psum_scatter(glob_out.reshape(size, G // share, 2 * HD), 'seq', scatt...  108 us
    all_gather x1, waiting for transfers between devices, body_chunks(): glob_parts = lax.all_gather(dglob, 'seq', axis=0, tiled=False)  84.1 us
    all_to_all x5, waiting for transfers between devices, exchange(): return lax.all_to_all(array, 'seq', split_axis=0, concat_axis=0, tiled=True)  68.7 us
    pallas_call x2, Pallas kernels, chunk_call(): pl.pallas_call(functools.partial(chunk_kernel, last, base), in_specs=[sme...  66.6 us
    all_to_all x5, starting transfers between devices, exchange(): return lax.all_to_all(array, 'seq', split_axis=0, concat_axis=0, tiled=True)  27.3 us
    pallas_call x2, Pallas kernels, pack(): pl.pallas_call(pack_kernel, grid=(share,), in_specs=[spec] * 3 + [pl.Bloc...  9.18 us
  transfers between devices with their start and end apart: 10, of which 8 were waited for; matrix products, arithmetic and copies ran while one was open for 4% of the time, Pallas kernels for 18%

profile of v3, /device:TPU:15, one launch (start us, length us, event | category | flops | bytes accessed | tf_op | source)
XLA Modules:
  0.0 412.1 jit_solution(2874365809280158560)
XLA Ops:
  7.2 5.8 %shard_map.138 = bf16[8,2,776,256]{3,2,1,0:T(8,128)(2,1)} custom-call(bf16[1024,1024]{1,0:T(8,128)(2,1)} %query_ref.3, bf16[1024,1024]{1,0:T(8,128)(2,1)} %grad_ref.3, bf16[1024,1024]{1,0:T(8,128)(2,1)} %saved_ref.3, f32[8,1024]{1,0:T(8,128)} %norm_ref.3, bf16[1024,1024]{1,0:T(8,128)(2,1)} %refs_0_.1, bf16[1024,1024]{1,0:T(8,128)(2,1)} %refs_1_.1), custom_call_target="tpu_custom_call" | custom-call | bytes 12713984 | tf_op jit(solution)/shard_map/pallas_call | solution.py:305
  13.0 6.7 %all-to-all-start = ((bf16[16,776,256]{2,1,0:T(8,128)(2,1)}), bf16[16,776,256]{2,1,0:T(8,128)(2,1)}, u32[]{:S(2)}, u32[]{:S(2)}) async-start(bf16[16,776,256]{2,1,0:T(8,128)(2,1)} %bitcast.22), calls=%async_computation | async-start | bytes 12713984 | tf_op jit(solution)/shard_map/all_to_all | solution.py:174
  20.0 0.9 maximum_select_fusion
  20.9 3.4 shard_map.137
  24.3 107.7 %reduce-scatter.2.cloned.1.call-done = bf16[1,64,256]{2,1,0:T(8,128)(2,1)} async-done(((bf16[16,64,256]{2,1,0:T(8,128)(2,1)}), bf16[1,64,256]{2,1,0:T(8,128)(2,1)}) %reduce-scatter.2.cloned.1.call-update) | async-done | bytes 32784 | tf_op jit(solution)/shard_map/reduce_scatter | solution.py:531
  132.0 29.7 %all-to-all-done.own_ref.pair_ref = bf16[16,776,256]{2,1,0:T(8,128)(2,1)} async-done(((bf16[16,776,256]{2,1,0:T(8,128)(2,1)}), bf16[16,776,256]{2,1,0:T(8,128)(2,1)}, u32[]{:S(2)}, u32[]{:S(2)}) %all-to-all-start) | async-done | bytes 6357024 | tf_op jit(solution)/shard_map/all_to_all | solution.py:174
  161.9 4.9 %all-to-all-start.1 = ((bf16[16,264,256]{2,1,0:T(8,128)(2,1)}), bf16[16,264,256]{2,1,0:T(8,128)(2,1)S(1)}, u32[]{:S(2)}, u32[]{:S(2)}) async-start(bf16[16,264,256]{2,1,0:T(8,128)(2,1)} %bitcast.23), calls=%async_computation.2 | async-start | bytes 4325376 | tf_op jit(solution)/shard_map/all_to_all | solution.py:174
  168.1 0.7 reshape_squeeze.7.table_ref
  168.8 3.3 collective-permute-done
  172.1 0.6 maximum_select_fusion.1.glob_ref
  172.7 29.9 %shard_map.139 = (bf16[16,256,128]{2,1,0:T(8,128)(2,1)}, f32[128,128,256]{2,1,0:T(8,128)}, f32[128,256]{1,0:T(8,128)}) custom-call(s32[192]{0:T(256)} %reshape_squeeze.7.table_ref, bf16[128,256]{1,0:T(8,128)(2,1)} %maximum_select_fusion.1.glob_ref, bf16[16,776,256]{2,1,0:T(8,128)(2,1)} %all-to-all-done.own_ref.pair_ref, ...), custom_call_target="tpu_custom_call" | custom-call | flops 7516192768 | bytes 33554432 | tf_op jit(solution)/shard_map/pallas_call | solution.py:459
  202.6 13.1 %all-to-all-done.1.pair_ref = bf16[16,264,256]{2,1,0:T(8,128)(2,1)S(1)} async-done(((bf16[16,264,256]{2,1,0:T(8,128)(2,1)}), bf16[16,264,256]{2,1,0:T(8,128)(2,1)S(1)}, u32[]{:S(2)}, u32[]{:S(2)}) %all-to-all-start.1) | async-done | bytes 2162720 | tf_op jit(solution)/shard_map/all_to_all | solution.py:174
  215.7 4.9 %all-to-all-start.2 = ((bf16[16,256,128]{2,1,0:T(8,128)(2,1)}), bf16[16,256,128]{2,1,0:T(8,128)(2,1)S(1)}, u32[]{:S(2)}, u32[]{:S(2)}) async-start(bf16[16,256,128]{2,1,0:T(8,128)(2,1)} %get-tuple-element.33), calls=%async_computation.3 | async-start | bytes 2097152 | tf_op jit(solution)/shard_map/all_to_all | solution.py:174
  220.6 0.6 reshape_squeeze.6.table_ref
  221.2 36.7 %shard_map.140 = (bf16[16,256,128]{2,1,0:T(8,128)(2,1)}, bf16[16,512,256]{2,1,0:T(8,128)(2,1)}, bf16[16,512,256]{2,1,0:T(8,128)(2,1)}, f32[128,256]{1,0:T(8,128)}) custom-call(s32[192]{0:T(256)} %reshape_squeeze.6.table_ref, bf16[128,256]{1,0:T(8,128)(2,1)} %maximum_select_fusion.1.glob_ref, bf16[16,776,256]{2,1,0:T(8,128)(2,1)} %all-to-all-done.own_ref.pair_ref, ...), custom_call_target="tpu_custom_call" | custom-call | flops 7516192768 | bytes 33554432 | tf_op jit(solution)/shard_map/pallas_call | solution.py:459
  257.9 0.4 collective-permute-start.2
  258.4 5.8 %all-to-all-start.3 = ((bf16[16,256,128]{2,1,0:T(8,128)(2,1)}), bf16[16,256,128]{2,1,0:T(8,128)(2,1)S(1)}, u32[]{:S(2)}, u32[]{:S(2)}) async-start(bf16[16,256,128]{2,1,0:T(8,128)(2,1)} %get-tuple-element.37), calls=%async_computation.4 | async-start | bytes 2097152 | tf_op jit(solution)/shard_map/all_to_all | solution.py:174
  264.2 1.3 collective-permute-done.2
  265.5 6.7 %add_convert_fusion = bf16[16,512,256]{2,1,0:T(8,128)(2,1)} fusion(bf16[16,512,256]{2,1,0:T(8,128)(2,1)} %collective-permute-done.2, bf16[16,512,256]{2,1,0:T(8,128)(2,1)} %get-tuple-element.35), kind=kLoop, calls=%fused_computation | loop fusion | flops 8388608 | bytes 12582912 | tf_op jit(solution)/shard_map/convert_element_type | solution.py:572
  272.3 16.8 %all-to-all-done.3.refs_1_ = bf16[16,256,128]{2,1,0:T(8,128)(2,1)S(1)} async-done(((bf16[16,256,128]{2,1,0:T(8,128)(2,1)}), bf16[16,256,128]{2,1,0:T(8,128)(2,1)S(1)}, u32[]{:S(2)}, u32[]{:S(2)}) %all-to-all-start.3) | async-done | bytes 1048608 | tf_op jit(solution)/shard_map/all_to_all | solution.py:174
  289.1 1.0 copy-done.2
  290.0 4.9 %all-to-all-start.4 = ((bf16[16,512,256]{2,1,0:T(8,128)(2,1)}), bf16[16,512,256]{2,1,0:T(8,128)(2,1)}, u32[]{:S(2)}, u32[]{:S(2)}) async-start(bf16[16,512,256]{2,1,0:T(8,128)(2,1)} %add_convert_fusion), calls=%async_computation.5 | async-start | bytes 8388608 | tf_op jit(solution)/shard_map/all_to_all | solution.py:174
  295.2 0.5 all-gather.3.cloned.1.call-update
  295.7 84.1 %all-gather.3.cloned.1.call-done = f32[2048,256]{1,0:T(8,128)} async-done(((f32[128,256]{1,0:T(8,128)}), f32[2048,256]{1,0:T(8,128)}) %all-gather.3.cloned.1.call-update) | async-done | bytes 2097168 | tf_op jit(solution)/shard_map/all_gather | solution.py:578
  379.9 2.3 reshape.82
  382.2 1.9 reduce_sum.9
  384.1 0.9 fusion.8
  385.4 0.9 copy.29
  386.7 0.9 copy.28
  387.5 3.5 shard_map.141
  391.0 9.1 %all-to-all-done.4 = bf16[16,512,256]{2,1,0:T(8,128)(2,1)} async-done(((bf16[16,512,256]{2,1,0:T(8,128)(2,1)}), bf16[16,512,256]{2,1,0:T(8,128)(2,1)}, u32[]{:S(2)}, u32[]{:S(2)}) %all-to-all-start.4) | async-done | bytes 4194336 | tf_op jit(solution)/shard_map/all_to_all | solution.py:174
  400.1 5.2 %shard_map.142 = (bf16[1024,1024]{1,0:T(8,128)(2,1)}, bf16[1024,1024]{1,0:T(8,128)(2,1)}) custom-call(bf16[8,2,512,256]{3,2,1,0:T(8,128)(2,1)} %bitcast.5.in_ref), custom_call_target="tpu_custom_call" | custom-call | bytes 8388608 | tf_op jit(solution)/shard_map/pallas_call | solution.py:63
  (40 shorter events, 2.7 us)
Async XLA Ops:
  13.0 6.8 %copy-start.3 = (bf16[1,128,1024]{2,1,0:T(8,128)(2,1)S(1)}, bf16[1,128,1024]{2,1,0:T(8,128)(2,1)}, u32[]{:S(2)}) copy-start(bf16[1,128,1024]{2,1,0:T(8,128)(2,1)} %param.16) | copy-start | bytes 786436
  13.0 6.9 %copy-start.4 = (bf16[1,128,1024]{2,1,0:T(8,128)(2,1)S(1)}, bf16[1,128,1024]{2,1,0:T(8,128)(2,1)}, u32[]{:S(2)}) copy-start(bf16[1,128,1024]{2,1,0:T(8,128)(2,1)} %param.17) | copy-start | bytes 786436
  13.0 7.0 %copy-start.7 = (s32[128]{0:T(128)S(1)}, s32[128]{0:T(128)}, u32[]{:S(2)}) copy-start(s32[128]{0:T(128)} %param.19) | copy-start | bytes 1540
  13.0 148.7 %all-to-all-start = ((bf16[16,776,256]{2,1,0:T(8,128)(2,1)}), bf16[16,776,256]{2,1,0:T(8,128)(2,1)}, u32[]{:S(2)}, u32[]{:S(2)}) async-start(bf16[16,776,256]{2,1,0:T(8,128)(2,1)} %bitcast.22), calls=%async_computation | async-start | bytes 12713984 | tf_op jit(solution)/shard_map/all_to_all | solution.py:174
  19.7 112.4 %reduce-scatter.2.cloned.1.call-start = ((), (), s32[]{:S(2)}) async-start(), calls=%async_computation.6 | async-start | bytes 557056 | tf_op jit(solution)/shard_map/reduce_scatter | solution.py:531
  24.3 142.5 %copy-start.6 = (s32[128,3]{0,1:T(4,128)S(1)}, s32[128,3]{0,1:T(4,128)}, u32[]{:S(2)}) copy-start(s32[128,3]{0,1:T(4,128)} %param.18) | copy-start | bytes 4612
  132.0 35.6 %copy-start.5 = (bf16[1,64,256]{2,1,0:T(8,128)(2,1)S(1)}, bf16[1,64,256]{2,1,0:T(8,128)(2,1)}, u32[]{:S(2)}) copy-start(bf16[1,64,256]{2,1,0:T(8,128)(2,1)} %reduce-scatter.2.cloned.1.call-done) | copy-start | bytes 98308
  161.7 11.0 %collective-permute-start.1 = (bf16[16,776,256]{2,1,0:T(8,128)(2,1)}, bf16[16,776,256]{2,1,0:T(8,128)(2,1)}, u32[]{:S(2)}, u32[]{:S(2)}) collective-permute-start(bf16[16,776,256]{2,1,0:T(8,128)(2,1)} %all-to-all-done.own_ref.pair_ref), channel_id=1, source_target_pairs={{0,2},{2,0},{4,6},{6,4},{8,10},{10,8},{12,14},{14,12},{16,18},{18,... | collective-permute-start | bytes 19070984 | tf_op jit(solution)/shard_map/ppermute | solution.py:179
  161.9 53.8 %all-to-all-start.1 = ((bf16[16,264,256]{2,1,0:T(8,128)(2,1)}), bf16[16,264,256]{2,1,0:T(8,128)(2,1)S(1)}, u32[]{:S(2)}, u32[]{:S(2)}) async-start(bf16[16,264,256]{2,1,0:T(8,128)(2,1)} %bitcast.23), calls=%async_computation.2 | async-start | bytes 4325376 | tf_op jit(solution)/shard_map/all_to_all | solution.py:174
  167.7 4.4 %collective-permute-start = (bf16[64,256]{1,0:T(8,128)(2,1)S(1)}, bf16[64,256]{1,0:T(8,128)(2,1)S(1)}, u32[]{:S(2)}, u32[]{:S(2)}) collective-permute-start(bf16[64,256]{1,0:T(8,128)(2,1)S(1)} %bitcast.32), channel_id=1, source_target_pairs={{0,2},{2,0},{4,6},{6,4},{8,10},{10,8},{12,14},{14,12},{16,18},{18,... | collective-permute-start | bytes 98312 | tf_op jit(solution)/shard_map/ppermute | solution.py:179
  215.7 5.5 %copy-start = (bf16[16,264,256]{2,1,0:T(8,128)(2,1)}, bf16[16,264,256]{2,1,0:T(8,128)(2,1)S(1)}, u32[]{:S(2)}) copy-start(bf16[16,264,256]{2,1,0:T(8,128)(2,1)S(1)} %all-to-all-done.1.pair_ref) | copy-start | bytes 6488068
  215.7 42.2 %all-to-all-start.2 = ((bf16[16,256,128]{2,1,0:T(8,128)(2,1)}), bf16[16,256,128]{2,1,0:T(8,128)(2,1)S(1)}, u32[]{:S(2)}, u32[]{:S(2)}) async-start(bf16[16,256,128]{2,1,0:T(8,128)(2,1)} %get-tuple-element.33), calls=%async_computation.3 | async-start | bytes 2097152 | tf_op jit(solution)/shard_map/all_to_all | solution.py:174
  257.9 14.3 %copy-start.1 = (bf16[16,256,128]{2,1,0:T(8,128)(2,1)}, bf16[16,256,128]{2,1,0:T(8,128)(2,1)S(1)}, u32[]{:S(2)}) copy-start(bf16[16,256,128]{2,1,0:T(8,128)(2,1)S(1)} %all-to-all-done.2.refs_0_) | copy-start | bytes 3145732
  257.9 7.6 %collective-permute-start.2 = (bf16[16,512,256]{2,1,0:T(8,128)(2,1)}, bf16[16,512,256]{2,1,0:T(8,128)(2,1)}, u32[]{:S(2)}, u32[]{:S(2)}) collective-permute-start(bf16[16,512,256]{2,1,0:T(8,128)(2,1)} %get-tuple-element.36), channel_id=1, source_target_pairs={{0,2},{2,0},{4,6},{6,4},{8,10},{10,8},{12,14},{14,12},{16,18},{18,... | collective-permute-start | bytes 12582920 | tf_op jit(solution)/shard_map/ppermute | solution.py:179
  258.4 30.7 %all-to-all-start.3 = ((bf16[16,256,128]{2,1,0:T(8,128)(2,1)}), bf16[16,256,128]{2,1,0:T(8,128)(2,1)S(1)}, u32[]{:S(2)}, u32[]{:S(2)}) async-start(bf16[16,256,128]{2,1,0:T(8,128)(2,1)} %get-tuple-element.37), calls=%async_computation.4 | async-start | bytes 2097152 | tf_op jit(solution)/shard_map/all_to_all | solution.py:174
  289.1 1.0 copy-start.2
  290.0 110.0 %all-to-all-start.4 = ((bf16[16,512,256]{2,1,0:T(8,128)(2,1)}), bf16[16,512,256]{2,1,0:T(8,128)(2,1)}, u32[]{:S(2)}, u32[]{:S(2)}) async-start(bf16[16,512,256]{2,1,0:T(8,128)(2,1)} %add_convert_fusion), calls=%async_computation.5 | async-start | bytes 8388608 | tf_op jit(solution)/shard_map/all_to_all | solution.py:174
  295.0 84.9 %all-gather.3.cloned.1.call-start = ((), (), s32[]{:S(2)}) async-start(), calls=%async_computation.7 | async-start | bytes 2228224 | tf_op jit(solution)/shard_map/all_gather | solution.py:578
Sparse Core Ops, SparseCore 0:
  24.6 107.3 reduce-scatter.1
  298.8 81.0 all-gather.2

commit v4 on v1

--- a/solution.py
+++ b/solution.py
@@ -181,7 +181,7 @@
     )
 
 
-def body(
+def body_shared(
     queries,
     keys,
     values,
@@ -262,6 +262,458 @@
     return (grad_queries, grad_keys, grad_values, glob_grads[0], glob_grads[1])
 
 
+CHUNKS = ((0, 6), (6, 2))
+UNROLL = (1, 4)
+VMEM_LIMIT = 60 * 1024 * 1024
+
+
+def pad_of(some):
+    return (2 * some + 7) // 8 * 8
+
+
+def split_two(row):
+    high = row.astype(jnp.bfloat16).astype(jnp.float32)
+    return jnp.concatenate([high, row - high], axis=1)
+
+
+def pack_kernel(query_ref, grad_ref, saved_ref, norm_ref, out_ref):
+    rows = query_ref.shape[0]
+    for head in range(out_ref.shape[1]):
+        cols = slice(head * HD, (head + 1) * HD)
+        query = query_ref[:, cols]
+        grad = grad_ref[:, cols]
+        product = grad.astype(jnp.float32) * saved_ref[:, cols].astype(jnp.float32)
+        delta = jnp.sum(product.T, axis=0, keepdims=True)
+        norm = norm_ref[head : head + 1, :]
+        stats = []
+        for block in range(rows // BLK):
+            lanes = slice(block * BLK, (block + 1) * BLK)
+            stats += [split_two(norm[:, lanes]), split_two(delta[:, lanes])]
+        pad = out_ref.shape[2] - rows
+        if len(stats) < pad:
+            stats.append(jnp.zeros((pad - len(stats), 2 * HD), jnp.float32))
+        stats = jnp.concatenate(stats, axis=0).astype(jnp.bfloat16)
+        for half in range(2):
+            out_ref[half, head, :rows, :HD] = query
+            out_ref[half, head, :rows, HD:] = grad
+            out_ref[half, head, rows:, :] = stats
+
+
+def pack_queries(queries, grad_output, saved_output, log_norm, first, some):
+    tokens, features = queries.shape
+    heads = features // HD
+    rows = some * BLK
+    place = first // some
+    spec = pl.BlockSpec((rows, features), lambda i: (place, 0))
+    shape = (2, heads, rows + pad_of(some), 2 * HD)
+    out = pl.pallas_call(
+        pack_kernel,
+        grid=(1,),
+        in_specs=[spec] * 3 + [pl.BlockSpec((heads, rows), lambda i: (0, place))],
+        out_specs=pl.BlockSpec(shape, lambda i: (0, 0, 0, 0)),
+        out_shape=jax.ShapeDtypeStruct(shape, jnp.bfloat16),
+        compiler_params=pltpu.CompilerParams(vmem_limit_bytes=VMEM_LIMIT),
+        cost_estimate=pl.CostEstimate(
+            flops=0, bytes_accessed=rows * features * 14, transcendentals=0
+        ),
+    )(queries, grad_output, saved_output, log_norm)
+    return out.reshape(2 * heads, rows + pad_of(some), 2 * HD)
+
+
+def pack_keys_kernel(mine_ref, key_ref, value_ref, glob_key_ref, glob_value_ref, *out_refs):
+    tokens = key_ref.shape[0]
+    chips = len(out_refs)
+    chip, core = mine_ref[0] // 2, mine_ref[0] % 2
+    for step, out_ref in enumerate(out_refs):
+        there = lax.rem(chip + step, chips)
+        for side in range(2):
+            head = 2 * there + (core if side == 0 else 1 - core)
+            cols = pl.ds(pl.multiple_of(head * HD, HD), HD)
+            start = side * (tokens + G)
+            out_ref[start : start + tokens, :HD] = key_ref[:, cols]
+            out_ref[start : start + tokens, HD:] = value_ref[:, cols]
+            out_ref[start + tokens : start + tokens + G, :HD] = glob_key_ref[:, cols]
+            out_ref[start + tokens : start + tokens + G, HD:] = glob_value_ref[:, cols]
+
+
+def pack_keys(mine, keys, values, glob_keys, glob_values):
+    tokens, features = keys.shape
+    chips = features // HD // 2
+    vmem = pl.BlockSpec(memory_space=pltpu.VMEM)
+    return pl.pallas_call(
+        pack_keys_kernel,
+        in_specs=[pl.BlockSpec(memory_space=pltpu.SMEM)] + [vmem] * 4,
+        out_specs=[vmem] * chips,
+        out_shape=[jax.ShapeDtypeStruct((2 * (tokens + G), 2 * HD), jnp.bfloat16)] * chips,
+        compiler_params=pltpu.CompilerParams(vmem_limit_bytes=VMEM_LIMIT),
+        cost_estimate=pl.CostEstimate(
+            flops=0, bytes_accessed=(tokens + G) * features * 8, transcendentals=0
+        ),
+    )(mine, keys, values, glob_keys, glob_values)
+
+
+def pair_grads(pair, stats, rows, valid):
+    zero = jnp.zeros((BLK, HD), jnp.bfloat16)
+    mixed = jnp.concatenate(
+        [
+            jnp.concatenate([pair[:, :HD], zero], axis=1),
+            jnp.concatenate([zero, pair[:, HD:]], axis=1),
+        ],
+        axis=0,
+    )
+    norm = (stats[0:1, :HD] + stats[0:1, HD:]) * LOG2E
+    delta = stats[1:2, :HD] + stats[1:2, HD:]
+    rows = jnp.concatenate(rows, axis=0) if len(rows) > 1 else rows[0]
+    both = lax.dot_general(
+        rows, mixed, (((1,), (1,)), ((), ())), preferred_element_type=jnp.float32
+    )
+    attend = jnp.exp2(both[:, :HD] * (FACTOR * LOG2E) - norm)
+    parts = []
+    for kind, known in enumerate(valid):
+        part = attend[kind * BLK : (kind + 1) * BLK]
+        parts.append(part if known is None else jnp.where(known, part, 0.0))
+    attend = jnp.concatenate(parts, axis=0) if len(parts) > 1 else parts[0]
+    grad_scores = attend * (both[:, HD:] - delta)
+    scores_low = grad_scores.astype(jnp.bfloat16)
+    grad_kv = jnp.dot(
+        jnp.concatenate([scores_low, attend.astype(jnp.bfloat16)], axis=1),
+        mixed,
+        preferred_element_type=jnp.float32,
+    )
+    grad_q = lax.dot_general(
+        scores_low, rows[:, :HD], (((0,), (0,)), ((), ())), preferred_element_type=jnp.float32
+    )
+    return grad_kv, grad_q * FACTOR
+
+
+def chunk_kernel(chunk, heads, table_ref, glob_ref, pair_ref, *refs):
+    kv_refs, refs = refs[:heads], refs[heads:]
+    last = chunk == len(CHUNKS) - 1
+    some = CHUNKS[chunk][1]
+    if last:
+        before_ref, glob_before_ref, dq_ref = refs[:3]
+        out_refs, refs = refs[3 : 3 + heads // 2], refs[3 + heads // 2 :]
+        dglob_ref, kv, pairs, acc, sems, before, stage, out_sems = refs
+    else:
+        dq_ref, sum_ref, dglob_ref, kv, pairs, acc, sems = refs
+    sources = pairs.shape[0]
+    total = acc.shape[0]
+    blocks = total // heads
+    own_kinds = W + R
+    own_base = heads * some * own_kinds
+    rim_base = own_base + heads * some * R
+    half = table_ref[rim_base + 2]
+    copies = [
+        pltpu.make_async_copy(
+            kv_ref.at[pl.ds(step % 2 * (blocks * BLK + G), blocks * BLK), :],
+            kv.at[step],
+            sems.at[step],
+        )
+        for step, kv_ref in enumerate(kv_refs)
+    ]
+    copies.append(pltpu.make_async_copy(pair_ref, pairs, sems.at[heads]))
+    for copy in copies:
+        copy.start()
+    if last:
+        earlier = pltpu.make_async_copy(before_ref, before, sems.at[heads + 1])
+        earlier.start()
+        dglob_ref[...] = glob_before_ref[...]
+    else:
+        dglob_ref[...] = jnp.zeros_like(dglob_ref)
+
+    def clear(block, carry):
+        acc[block] = jnp.zeros((BLK, 2 * HD), jnp.float32)
+        return carry
+
+    lax.fori_loop(0, total, clear, 0)
+    for copy in copies:
+        copy.wait()
+
+    def meet(source, inner, wanted, with_glob):
+        lines = slice(inner * BLK, (inner + 1) * BLK)
+        stats = pairs[source, some * BLK :, :].astype(jnp.float32)
+        places = [jnp.maximum(place, 0) for place in wanted]
+        rows = [
+            kv[place // blocks, pl.ds(pl.multiple_of((place % blocks) * BLK, BLK), BLK), :]
+            for place in places
+        ]
+        valid = [place >= 0 for place in wanted]
+        if with_glob:
+            rows.append(glob_ref[...])
+            valid.append(None)
+        grad_kv, grad_q = pair_grads(
+            pairs[source, lines, :], stats[2 * inner : 2 * inner + 2], rows, valid
+        )
+        for kind, place in enumerate(places):
+            acc[place] += grad_kv[kind * BLK : (kind + 1) * BLK]
+        if with_glob:
+            dglob_ref[...] += grad_kv[len(places) * BLK :]
+        return lines, grad_q
+
+    def one_own(index, carry):
+        source = half * heads + index
+        for inner in range(some):
+            entry = (index * some + inner) * own_kinds
+            wanted = [table_ref[entry + kind] for kind in range(own_kinds)]
+            lines, grad_q = meet(source, inner, wanted, True)
+            dq_ref[source, lines, :] = grad_q.astype(jnp.bfloat16)
+        return carry
+
+    def one_other(index, carry):
+        source = (1 - half) * heads + index
+        for inner in range(some):
+            entry = own_base + (index * some + inner) * R
+            wanted = [table_ref[entry + kind] for kind in range(R)]
+            lines, grad_q = meet(source, inner, wanted, True)
+            dq_ref[source, lines, :] = grad_q.astype(jnp.bfloat16)
+        return carry
+
+    lax.fori_loop(0, heads, one_own, 0, unroll=UNROLL[chunk])
+    lax.fori_loop(0, heads, one_other, 0, unroll=UNROLL[chunk])
+    rims = []
+    if chunk == 0:
+        rims.append((0, 0, rim_base))
+    if last:
+        rims.append((heads - 1, some - 1, rim_base + 1))
+    for index, inner, entry in rims:
+        source = (1 - half) * heads + index
+        lines, grad_q = meet(source, inner, [table_ref[entry]], False)
+        dq_ref[source, lines, :] = (
+            dq_ref[source, lines, :].astype(jnp.float32) + grad_q
+        ).astype(jnp.bfloat16)
+    if not last:
+        leave = pltpu.make_async_copy(acc, sum_ref, sems.at[heads + 1])
+        leave.start()
+        leave.wait()
+        return
+    dglob_ref[:, :HD] = dglob_ref[:, :HD] * FACTOR
+    earlier.wait()
+
+    def copy_out(step):
+        slot = step % 2
+        out = out_refs[step // 2].at[pl.ds(step % 2 * (blocks * BLK), blocks * BLK), :]
+        return pltpu.make_async_copy(stage.at[slot], out, out_sems.at[slot])
+
+    for step in range(heads):
+        if step >= 2:
+            copy_out(step - 2).wait()
+        for inner in range(blocks):
+            value = acc[step * blocks + inner] + before[step * blocks + inner]
+            lines = slice(inner * BLK, (inner + 1) * BLK)
+            stage[step % 2, lines, :HD] = (value[:, :HD] * FACTOR).astype(jnp.bfloat16)
+            stage[step % 2, lines, HD:] = value[:, HD:].astype(jnp.bfloat16)
+        copy_out(step).start()
+    for step in range(max(0, heads - 2), heads):
+        copy_out(step).wait()
+
+
+def chunk_call(chunk, table, glob, pairs, kv, before=()):
+    sources = pairs.shape[0]
+    heads = len(kv)
+    rows = CHUNKS[chunk][1] * BLK
+    tokens = kv[0].shape[0] // 2 - G
+    total = heads * (tokens // BLK)
+    last = chunk == len(CHUNKS) - 1
+    vmem = pl.BlockSpec(memory_space=pltpu.VMEM)
+    smem = pl.BlockSpec(memory_space=pltpu.SMEM)
+    hbm = pl.BlockSpec(memory_space=pl.ANY)
+    sums = jax.ShapeDtypeStruct((total, BLK, 2 * HD), jnp.float32)
+    rounded = jax.ShapeDtypeStruct((2 * tokens, 2 * HD), jnp.bfloat16)
+    scratch = [
+        pltpu.VMEM((heads, tokens, 2 * HD), jnp.bfloat16),
+        pltpu.VMEM(pairs.shape, jnp.bfloat16),
+        pltpu.VMEM(sums.shape, jnp.float32),
+        pltpu.SemaphoreType.DMA((heads + 2,)),
+    ]
+    if last:
+        scratch += [
+            pltpu.VMEM(sums.shape, jnp.float32),
+            pltpu.VMEM((2, tokens, 2 * HD), jnp.bfloat16),
+            pltpu.SemaphoreType.DMA((2,)),
+        ]
+    units = heads * (rows // BLK) * (W + 2 * R + 2)
+    return pl.pallas_call(
+        functools.partial(chunk_kernel, chunk, heads),
+        in_specs=[smem, vmem, hbm] + [hbm] * heads + [hbm, vmem] * last,
+        out_specs=[vmem] + [hbm] * (heads // 2 if last else 1) + [vmem],
+        out_shape=[jax.ShapeDtypeStruct((sources, rows, HD), jnp.bfloat16)]
+        + ([rounded] * (heads // 2) if last else [sums])
+        + [jax.ShapeDtypeStruct((G, 2 * HD), jnp.float32)],
+        scratch_shapes=scratch,
+        compiler_params=pltpu.CompilerParams(vmem_limit_bytes=VMEM_LIMIT),
+        cost_estimate=pl.CostEstimate(
+            flops=units * 16 * BLK * BLK * HD,
+            bytes_accessed=total * BLK * HD * 16,
+            transcendentals=units * BLK * BLK,
+        ),
+    )(table, glob, pairs, *kv, *before)
+
+
+def unpack_queries_kernel(*refs):
+    *in_refs, out_ref = refs
+    heads = in_refs[0].shape[0] // 2
+    for (first, some), in_ref in zip(CHUNKS, in_refs):
+        for head in range(heads):
+            total = in_ref[head].astype(jnp.float32) + in_ref[heads + head].astype(jnp.float32)
+            out_ref[first * BLK : (first + some) * BLK, head * HD : (head + 1) * HD] = total.astype(
+                jnp.bfloat16
+            )
+
+
+def unpack_queries(arrays):
+    shape = (sum(array.shape[1] for array in arrays), arrays[0].shape[0] // 2 * HD)
+    vmem = pl.BlockSpec(memory_space=pltpu.VMEM)
+    return pl.pallas_call(
+        unpack_queries_kernel,
+        in_specs=[vmem] * len(arrays),
+        out_specs=vmem,
+        out_shape=jax.ShapeDtypeStruct(shape, jnp.bfloat16),
+        compiler_params=pltpu.CompilerParams(vmem_limit_bytes=VMEM_LIMIT),
+        cost_estimate=pl.CostEstimate(
+            flops=0, bytes_accessed=shape[0] * shape[1] * 6, transcendentals=0
+        ),
+    )(*arrays)
+
+
+def unpack_keys_kernel(mine_ref, *refs):
+    *in_refs, dk_ref, dv_ref = refs
+    chips = len(in_refs) // 2
+    chip, core = mine_ref[0] // 2, mine_ref[0] % 2
+    for step, in_ref in enumerate(in_refs):
+        there = lax.rem(chip + step // 2, chips)
+        head = 2 * there + (core if step % 2 == 0 else 1 - core)
+        cols = pl.ds(pl.multiple_of(head * HD, HD), HD)
+        dk_ref[:, cols] = in_ref[:, :HD]
+        dv_ref[:, cols] = in_ref[:, HD:]
+
+
+def unpack_keys(mine, arrays):
+    tokens = arrays[0].shape[0] // 2
+    heads = len(arrays)
+    rows = tokens // 2
+    shape = jax.ShapeDtypeStruct((tokens, heads * HD), jnp.bfloat16)
+    sides = [
+        pl.BlockSpec((rows, 2 * HD), lambda i: (i, 0)),
+        pl.BlockSpec((rows, 2 * HD), lambda i: (2 + i, 0)),
+    ]
+    return pl.pallas_call(
+        unpack_keys_kernel,
+        grid=(2,),
+        in_specs=[pl.BlockSpec(memory_space=pltpu.SMEM)] + sides * (heads // 2),
+        out_specs=[pl.BlockSpec((rows, heads * HD), lambda i: (i, 0))] * 2,
+        out_shape=[shape] * 2,
+        compiler_params=pltpu.CompilerParams(vmem_limit_bytes=VMEM_LIMIT),
+        cost_estimate=pl.CostEstimate(
+            flops=0, bytes_accessed=tokens * heads * HD * 8, transcendentals=0
+        ),
+    )(mine, *arrays)
+
+
+def body_halves(
+    queries,
+    keys,
+    values,
+    saved_output,
+    grad_output,
+    log_norm,
+    global_keys,
+    global_values,
+    flow_links,
+    glob_owner,
+):
+    size = lax.axis_size("seq")
+    my_index = lax.axis_index("seq")
+    tokens, features = queries.shape
+    heads = features // HD
+    blocks = tokens // BLK
+    count = heads * blocks
+    half = my_index // heads
+    mine = my_index % heads
+    mine_one = mine.astype(jnp.int32).reshape(1)
+
+    chips = heads // 2
+
+    def turn(array, step):
+        pairs = [
+            (i, i - i % heads + (i % heads // 2 + step) % chips * 2 + i % 2) for i in range(size)
+        ]
+        return lax.ppermute(array, "seq", pairs) if step % chips else array
+
+    def over(array):
+        return lax.ppermute(array, "seq", [(i, i ^ 1) for i in range(size)])
+
+    first = exchange(pack_queries(queries, grad_output, saved_output, log_norm, *CHUNKS[0]))
+    owned = (glob_owner == my_index)[:, None]
+    slabs = pack_keys(
+        mine_one,
+        keys,
+        values,
+        jnp.where(owned, global_keys[0], jnp.bfloat16(0)),
+        jnp.where(owned, global_values[0], jnp.bfloat16(0)),
+    )
+    near_kv = [turn(slab, step) for step, slab in enumerate(slabs)]
+    kv = [piece for slab in near_kv for piece in (slab, over(slab))]
+    packed = pack_queries(queries, grad_output, saved_output, log_norm, *CHUNKS[1])
+    packed, first, *kv = lax.optimization_barrier((packed, first, *kv))
+    second = exchange(packed)
+    glob_now = functools.reduce(
+        jnp.add,
+        [
+            piece[tokens + step % 2 * (tokens + G) :][:G].astype(jnp.float32)
+            for step, piece in enumerate(kv)
+        ],
+    ).astype(jnp.bfloat16)
+
+    def places(wanted):
+        here = wanted - half * count
+        owner = here // blocks
+        step = (mine // 2 - owner // 2 + chips) % chips * 2 + (mine + owner) % 2
+        return jnp.where((here >= 0) & (here < count), step * blocks + here % blocks, -1)
+
+    links = flow_links.reshape(2, count, R)
+    my_links = lax.dynamic_index_in_dim(links, half, axis=0, keepdims=False)
+    other_links = lax.dynamic_index_in_dim(links, 1 - half, axis=0, keepdims=False)
+    order = half * count + jnp.arange(count, dtype=jnp.int32)
+    near = (order[:, None] + jnp.arange(-1, 2, dtype=jnp.int32) + 2 * count) % (2 * count)
+    own = places(jnp.concatenate([near, my_links], axis=1)).reshape(heads, blocks, -1)
+    other = places(other_links).reshape(heads, blocks, -1)
+    ends = places(jnp.stack([half * count + count - 1, half * count]))
+    tail = jnp.concatenate([ends, half.reshape(1)])
+    tables = [
+        jnp.concatenate(
+            [part[:, first : first + some].reshape(-1) for part in (own, other)] + [tail]
+        ).astype(jnp.int32)
+        for first, some in CHUNKS
+    ]
+
+    dq_first, sums, dglob = chunk_call(0, tables[0], glob_now, first, kv)
+    back_first = exchange(dq_first)
+    dq_second, *slabs, dglob = chunk_call(1, tables[1], glob_now, second, kv, (sums, dglob))
+    dq_second, back_first, dglob = lax.optimization_barrier((dq_second, back_first, dglob))
+    slabs = [turn(slab, chips - step) for step, slab in enumerate(slabs)]
+    dq_second, slabs[2] = lax.optimization_barrier((dq_second, slabs[2]))
+    back_second = exchange(dq_second)
+    grad_keys, grad_values = unpack_keys(
+        mine_one, [piece for slab in slabs for piece in (slab, over(slab))]
+    )
+    grad_queries = unpack_queries((back_first, back_second))
+    held = (glob_owner // heads == half)[:, None]
+    glob_parts = lax.all_gather(
+        jnp.where(held, dglob, 0.0).astype(jnp.bfloat16), "seq", axis=0, tiled=False
+    ).astype(jnp.float32)
+    glob_sum = (glob_parts[:heads] + glob_parts[heads:]).reshape(heads, G, 2, HD)
+    glob_grads = jnp.transpose(glob_sum, (2, 1, 0, 3)).reshape(2, G, features).astype(jnp.bfloat16)
+    return (grad_queries, grad_keys, grad_values, glob_grads[0], glob_grads[1])
+
+
+def body(queries, *rest):
+    tokens, features = queries.shape
+    blocks = sum(some for _, some in CHUNKS)
+    if lax.axis_size("seq") == 2 * (features // HD) and tokens == blocks * BLK:
+        return body_halves(queries, *rest)
+    return body_shared(queries, *rest)
+
+
 def solution(mesh):
     return jax.shard_map(
         body,

time: 499 us -> 394 us (0.79); the launches traced: 498 us -> 388 us
  waiting for transfers between devices: 326 us -> 229 us
  Pallas kernels: 78.8 us -> 97 us
  other arithmetic: 25.2 us -> 7.66 us
  local copies, waits for them, and re-layouts: 19.7 us -> 4.65 us
    all_to_all x6 -> x4, waiting for transfers between devices: 236 us -> 44.8 us  [exchange(): return lax.all_to_all(array, 'seq', split_axis=0, concat_axis=0, tiled=True)]
    ppermute x2 -> x14, waiting for transfers between devices: 6.16 us -> 184 us  [the longest x6 179 us: turn(): return lax.ppermute(array, 'seq', pairs) if step % chips else array]
    all_gather x1, waiting for transfers between devices: 84.2 us -> 0.05 us  [body_halves(): lax.all_gather(jnp.where(held, dglob, 0.0).astype(jnp.bfloat16), 'seq', a...]
    pallas_call x5 -> x7, Pallas kernels: 78.8 us -> 97 us  [the longest x2 73.5 us: chunk_call(): pl.pallas_call(functools.partial(chunk_kernel, chunk, heads), in_specs=[s...]
    ppermute x2 -> x14, starting transfers between devices: 0.58 us -> 11.6 us  [the longest x8 7.13 us: over(): return lax.ppermute(array, 'seq', [(i, i ^ 1) for i in range(size)])]
    all_to_all x6 -> x4, starting transfers between devices: 32.6 us -> 23.2 us  [exchange(): return lax.all_to_all(array, 'seq', split_axis=0, concat_axis=0, tiled=True)]
    concatenate x3 -> x2, other arithmetic: 8.17 us -> 1.31 us  [body_halves(): jnp.concatenate([part[:, first:first + some].reshape(-1) for part in (own...]
    reduce_sum x3 -> x0, other arithmetic: 6.41 us -> none  [the longest x1 3.42 us: body(): delta = jnp.sum(product.reshape(tokens, heads, HD), axis=2).T]
  transfers between devices with their start and end apart: 9 -> 19, of which waited for: 9 -> 10; matrix products, arithmetic and copies ran while one was open for 5% -> 3% of each run, Pallas kernels for 3% -> 22%
where the time goes in v4:
time: 394 us; the launch traced here: 388 us
  waiting for transfers between devices  229 us (58%)
  Pallas kernels  97 us (25%)
  starting transfers between devices  35 us (9%)
  between operations  14.2 us (4%)
  other arithmetic  7.66 us (2%)
  local copies, waits for them, and re-layouts  4.65 us (1%)
    ppermute x6, waiting for transfers between devices, turn(): return lax.ppermute(array, 'seq', pairs) if step % chips else array  179 us
    pallas_call x2, Pallas kernels, chunk_call(): pl.pallas_call(functools.partial(chunk_kernel, chunk, heads), in_specs=[s...  73.5 us
    all_to_all x4, waiting for transfers between devices, exchange(): return lax.all_to_all(array, 'seq', split_axis=0, concat_axis=0, tiled=True)  44.8 us
    all_to_all x4, starting transfers between devices, exchange(): return lax.all_to_all(array, 'seq', split_axis=0, concat_axis=0, tiled=True)  23.2 us
    pallas_call x2, Pallas kernels, pack_queries(): pl.pallas_call(pack_kernel, grid=(1,), in_specs=[spec] * 3 + [pl.BlockSpe...  9.47 us
  transfers between devices with their start and end apart: 19, of which 10 were waited for; matrix products, arithmetic and copies ran while one was open for 3% of the time, Pallas kernels for 22%

profile of v4, /device:TPU:15, one launch (start us, length us, event | category | flops | bytes accessed | tf_op | source)
XLA Modules:
  0.0 387.6 jit_solution(4969483970228267760)
XLA Ops:
  7.2 6.3 %shard_map.138 = bf16[2,8,784,256]{3,2,1,0:T(8,128)(2,1)} custom-call(bf16[1024,1024]{1,0:T(8,128)(2,1)} %query_ref.3, bf16[1024,1024]{1,0:T(8,128)(2,1)} %grad_ref.3, bf16[1024,1024]{1,0:T(8,128)(2,1)} %saved_ref.3, f32[8,1024]{1,0:T(8,128)} %norm_ref.3), custom_call_target="tpu_custom_call" | custom-call | bytes 11010048 | tf_op jit(solution)/shard_map/pallas_call | solution.py:309
  13.5 6.7 %all-to-all-start = ((bf16[16,784,256]{2,1,0:T(8,128)(2,1)}), bf16[16,784,256]{2,1,0:T(8,128)(2,1)}, u32[]{:S(2)}, u32[]{:S(2)}) async-start(bf16[16,784,256]{2,1,0:T(8,128)(2,1)} %bitcast.50), calls=%async_computation | async-start | bytes 12845056 | tf_op jit(solution)/shard_map/all_to_all | solution.py:174
  20.2 0.9 bitcast_select_fusion
  21.1 5.7 %shard_map.139 = (bf16[2304,256]{1,0:T(8,128)(2,1)}, bf16[2304,256]{1,0:T(8,128)(2,1)}, bf16[2304,256]{1,0:T(8,128)(2,1)}, bf16[2304,256]{1,0:T(8,128)(2,1)}) custom-call(s32[1]{0:T(128)} %bitcast.7.mine_ref, bf16[1024,1024]{1,0:T(8,128)(2,1)} %key_ref.1, bf16[1024,1024]{1,0:T(8,128)(2,1)} %value_ref.1, bf16[128,1024]{1,0:T(8,128)(2,1)} %get-tuple-element.72.glob_key_ref, ...), custom_call_target="tpu_custom_call" | custom-call | bytes 9437184 | tf_op jit(solution)/shard_map/pallas_call | solution.py:343
  26.9 1.4 collective-permute-start.3
  28.6 1.2 collective-permute-start
  29.8 119.5 %collective-permute-done.1.refs_2_ = bf16[2304,256]{1,0:T(8,128)(2,1)S(1)} collective-permute-done((bf16[2304,256]{1,0:T(8,128)(2,1)}, bf16[2304,256]{1,0:T(8,128)(2,1)S(1)}, u32[]{:S(2)}, u32[]{:S(2)}) %collective-permute-start.1) | collective-permute-done | bytes 1179680 | tf_op jit(solution)/shard_map/ppermute | solution.py:640
  149.3 1.3 collective-permute-start.2
  150.6 32.8 %collective-permute-done.3.refs_4_ = bf16[2304,256]{1,0:T(8,128)(2,1)S(1)} collective-permute-done((bf16[2304,256]{1,0:T(8,128)(2,1)}, bf16[2304,256]{1,0:T(8,128)(2,1)S(1)}, u32[]{:S(2)}, u32[]{:S(2)}) %collective-permute-start.3) | collective-permute-done | bytes 1179680 | tf_op jit(solution)/shard_map/ppermute | solution.py:640
  183.5 0.9 collective-permute-start.4
  184.8 3.1 shard_map.137
  188.6 4.4 %all-to-all-start.1 = ((bf16[16,264,256]{2,1,0:T(8,128)(2,1)}), bf16[16,264,256]{2,1,0:T(8,128)(2,1)S(1)}, u32[]{:S(2)}, u32[]{:S(2)}) async-start(bf16[16,264,256]{2,1,0:T(8,128)(2,1)} %bitcast.51), calls=%async_computation.1 | async-start | bytes 4325376 | tf_op jit(solution)/shard_map/all_to_all | solution.py:174
  194.7 1.8 add_convert_fusion.glob_ref
  196.4 50.9 %shard_map.140 = (bf16[16,768,128]{2,1,0:T(8,128)(2,1)}, f32[64,128,256]{2,1,0:T(8,128)}, f32[128,256]{1,0:T(8,128)}) custom-call(s32[435]{0:T(512)} %pad_add_fusion.table_ref, bf16[128,256]{1,0:T(8,128)(2,1)} %add_convert_fusion.glob_ref, bf16[16,784,256]{2,1,0:T(8,128)(2,1)} %all-to-all-done.pair_ref, bf16[2304,256]{1,0:T(8,128)(2,1)} %get-tuple-element.39.refs_0_, ...), custom_call_target="tpu_custom_call" | custom-call | flops 17716740096 | bytes 16777216 | tf_op jit(solution)/shard_map/pallas_call | solution.py:535
  247.3 1.3 copy-done.1
  248.7 6.0 %all-to-all-start.2 = ((bf16[16,768,128]{2,1,0:T(8,128)(2,1)}), bf16[16,768,128]{2,1,0:T(8,128)(2,1)S(1)}, u32[]{:S(2)}, u32[]{:S(2)}) async-start(bf16[16,768,128]{2,1,0:T(8,128)(2,1)} %get-tuple-element.52), calls=%async_computation.2 | async-start | bytes 6291456 | tf_op jit(solution)/shard_map/all_to_all | solution.py:174
  255.8 22.6 %shard_map.141 = (bf16[16,256,128]{2,1,0:T(8,128)(2,1)}, bf16[2048,256]{1,0:T(8,128)(2,1)}, bf16[2048,256]{1,0:T(8,128)(2,1)}, bf16[2048,256]{1,0:T(8,128)(2,1)}...) custom-call(s32[147]{0:T(256)} %pad_add_fusion.1.table_ref, bf16[128,256]{1,0:T(8,128)(2,1)} %add_convert_fusion.glob_ref, ...), custom_call_target="tpu_custom_call" | custom-call | flops 5905580032 | bytes 16777216 | tf_op jit(solution)/shard_map/pallas_call | solution.py:535
  278.9 2.3 collective-permute-start.12
  281.2 44.0 %all-to-all-done.2.refs_0_ = bf16[16,768,128]{2,1,0:T(8,128)(2,1)S(1)} async-done(((bf16[16,768,128]{2,1,0:T(8,128)(2,1)}), bf16[16,768,128]{2,1,0:T(8,128)(2,1)S(1)}, u32[]{:S(2)}, u32[]{:S(2)}) %all-to-all-start.2) | async-done | bytes 3145760 | tf_op jit(solution)/shard_map/all_to_all | solution.py:174
  325.2 1.7 select_convert_fusion
  326.9 3.4 collective-permute-done.7.refs_4_
  330.4 6.2 %all-to-all-start.3 = ((bf16[16,256,128]{2,1,0:T(8,128)(2,1)}), bf16[16,256,128]{2,1,0:T(8,128)(2,1)}, u32[]{:S(2)}, u32[]{:S(2)}) async-start(bf16[16,256,128]{2,1,0:T(8,128)(2,1)} %get-tuple-element.57), calls=%async_computation.3 | async-start | bytes 2097152 | tf_op jit(solution)/shard_map/all_to_all | solution.py:174
  336.9 19.2 %collective-permute-done.9.refs_2_ = bf16[2048,256]{1,0:T(8,128)(2,1)} collective-permute-done((bf16[2048,256]{1,0:T(8,128)(2,1)}, bf16[2048,256]{1,0:T(8,128)(2,1)}, u32[]{:S(2)}, u32[]{:S(2)}) %collective-permute-start.9) | collective-permute-done | bytes 1048608 | tf_op jit(solution)/shard_map/ppermute | solution.py:640
  356.8 4.4 %collective-permute-done.12.refs_6_ = bf16[2048,256]{1,0:T(8,128)(2,1)} collective-permute-done((bf16[2048,256]{1,0:T(8,128)(2,1)}, bf16[2048,256]{1,0:T(8,128)(2,1)}, u32[]{:S(2)}, u32[]{:S(2)}) %collective-permute-start.12) | collective-permute-done | bytes 1048608 | tf_op jit(solution)/shard_map/ppermute | solution.py:640
  361.2 2.1 collective-permute-start.13
  363.3 2.6 collective-permute-done.13.refs_7_
  365.9 1.5 collective-permute-done.11.refs_5_
  367.5 4.2 %shard_map.143 = (bf16[1024,1024]{1,0:T(8,128)(2,1)}, bf16[1024,1024]{1,0:T(8,128)(2,1)}) custom-call(s32[1]{0:T(128)} %bitcast.7.mine_ref, bf16[2048,256]{1,0:T(8,128)(2,1)} %get-tuple-element.58.refs_0_, bf16[2048,256]{1,0:T(8,128)(2,1)} %collective-permute-done.8.refs_1_, bf16[2048,256]{1,0:T(8,128)(2,1)} %collective-permute-done.9.refs_2_, ...), custom_call_target="tpu_custom_call" | custom-call | bytes 8388608 | tf_op jit(solution)/shard_map/pallas_call | solution.py:599
  371.7 1.4 convert_element_type.57
  373.3 0.9 fusion.34
  374.9 0.9 copy_bitcast_fusion
  376.6 4.1 %shard_map.142 = bf16[1024,1024]{1,0:T(8,128)(2,1)} custom-call(bf16[16,768,128]{2,1,0:T(8,128)(2,1)} %copy-done, bf16[16,256,128]{2,1,0:T(8,128)(2,1)} %all-to-all-done.3.refs_1_), custom_call_target="tpu_custom_call" | custom-call | bytes 6291456 | tf_op jit(solution)/shard_map/pallas_call | solution.py:566
  (61 shorter events, 7.6 us)
Async XLA Ops:
  13.5 6.7 %copy-start.8 = (s32[128]{0:T(128)S(1)}, s32[128]{0:T(128)}, u32[]{:S(2)}) copy-start(s32[128]{0:T(128)} %param.19) | copy-start | bytes 1540
  13.5 6.7 %copy-start.2 = (bf16[1,128,1024]{2,1,0:T(8,128)(2,1)S(1)}, bf16[1,128,1024]{2,1,0:T(8,128)(2,1)}, u32[]{:S(2)}) copy-start(bf16[1,128,1024]{2,1,0:T(8,128)(2,1)} %param.17) | copy-start | bytes 786436
  13.5 6.7 %copy-start.3 = (bf16[1,128,1024]{2,1,0:T(8,128)(2,1)S(1)}, bf16[1,128,1024]{2,1,0:T(8,128)(2,1)}, u32[]{:S(2)}) copy-start(bf16[1,128,1024]{2,1,0:T(8,128)(2,1)} %param.16) | copy-start | bytes 786436
  13.5 175.1 %all-to-all-start = ((bf16[16,784,256]{2,1,0:T(8,128)(2,1)}), bf16[16,784,256]{2,1,0:T(8,128)(2,1)}, u32[]{:S(2)}, u32[]{:S(2)}) async-start(bf16[16,784,256]{2,1,0:T(8,128)(2,1)} %bitcast.50), calls=%async_computation | async-start | bytes 12845056 | tf_op jit(solution)/shard_map/all_to_all | solution.py:174
  26.9 122.4 %collective-permute-start.1 = (bf16[2304,256]{1,0:T(8,128)(2,1)}, bf16[2304,256]{1,0:T(8,128)(2,1)S(1)}, u32[]{:S(2)}, u32[]{:S(2)}) collective-permute-start(bf16[2304,256]{1,0:T(8,128)(2,1)} %get-tuple-element.36), channel_id=1, source_target_pairs={{0,4},{2,6},{4,8},{6,10},{8,12},{10,14},{12,0},{14,2},{16,20},{18,... | collective-permute-start | bytes 3538952 | tf_op jit(solution)/shard_map/ppermute | solution.py:640
  26.9 156.5 %collective-permute-start.3 = (bf16[2304,256]{1,0:T(8,128)(2,1)}, bf16[2304,256]{1,0:T(8,128)(2,1)S(1)}, u32[]{:S(2)}, u32[]{:S(2)}) collective-permute-start(bf16[2304,256]{1,0:T(8,128)(2,1)} %get-tuple-element.37), channel_id=1, source_target_pairs={{0,8},{2,10},{4,12},{6,14},{8,0},{10,2},{12,4},{14,6},{16,24},{18,... | collective-permute-start | bytes 3538952 | tf_op jit(solution)/shard_map/ppermute | solution.py:640
  28.3 156.0 %collective-permute-start.5 = (bf16[2304,256]{1,0:T(8,128)(2,1)}, bf16[2304,256]{1,0:T(8,128)(2,1)S(1)}, u32[]{:S(2)}, u32[]{:S(2)}) collective-permute-start(bf16[2304,256]{1,0:T(8,128)(2,1)} %get-tuple-element.38), channel_id=1, source_target_pairs={{0,12},{2,14},{4,0},{6,2},{8,4},{10,6},{12,8},{14,10},{16,28},{18,... | collective-permute-start | bytes 3538952 | tf_op jit(solution)/shard_map/ppermute | solution.py:640
  28.6 159.4 %collective-permute-start = (bf16[2304,256]{1,0:T(8,128)(2,1)}, bf16[2304,256]{1,0:T(8,128)(2,1)}, u32[]{:S(2)}, u32[]{:S(2)}) collective-permute-start(bf16[2304,256]{1,0:T(8,128)(2,1)} %get-tuple-element.39.refs_0_), channel_id=1, source_target_pairs={{0,2},{2,0},{4,6},{6,4},{8,10},{10,8},{12,14},{14,12},{16,18},{18,... | collective-permute-start | bytes 3538952 | tf_op jit(solution)/shard_map/ppermute | solution.py:643
  149.3 38.7 %copy-start.4 = (bf16[2304,256]{1,0:T(8,128)(2,1)}, bf16[2304,256]{1,0:T(8,128)(2,1)S(1)}, u32[]{:S(2)}) copy-start(bf16[2304,256]{1,0:T(8,128)(2,1)S(1)} %collective-permute-done.1.refs_2_) | copy-start | bytes 3538948
  149.3 38.7 %collective-permute-start.2 = (bf16[2304,256]{1,0:T(8,128)(2,1)S(1)}, bf16[2304,256]{1,0:T(8,128)(2,1)}, u32[]{:S(2)}, u32[]{:S(2)}) collective-permute-start(bf16[2304,256]{1,0:T(8,128)(2,1)S(1)} %collective-permute-done.1.refs_2_), channel_id=1, source_target_pairs={{0,2},{2,0},{4,6},{6,4},{8,10},{10,8},{12,14},{14,12},{16,18},{18,... | collective-permute-start | bytes 3538952 | tf_op jit(solution)/shard_map/ppermute | solution.py:643
  183.4 4.5 %copy-start.5 = (bf16[2304,256]{1,0:T(8,128)(2,1)}, bf16[2304,256]{1,0:T(8,128)(2,1)S(1)}, u32[]{:S(2)}) copy-start(bf16[2304,256]{1,0:T(8,128)(2,1)S(1)} %collective-permute-done.3.refs_4_) | copy-start | bytes 3538948
  183.5 4.5 %collective-permute-start.4 = (bf16[2304,256]{1,0:T(8,128)(2,1)S(1)}, bf16[2304,256]{1,0:T(8,128)(2,1)}, u32[]{:S(2)}, u32[]{:S(2)}) collective-permute-start(bf16[2304,256]{1,0:T(8,128)(2,1)S(1)} %collective-permute-done.3.refs_4_), channel_id=1, source_target_pairs={{0,2},{2,0},{4,6},{6,4},{8,10},{10,8},{12,14},{14,12},{16,18},{18,... | collective-permute-start | bytes 3538952 | tf_op jit(solution)/shard_map/ppermute | solution.py:643
  184.3 3.6 copy-start.6
  184.3 4.3 %collective-permute-start.6 = (bf16[2304,256]{1,0:T(8,128)(2,1)S(1)}, bf16[2304,256]{1,0:T(8,128)(2,1)}, u32[]{:S(2)}, u32[]{:S(2)}) collective-permute-start(bf16[2304,256]{1,0:T(8,128)(2,1)S(1)} %collective-permute-done.5.refs_6_), channel_id=1, source_target_pairs={{0,2},{2,0},{4,6},{6,4},{8,10},{10,8},{12,14},{14,12},{16,18},{18,... | collective-permute-start | bytes 3538952 | tf_op jit(solution)/shard_map/ppermute | solution.py:643
  188.6 4.4 %copy-start.7 = (s32[128,3]{0,1:T(4,128)S(1)}, s32[128,3]{0,1:T(4,128)}, u32[]{:S(2)}) copy-start(s32[128,3]{0,1:T(4,128)} %param.18) | copy-start | bytes 4612
  188.6 58.7 %all-to-all-start.1 = ((bf16[16,264,256]{2,1,0:T(8,128)(2,1)}), bf16[16,264,256]{2,1,0:T(8,128)(2,1)S(1)}, u32[]{:S(2)}, u32[]{:S(2)}) async-start(bf16[16,264,256]{2,1,0:T(8,128)(2,1)} %bitcast.51), calls=%async_computation.1 | async-start | bytes 4325376 | tf_op jit(solution)/shard_map/all_to_all | solution.py:174
  247.3 1.4 copy-start.1
  248.7 76.5 %all-to-all-start.2 = ((bf16[16,768,128]{2,1,0:T(8,128)(2,1)}), bf16[16,768,128]{2,1,0:T(8,128)(2,1)S(1)}, u32[]{:S(2)}, u32[]{:S(2)}) async-start(bf16[16,768,128]{2,1,0:T(8,128)(2,1)} %get-tuple-element.52), calls=%async_computation.2 | async-start | bytes 6291456 | tf_op jit(solution)/shard_map/all_to_all | solution.py:174
  254.7 117.0 %all-gather.3.cloned.1.call-start = ((), (), s32[]{:S(2)}) async-start(), calls=%async_computation.4 | async-start | bytes 1114112 | tf_op jit(solution)/shard_map/all_gather | solution.py:701
  278.4 51.9 %collective-permute-start.7 = (bf16[2048,256]{1,0:T(8,128)(2,1)}, bf16[2048,256]{1,0:T(8,128)(2,1)}, u32[]{:S(2)}, u32[]{:S(2)}) collective-permute-start(bf16[2048,256]{1,0:T(8,128)(2,1)} %get-tuple-element.56), channel_id=1, source_target_pairs={{0,8},{2,10},{4,12},{6,14},{8,0},{10,2},{12,4},{14,6},{16,24},{18,... | collective-permute-start | bytes 3145736 | tf_op jit(solution)/shard_map/ppermute | solution.py:640
  278.8 77.3 %collective-permute-start.9 = (bf16[2048,256]{1,0:T(8,128)(2,1)}, bf16[2048,256]{1,0:T(8,128)(2,1)}, u32[]{:S(2)}, u32[]{:S(2)}) collective-permute-start(bf16[2048,256]{1,0:T(8,128)(2,1)} %get-tuple-element.59), channel_id=1, source_target_pairs={{0,12},{2,14},{4,0},{6,2},{8,4},{10,6},{12,8},{14,10},{16,28},{18,... | collective-permute-start | bytes 3145736 | tf_op jit(solution)/shard_map/ppermute | solution.py:640
  278.9 82.3 %collective-permute-start.12 = (bf16[2048,256]{1,0:T(8,128)(2,1)}, bf16[2048,256]{1,0:T(8,128)(2,1)}, u32[]{:S(2)}, u32[]{:S(2)}) collective-permute-start(bf16[2048,256]{1,0:T(8,128)(2,1)} %get-tuple-element.61), channel_id=1, source_target_pairs={{0,4},{2,6},{4,8},{6,10},{8,12},{10,14},{12,0},{14,2},{16,20},{18,... | collective-permute-start | bytes 3145736 | tf_op jit(solution)/shard_map/ppermute | solution.py:640
  325.2 46.5 %copy-start = (bf16[16,768,128]{2,1,0:T(8,128)(2,1)}, bf16[16,768,128]{2,1,0:T(8,128)(2,1)S(1)}, u32[]{:S(2)}) copy-start(bf16[16,768,128]{2,1,0:T(8,128)(2,1)S(1)} %all-to-all-done.2.refs_0_) | copy-start | bytes 9437188
  330.4 46.2 %all-to-all-start.3 = ((bf16[16,256,128]{2,1,0:T(8,128)(2,1)}), bf16[16,256,128]{2,1,0:T(8,128)(2,1)}, u32[]{:S(2)}, u32[]{:S(2)}) async-start(bf16[16,256,128]{2,1,0:T(8,128)(2,1)} %get-tuple-element.57), calls=%async_computation.3 | async-start | bytes 2097152 | tf_op jit(solution)/shard_map/all_to_all | solution.py:174
  336.5 26.8 %collective-permute-start.8 = (bf16[2048,256]{1,0:T(8,128)(2,1)}, bf16[2048,256]{1,0:T(8,128)(2,1)}, u32[]{:S(2)}, u32[]{:S(2)}) collective-permute-start(bf16[2048,256]{1,0:T(8,128)(2,1)} %get-tuple-element.58.refs_0_), channel_id=1, source_target_pairs={{0,2},{2,0},{4,6},{6,4},{8,10},{10,8},{12,14},{14,12},{16,18},{18,... | collective-permute-start | bytes 3145736 | tf_op jit(solution)/shard_map/ppermute | solution.py:643
  356.0 7.3 %collective-permute-start.10 = (bf16[2048,256]{1,0:T(8,128)(2,1)}, bf16[2048,256]{1,0:T(8,128)(2,1)}, u32[]{:S(2)}, u32[]{:S(2)}) collective-permute-start(bf16[2048,256]{1,0:T(8,128)(2,1)} %collective-permute-done.9.refs_2_), channel_id=1, source_target_pairs={{0,2},{2,0},{4,6},{6,4},{8,10},{10,8},{12,14},{14,12},{16,18},{18,... | collective-permute-start | bytes 3145736 | tf_op jit(solution)/shard_map/ppermute | solution.py:643
  361.2 4.7 %collective-permute-start.13 = (bf16[2048,256]{1,0:T(8,128)(2,1)}, bf16[2048,256]{1,0:T(8,128)(2,1)}, u32[]{:S(2)}, u32[]{:S(2)}) collective-permute-start(bf16[2048,256]{1,0:T(8,128)(2,1)} %collective-permute-done.12.refs_6_), channel_id=1, source_target_pairs={{0,2},{2,0},{4,6},{6,4},{8,10},{10,8},{12,14},{14,12},{16,18},{18,... | collective-permute-start | bytes 3145736 | tf_op jit(solution)/shard_map/ppermute | solution.py:643
  363.3 4.2 %collective-permute-start.11 = (bf16[2048,256]{1,0:T(8,128)(2,1)}, bf16[2048,256]{1,0:T(8,128)(2,1)}, u32[]{:S(2)}, u32[]{:S(2)}) collective-permute-start(bf16[2048,256]{1,0:T(8,128)(2,1)} %collective-permute-done.7.refs_4_), channel_id=1, source_target_pairs={{0,2},{2,0},{4,6},{6,4},{8,10},{10,8},{12,14},{14,12},{16,18},{18,... | collective-permute-start | bytes 3145736 | tf_op jit(solution)/shard_map/ppermute | solution.py:643
Sparse Core Ops, SparseCore 0:
  327.1 44.5 all-gather.2

commit v5 on v4

--- a/solution.py
+++ b/solution.py
@@ -263,7 +263,7 @@
 
 
 CHUNKS = ((0, 6), (6, 2))
-UNROLL = (1, 4)
+UNROLL = (2, 4)
 VMEM_LIMIT = 60 * 1024 * 1024
 
 
@@ -644,17 +644,18 @@
 
     first = exchange(pack_queries(queries, grad_output, saved_output, log_norm, *CHUNKS[0]))
     owned = (glob_owner == my_index)[:, None]
-    slabs = pack_keys(
+    (*slabs,) = pack_keys(
         mine_one,
         keys,
         values,
         jnp.where(owned, global_keys[0], jnp.bfloat16(0)),
         jnp.where(owned, global_values[0], jnp.bfloat16(0)),
     )
+    packed = pack_queries(queries, grad_output, saved_output, log_norm, *CHUNKS[1])
+    slabs[3], packed = lax.optimization_barrier((slabs[3], packed))
     near_kv = [turn(slab, step) for step, slab in enumerate(slabs)]
     kv = [piece for slab in near_kv for piece in (slab, over(slab))]
-    packed = pack_queries(queries, grad_output, saved_output, log_norm, *CHUNKS[1])
-    packed, first, *kv = lax.optimization_barrier((packed, first, *kv))
+    packed, first, kv[4] = lax.optimization_barrier((packed, first, kv[4]))
     second = exchange(packed)
     glob_now = functools.reduce(
         jnp.add,
@@ -689,7 +690,7 @@
     dq_first, sums, dglob = chunk_call(0, tables[0], glob_now, first, kv)
     back_first = exchange(dq_first)
     dq_second, *slabs, dglob = chunk_call(1, tables[1], glob_now, second, kv, (sums, dglob))
-    dq_second, back_first, dglob = lax.optimization_barrier((dq_second, back_first, dglob))
+    dq_second, back_first = lax.optimization_barrier((dq_second, back_first))
     slabs = [turn(slab, chips - step) for step, slab in enumerate(slabs)]
     dq_second, slabs[2] = lax.optimization_barrier((dq_second, slabs[2]))
     back_second = exchange(dq_second)

time: 394 us -> 392 us (level)
    ppermute x6, waiting for transfers between devices: 179 us -> 157 us  [turn(): return lax.ppermute(array, 'seq', pairs) if step % chips else array]
    all_to_all x4, waiting for transfers between devices: 44.8 us -> 65.2 us  [exchange(): return lax.all_to_all(array, 'seq', split_axis=0, concat_axis=0, tiled=True)]
  transfers between devices with their start and end apart: 19 -> 19, of which waited for: 10 -> 11; matrix products, arithmetic and copies ran while one was open for 3% -> 3% of each run, Pallas kernels for 22% -> 22%
where the time goes in v5:
time: 392 us; the launch traced here: 385 us
  waiting for transfers between devices  226 us (58%)
  Pallas kernels  96 us (24%)
  starting transfers between devices  34.8 us (9%)
  between operations  14.2 us (4%)
  other arithmetic  8.31 us (2%)
  local copies, waits for them, and re-layouts  5.71 us (1%)
    ppermute x6, waiting for transfers between devices, turn(): return lax.ppermute(array, 'seq', pairs) if step % chips else array  157 us
    pallas_call x2, Pallas kernels, chunk_call(): pl.pallas_call(functools.partial(chunk_kernel, chunk, heads), in_specs=[s...  72.6 us
    all_to_all x4, waiting for transfers between devices, exchange(): return lax.all_to_all(array, 'seq', split_axis=0, concat_axis=0, tiled=True)  65.2 us
    all_to_all x4, starting transfers between devices, exchange(): return lax.all_to_all(array, 'seq', split_axis=0, concat_axis=0, tiled=True)  23.8 us
    pallas_call x2, Pallas kernels, pack_queries(): pl.pallas_call(pack_kernel, grid=(1,), in_specs=[spec] * 3 + [pl.BlockSpe...  9.46 us
  transfers between devices with their start and end apart: 19, of which 11 were waited for; matrix products, arithmetic and copies ran while one was open for 3% of the time, Pallas kernels for 22%

profile of v5, /device:TPU:15, one launch (start us, length us, event | category | flops | bytes accessed | tf_op | source)
XLA Modules:
  0.0 385.2 jit_solution(4049898016924120267)
XLA Ops:
  7.2 6.3 %shard_map.139 = bf16[2,8,784,256]{3,2,1,0:T(8,128)(2,1)} custom-call(bf16[1024,1024]{1,0:T(8,128)(2,1)} %query_ref.3, bf16[1024,1024]{1,0:T(8,128)(2,1)} %grad_ref.3, bf16[1024,1024]{1,0:T(8,128)(2,1)} %saved_ref.3, f32[8,1024]{1,0:T(8,128)} %norm_ref.3), custom_call_target="tpu_custom_call" | custom-call | bytes 11010048 | tf_op jit(solution)/shard_map/pallas_call | solution.py:309
  13.5 6.7 %all-to-all-start = ((bf16[16,784,256]{2,1,0:T(8,128)(2,1)}), bf16[16,784,256]{2,1,0:T(8,128)(2,1)}, u32[]{:S(2)}, u32[]{:S(2)}) async-start(bf16[16,784,256]{2,1,0:T(8,128)(2,1)} %bitcast.50), calls=%async_computation | async-start | bytes 12845056 | tf_op jit(solution)/shard_map/all_to_all | solution.py:174
  20.2 0.9 bitcast_select_fusion
  21.1 5.7 %shard_map.137 = (bf16[2304,256]{1,0:T(8,128)(2,1)}, bf16[2304,256]{1,0:T(8,128)(2,1)}, bf16[2304,256]{1,0:T(8,128)(2,1)}, bf16[2304,256]{1,0:T(8,128)(2,1)}) custom-call(s32[1]{0:T(128)} %bitcast.5.mine_ref, bf16[1024,1024]{1,0:T(8,128)(2,1)} %key_ref.1, bf16[1024,1024]{1,0:T(8,128)(2,1)} %value_ref.1, bf16[128,1024]{1,0:T(8,128)(2,1)} %get-tuple-element.60.glob_key_ref, ...), custom_call_target="tpu_custom_call" | custom-call | bytes 9437184 | tf_op jit(solution)/shard_map/pallas_call | solution.py:343
  27.1 3.1 shard_map.138
  30.3 2.3 collective-permute-start.1
  32.6 118.7 %collective-permute-done.3.refs_4_ = bf16[2304,256]{1,0:T(8,128)(2,1)} collective-permute-done((bf16[2304,256]{1,0:T(8,128)(2,1)}, bf16[2304,256]{1,0:T(8,128)(2,1)}, u32[]{:S(2)}, u32[]{:S(2)}) %collective-permute-start.3) | collective-permute-done | bytes 1179680 | tf_op jit(solution)/shard_map/ppermute | solution.py:640
  151.3 17.6 %all-to-all-done.pair_ref = bf16[16,784,256]{2,1,0:T(8,128)(2,1)} async-done(((bf16[16,784,256]{2,1,0:T(8,128)(2,1)}), bf16[16,784,256]{2,1,0:T(8,128)(2,1)}, u32[]{:S(2)}, u32[]{:S(2)}) %all-to-all-start) | async-done | bytes 6422560 | tf_op jit(solution)/shard_map/all_to_all | solution.py:174
  169.0 4.0 %all-to-all-start.1 = ((bf16[16,264,256]{2,1,0:T(8,128)(2,1)}), bf16[16,264,256]{2,1,0:T(8,128)(2,1)S(1)}, u32[]{:S(2)}, u32[]{:S(2)}) async-start(bf16[16,264,256]{2,1,0:T(8,128)(2,1)} %bitcast.51), calls=%async_computation.1 | async-start | bytes 4325376 | tf_op jit(solution)/shard_map/all_to_all | solution.py:174
  173.4 11.0 %collective-permute-done.5.refs_6_ = bf16[2304,256]{1,0:T(8,128)(2,1)} collective-permute-done((bf16[2304,256]{1,0:T(8,128)(2,1)}, bf16[2304,256]{1,0:T(8,128)(2,1)}, u32[]{:S(2)}, u32[]{:S(2)}) %collective-permute-start.5) | collective-permute-done | bytes 1179680 | tf_op jit(solution)/shard_map/ppermute | solution.py:640
  188.0 1.7 collective-permute-done.2.refs_3_
  189.7 1.7 collective-permute-done.4.refs_5_
  191.3 1.7 add_convert_fusion.glob_ref
  193.1 50.0 %shard_map.140 = (bf16[16,768,128]{2,1,0:T(8,128)(2,1)}, f32[64,128,256]{2,1,0:T(8,128)}, f32[128,256]{1,0:T(8,128)}) custom-call(s32[435]{0:T(512)} %pad_add_fusion.table_ref, bf16[128,256]{1,0:T(8,128)(2,1)} %add_convert_fusion.glob_ref, bf16[16,784,256]{2,1,0:T(8,128)(2,1)} %all-to-all-done.pair_ref, bf16[2304,256]{1,0:T(8,128)(2,1)} %get-tuple-element.29.refs_0_, ...), custom_call_target="tpu_custom_call" | custom-call | flops 17716740096 | bytes 16777216 | tf_op jit(solution)/shard_map/pallas_call | solution.py:535
  243.1 1.4 copy-done.1
  244.5 7.0 %all-to-all-start.2 = ((bf16[16,768,128]{2,1,0:T(8,128)(2,1)}), bf16[16,768,128]{2,1,0:T(8,128)(2,1)S(1)}, u32[]{:S(2)}, u32[]{:S(2)}) async-start(bf16[16,768,128]{2,1,0:T(8,128)(2,1)} %get-tuple-element.41), calls=%async_computation.2 | async-start | bytes 6291456 | tf_op jit(solution)/shard_map/all_to_all | solution.py:174
  252.6 22.6 %shard_map.141 = (bf16[16,256,128]{2,1,0:T(8,128)(2,1)}, bf16[2048,256]{1,0:T(8,128)(2,1)}, bf16[2048,256]{1,0:T(8,128)(2,1)}, bf16[2048,256]{1,0:T(8,128)(2,1)}...) custom-call(s32[147]{0:T(256)} %pad_add_fusion.1.table_ref, bf16[128,256]{1,0:T(8,128)(2,1)} %add_convert_fusion.glob_ref, ...), custom_call_target="tpu_custom_call" | custom-call | flops 5905580032 | bytes 16777216 | tf_op jit(solution)/shard_map/pallas_call | solution.py:535
  275.5 1.6 select_convert_fusion
  277.3 2.3 collective-permute-start.12
  279.6 45.6 %all-to-all-done.2.refs_0_ = bf16[16,768,128]{2,1,0:T(8,128)(2,1)S(1)} async-done(((bf16[16,768,128]{2,1,0:T(8,128)(2,1)}), bf16[16,768,128]{2,1,0:T(8,128)(2,1)S(1)}, u32[]{:S(2)}, u32[]{:S(2)}) %all-to-all-start.2) | async-done | bytes 3145760 | tf_op jit(solution)/shard_map/all_to_all | solution.py:174
  325.2 8.2 %collective-permute-done.7.refs_4_ = bf16[2048,256]{1,0:T(8,128)(2,1)} collective-permute-done((bf16[2048,256]{1,0:T(8,128)(2,1)}, bf16[2048,256]{1,0:T(8,128)(2,1)}, u32[]{:S(2)}, u32[]{:S(2)}) %collective-permute-start.7) | collective-permute-done | bytes 1048608 | tf_op jit(solution)/shard_map/ppermute | solution.py:640
  333.3 6.2 %all-to-all-start.3 = ((bf16[16,256,128]{2,1,0:T(8,128)(2,1)}), bf16[16,256,128]{2,1,0:T(8,128)(2,1)}, u32[]{:S(2)}, u32[]{:S(2)}) async-start(bf16[16,256,128]{2,1,0:T(8,128)(2,1)} %get-tuple-element.45), calls=%async_computation.3 | async-start | bytes 2097152 | tf_op jit(solution)/shard_map/all_to_all | solution.py:174
  339.9 17.9 %collective-permute-done.9.refs_2_ = bf16[2048,256]{1,0:T(8,128)(2,1)} collective-permute-done((bf16[2048,256]{1,0:T(8,128)(2,1)}, bf16[2048,256]{1,0:T(8,128)(2,1)}, u32[]{:S(2)}, u32[]{:S(2)}) %collective-permute-start.9) | collective-permute-done | bytes 1048608 | tf_op jit(solution)/shard_map/ppermute | solution.py:640
  358.6 1.2 collective-permute-done.12.refs_6_
  359.8 2.4 collective-permute-start.13
  362.2 1.4 convert_element_type.57
  363.6 0.9 fusion
  364.5 1.2 convert_element_type.55
  365.7 0.9 fusion.34
  368.1 4.2 %shard_map.143 = (bf16[1024,1024]{1,0:T(8,128)(2,1)}, bf16[1024,1024]{1,0:T(8,128)(2,1)}) custom-call(s32[1]{0:T(128)} %bitcast.5.mine_ref, bf16[2048,256]{1,0:T(8,128)(2,1)} %get-tuple-element.46.refs_0_, bf16[2048,256]{1,0:T(8,128)(2,1)} %collective-permute-done.8.refs_1_, bf16[2048,256]{1,0:T(8,128)(2,1)} %collective-permute-done.9.refs_2_, ...), custom_call_target="tpu_custom_call" | custom-call | bytes 8388608 | tf_op jit(solution)/shard_map/pallas_call | solution.py:599
  372.3 1.9 all-to-all-done.3.refs_1_
  374.3 4.1 %shard_map.142 = bf16[1024,1024]{1,0:T(8,128)(2,1)} custom-call(bf16[16,768,128]{2,1,0:T(8,128)(2,1)} %copy-done, bf16[16,256,128]{2,1,0:T(8,128)(2,1)} %all-to-all-done.3.refs_1_), custom_call_target="tpu_custom_call" | custom-call | bytes 6291456 | tf_op jit(solution)/shard_map/pallas_call | solution.py:566
  (55 shorter events, 8.6 us)
Async XLA Ops:
  13.5 6.7 %copy-start.5 = (s32[128]{0:T(128)S(1)}, s32[128]{0:T(128)}, u32[]{:S(2)}) copy-start(s32[128]{0:T(128)} %param.19) | copy-start | bytes 1540
  13.5 6.7 %copy-start.2 = (bf16[1,128,1024]{2,1,0:T(8,128)(2,1)S(1)}, bf16[1,128,1024]{2,1,0:T(8,128)(2,1)}, u32[]{:S(2)}) copy-start(bf16[1,128,1024]{2,1,0:T(8,128)(2,1)} %param.17) | copy-start | bytes 786436
  13.5 6.7 %copy-start.3 = (bf16[1,128,1024]{2,1,0:T(8,128)(2,1)S(1)}, bf16[1,128,1024]{2,1,0:T(8,128)(2,1)}, u32[]{:S(2)}) copy-start(bf16[1,128,1024]{2,1,0:T(8,128)(2,1)} %param.16) | copy-start | bytes 786436
  13.5 155.5 %all-to-all-start = ((bf16[16,784,256]{2,1,0:T(8,128)(2,1)}), bf16[16,784,256]{2,1,0:T(8,128)(2,1)}, u32[]{:S(2)}, u32[]{:S(2)}) async-start(bf16[16,784,256]{2,1,0:T(8,128)(2,1)} %bitcast.50), calls=%async_computation | async-start | bytes 12845056 | tf_op jit(solution)/shard_map/all_to_all | solution.py:174
  26.8 124.5 %collective-permute-start.3 = (bf16[2304,256]{1,0:T(8,128)(2,1)}, bf16[2304,256]{1,0:T(8,128)(2,1)}, u32[]{:S(2)}, u32[]{:S(2)}) collective-permute-start(bf16[2304,256]{1,0:T(8,128)(2,1)} %get-tuple-element.33), channel_id=1, source_target_pairs={{0,8},{2,10},{4,12},{6,14},{8,0},{10,2},{12,4},{14,6},{16,24},{18,... | collective-permute-start | bytes 3538952 | tf_op jit(solution)/shard_map/ppermute | solution.py:640
  30.2 154.1 %collective-permute-start.5 = (bf16[2304,256]{1,0:T(8,128)(2,1)}, bf16[2304,256]{1,0:T(8,128)(2,1)}, u32[]{:S(2)}, u32[]{:S(2)}) collective-permute-start(bf16[2304,256]{1,0:T(8,128)(2,1)} %get-tuple-element.35), channel_id=1, source_target_pairs={{0,12},{2,14},{4,0},{6,2},{8,4},{10,6},{12,8},{14,10},{16,28},{18,... | collective-permute-start | bytes 3538952 | tf_op jit(solution)/shard_map/ppermute | solution.py:640
  30.3 155.4 %copy-start.4 = (s32[128,3]{0,1:T(4,128)S(1)}, s32[128,3]{0,1:T(4,128)}, u32[]{:S(2)}) copy-start(s32[128,3]{0,1:T(4,128)} %param.18) | copy-start | bytes 4612
  30.3 154.8 %collective-permute-start.1 = (bf16[2304,256]{1,0:T(8,128)(2,1)}, bf16[2304,256]{1,0:T(8,128)(2,1)}, u32[]{:S(2)}, u32[]{:S(2)}) collective-permute-start(bf16[2304,256]{1,0:T(8,128)(2,1)} %get-tuple-element.30), channel_id=1, source_target_pairs={{0,4},{2,6},{4,8},{6,10},{8,12},{10,14},{12,0},{14,2},{16,20},{18,... | collective-permute-start | bytes 3538952 | tf_op jit(solution)/shard_map/ppermute | solution.py:640
  169.0 74.1 %all-to-all-start.1 = ((bf16[16,264,256]{2,1,0:T(8,128)(2,1)}), bf16[16,264,256]{2,1,0:T(8,128)(2,1)S(1)}, u32[]{:S(2)}, u32[]{:S(2)}) async-start(bf16[16,264,256]{2,1,0:T(8,128)(2,1)} %bitcast.51), calls=%async_computation.1 | async-start | bytes 4325376 | tf_op jit(solution)/shard_map/all_to_all | solution.py:174
  172.9 14.4 %collective-permute-start = (bf16[2304,256]{1,0:T(8,128)(2,1)}, bf16[2304,256]{1,0:T(8,128)(2,1)}, u32[]{:S(2)}, u32[]{:S(2)}) collective-permute-start(bf16[2304,256]{1,0:T(8,128)(2,1)} %get-tuple-element.29.refs_0_), channel_id=1, source_target_pairs={{0,2},{2,0},{4,6},{6,4},{8,10},{10,8},{12,14},{14,12},{16,18},{18,... | collective-permute-start | bytes 3538952 | tf_op jit(solution)/shard_map/ppermute | solution.py:643
  184.4 3.6 collective-permute-start.6
  185.2 4.5 %collective-permute-start.2 = (bf16[2304,256]{1,0:T(8,128)(2,1)}, bf16[2304,256]{1,0:T(8,128)(2,1)}, u32[]{:S(2)}, u32[]{:S(2)}) collective-permute-start(bf16[2304,256]{1,0:T(8,128)(2,1)} %collective-permute-done.1.refs_2_), channel_id=1, source_target_pairs={{0,2},{2,0},{4,6},{6,4},{8,10},{10,8},{12,14},{14,12},{16,18},{18,... | collective-permute-start | bytes 3538952 | tf_op jit(solution)/shard_map/ppermute | solution.py:643
  185.2 6.2 %collective-permute-start.4 = (bf16[2304,256]{1,0:T(8,128)(2,1)}, bf16[2304,256]{1,0:T(8,128)(2,1)}, u32[]{:S(2)}, u32[]{:S(2)}) collective-permute-start(bf16[2304,256]{1,0:T(8,128)(2,1)} %collective-permute-done.3.refs_4_), channel_id=1, source_target_pairs={{0,2},{2,0},{4,6},{6,4},{8,10},{10,8},{12,14},{14,12},{16,18},{18,... | collective-permute-start | bytes 3538952 | tf_op jit(solution)/shard_map/ppermute | solution.py:643
  243.1 1.4 copy-start.1
  244.5 80.7 %all-to-all-start.2 = ((bf16[16,768,128]{2,1,0:T(8,128)(2,1)}), bf16[16,768,128]{2,1,0:T(8,128)(2,1)S(1)}, u32[]{:S(2)}, u32[]{:S(2)}) async-start(bf16[16,768,128]{2,1,0:T(8,128)(2,1)} %get-tuple-element.41), calls=%async_computation.2 | async-start | bytes 6291456 | tf_op jit(solution)/shard_map/all_to_all | solution.py:174
  251.4 110.8 %all-gather.3.cloned.1.call-start = ((), (), s32[]{:S(2)}) async-start(), calls=%async_computation.4 | async-start | bytes 1114112 | tf_op jit(solution)/shard_map/all_gather | solution.py:702
  275.2 58.2 %collective-permute-start.7 = (bf16[2048,256]{1,0:T(8,128)(2,1)}, bf16[2048,256]{1,0:T(8,128)(2,1)}, u32[]{:S(2)}, u32[]{:S(2)}) collective-permute-start(bf16[2048,256]{1,0:T(8,128)(2,1)} %get-tuple-element.44), channel_id=1, source_target_pairs={{0,8},{2,10},{4,12},{6,14},{8,0},{10,2},{12,4},{14,6},{16,24},{18,... | collective-permute-start | bytes 3145736 | tf_op jit(solution)/shard_map/ppermute | solution.py:640
  277.2 80.6 %collective-permute-start.9 = (bf16[2048,256]{1,0:T(8,128)(2,1)}, bf16[2048,256]{1,0:T(8,128)(2,1)}, u32[]{:S(2)}, u32[]{:S(2)}) collective-permute-start(bf16[2048,256]{1,0:T(8,128)(2,1)} %get-tuple-element.47), channel_id=1, source_target_pairs={{0,12},{2,14},{4,0},{6,2},{8,4},{10,6},{12,8},{14,10},{16,28},{18,... | collective-permute-start | bytes 3145736 | tf_op jit(solution)/shard_map/ppermute | solution.py:640
  277.3 82.5 %collective-permute-start.12 = (bf16[2048,256]{1,0:T(8,128)(2,1)}, bf16[2048,256]{1,0:T(8,128)(2,1)}, u32[]{:S(2)}, u32[]{:S(2)}) collective-permute-start(bf16[2048,256]{1,0:T(8,128)(2,1)} %get-tuple-element.49), channel_id=1, source_target_pairs={{0,4},{2,6},{4,8},{6,10},{8,12},{10,14},{12,0},{14,2},{16,20},{18,... | collective-permute-start | bytes 3145736 | tf_op jit(solution)/shard_map/ppermute | solution.py:640
  325.2 38.4 %copy-start = (bf16[16,768,128]{2,1,0:T(8,128)(2,1)}, bf16[16,768,128]{2,1,0:T(8,128)(2,1)S(1)}, u32[]{:S(2)}) copy-start(bf16[16,768,128]{2,1,0:T(8,128)(2,1)S(1)} %all-to-all-done.2.refs_0_) | copy-start | bytes 9437188
  333.3 40.9 %all-to-all-start.3 = ((bf16[16,256,128]{2,1,0:T(8,128)(2,1)}), bf16[16,256,128]{2,1,0:T(8,128)(2,1)}, u32[]{:S(2)}, u32[]{:S(2)}) async-start(bf16[16,256,128]{2,1,0:T(8,128)(2,1)} %get-tuple-element.45), calls=%async_computation.3 | async-start | bytes 2097152 | tf_op jit(solution)/shard_map/all_to_all | solution.py:174
  339.5 28.6 %collective-permute-start.8 = (bf16[2048,256]{1,0:T(8,128)(2,1)}, bf16[2048,256]{1,0:T(8,128)(2,1)}, u32[]{:S(2)}, u32[]{:S(2)}) collective-permute-start(bf16[2048,256]{1,0:T(8,128)(2,1)} %get-tuple-element.46.refs_0_), channel_id=1, source_target_pairs={{0,2},{2,0},{4,6},{6,4},{8,10},{10,8},{12,14},{14,12},{16,18},{18,... | collective-permute-start | bytes 3145736 | tf_op jit(solution)/shard_map/ppermute | solution.py:643
  357.8 10.3 %collective-permute-start.10 = (bf16[2048,256]{1,0:T(8,128)(2,1)}, bf16[2048,256]{1,0:T(8,128)(2,1)}, u32[]{:S(2)}, u32[]{:S(2)}) collective-permute-start(bf16[2048,256]{1,0:T(8,128)(2,1)} %collective-permute-done.9.refs_2_), channel_id=1, source_target_pairs={{0,2},{2,0},{4,6},{6,4},{8,10},{10,8},{12,14},{14,12},{16,18},{18,... | collective-permute-start | bytes 3145736 | tf_op jit(solution)/shard_map/ppermute | solution.py:643
  359.8 8.4 %collective-permute-start.13 = (bf16[2048,256]{1,0:T(8,128)(2,1)}, bf16[2048,256]{1,0:T(8,128)(2,1)}, u32[]{:S(2)}, u32[]{:S(2)}) collective-permute-start(bf16[2048,256]{1,0:T(8,128)(2,1)} %collective-permute-done.12.refs_6_), channel_id=1, source_target_pairs={{0,2},{2,0},{4,6},{6,4},{8,10},{10,8},{12,14},{14,12},{16,18},{18,... | collective-permute-start | bytes 3145736 | tf_op jit(solution)/shard_map/ppermute | solution.py:643
  362.2 5.9 %collective-permute-start.11 = (bf16[2048,256]{1,0:T(8,128)(2,1)}, bf16[2048,256]{1,0:T(8,128)(2,1)}, u32[]{:S(2)}, u32[]{:S(2)}) collective-permute-start(bf16[2048,256]{1,0:T(8,128)(2,1)} %collective-permute-done.7.refs_4_), channel_id=1, source_target_pairs={{0,2},{2,0},{4,6},{6,4},{8,10},{10,8},{12,14},{14,12},{16,18},{18,... | collective-permute-start | bytes 3145736 | tf_op jit(solution)/shard_map/ppermute | solution.py:643
Sparse Core Ops, SparseCore 0:
  277.3 57.4 all-gather.2

commit v6 on v5

--- a/solution.py
+++ b/solution.py
@@ -549,30 +549,32 @@
     )(table, glob, pairs, *kv, *before)
 
 
-def unpack_queries_kernel(*refs):
-    *in_refs, out_ref = refs
-    heads = in_refs[0].shape[0] // 2
-    for (first, some), in_ref in zip(CHUNKS, in_refs):
-        for head in range(heads):
-            total = in_ref[head].astype(jnp.float32) + in_ref[heads + head].astype(jnp.float32)
-            out_ref[first * BLK : (first + some) * BLK, head * HD : (head + 1) * HD] = total.astype(
-                jnp.bfloat16
-            )
-
-
-def unpack_queries(arrays):
-    shape = (sum(array.shape[1] for array in arrays), arrays[0].shape[0] // 2 * HD)
-    vmem = pl.BlockSpec(memory_space=pltpu.VMEM)
+def unpack_queries_kernel(in_ref, *refs):
+    out_ref = refs[-1]
+    heads = in_ref.shape[0] // 2
+    for head in range(heads):
+        total = in_ref[head].astype(jnp.float32) + in_ref[heads + head].astype(jnp.float32)
+        out_ref[:, head * HD : (head + 1) * HD] = total.astype(jnp.bfloat16)
+
+
+def unpack_queries(array, chunk, tokens, *before):
+    first, some = CHUNKS[chunk]
+    sources, rows, _ = array.shape
+    width = sources // 2 * HD
+    place = first // some
     return pl.pallas_call(
         unpack_queries_kernel,
-        in_specs=[vmem] * len(arrays),
-        out_specs=vmem,
-        out_shape=jax.ShapeDtypeStruct(shape, jnp.bfloat16),
+        grid=(1,),
+        in_specs=[pl.BlockSpec(array.shape, lambda i: (0, 0, 0))]
+        + [pl.BlockSpec(memory_space=pl.ANY)] * len(before),
+        out_specs=pl.BlockSpec((rows, width), lambda i: (place, 0)),
+        out_shape=jax.ShapeDtypeStruct((tokens, width), jnp.bfloat16),
+        input_output_aliases={1: 0} if before else {},
         compiler_params=pltpu.CompilerParams(vmem_limit_bytes=VMEM_LIMIT),
         cost_estimate=pl.CostEstimate(
-            flops=0, bytes_accessed=shape[0] * shape[1] * 6, transcendentals=0
-        ),
-    )(*arrays)
+            flops=0, bytes_accessed=rows * width * 6, transcendentals=0
+        ),
+    )(array, *before)
 
 
 def unpack_keys_kernel(mine_ref, *refs):
@@ -697,7 +699,8 @@
     grad_keys, grad_values = unpack_keys(
         mine_one, [piece for slab in slabs for piece in (slab, over(slab))]
     )
-    grad_queries = unpack_queries((back_first, back_second))
+    early = unpack_queries(back_first, 0, tokens)
+    grad_queries = unpack_queries(back_second, 1, tokens, early)
     held = (glob_owner // heads == half)[:, None]
     glob_parts = lax.all_gather(
         jnp.where(held, dglob, 0.0).astype(jnp.bfloat16), "seq", axis=0, tiled=False

time: 392 us -> 390 us (level)
  transfers between devices with their start and end apart: 19 -> 19, of which waited for: 11 -> 11; matrix products, arithmetic and copies ran while one was open for 3% -> 3% of each run, Pallas kernels for 22% -> 23%
where the time goes in v6:
time: 390 us; the launch traced here: 383 us
  waiting for transfers between devices  225 us (58%)
  Pallas kernels  97.6 us (25%)
  starting transfers between devices  34.8 us (9%)
  between operations  14.2 us (4%)
  other arithmetic  7.52 us (2%)
  local copies, waits for them, and re-layouts  4.67 us (1%)
    ppermute x6, waiting for transfers between devices, turn(): return lax.ppermute(array, 'seq', pairs) if step % chips else array  157 us
    pallas_call x2, Pallas kernels, chunk_call(): pl.pallas_call(functools.partial(chunk_kernel, chunk, heads), in_specs=[s...  72.5 us
    all_to_all x4, waiting for transfers between devices, exchange(): return lax.all_to_all(array, 'seq', split_axis=0, concat_axis=0, tiled=True)  63.5 us
    all_to_all x4, starting transfers between devices, exchange(): return lax.all_to_all(array, 'seq', split_axis=0, concat_axis=0, tiled=True)  23.8 us
    pallas_call x2, Pallas kernels, pack_queries(): pl.pallas_call(pack_kernel, grid=(1,), in_specs=[spec] * 3 + [pl.BlockSpe...  9.46 us
  transfers between devices with their start and end apart: 19, of which 11 were waited for; matrix products, arithmetic and copies ran while one was open for 3% of the time, Pallas kernels for 23%

profile of v6, /device:TPU:15, one launch (start us, length us, event | category | flops | bytes accessed | tf_op | source)
XLA Modules:
  0.0 383.3 jit_solution(8146431366367605348)
XLA Ops:
  7.2 6.3 %shard_map.139 = bf16[2,8,784,256]{3,2,1,0:T(8,128)(2,1)} custom-call(bf16[1024,1024]{1,0:T(8,128)(2,1)} %query_ref.3, bf16[1024,1024]{1,0:T(8,128)(2,1)} %grad_ref.3, bf16[1024,1024]{1,0:T(8,128)(2,1)} %saved_ref.3, f32[8,1024]{1,0:T(8,128)} %norm_ref.3), custom_call_target="tpu_custom_call" | custom-call | bytes 11010048 | tf_op jit(solution)/shard_map/pallas_call | solution.py:309
  13.5 6.7 %all-to-all-start = ((bf16[16,784,256]{2,1,0:T(8,128)(2,1)}), bf16[16,784,256]{2,1,0:T(8,128)(2,1)}, u32[]{:S(2)}, u32[]{:S(2)}) async-start(bf16[16,784,256]{2,1,0:T(8,128)(2,1)} %bitcast.50), calls=%async_computation | async-start | bytes 12845056 | tf_op jit(solution)/shard_map/all_to_all | solution.py:174
  20.2 0.9 bitcast_select_fusion
  21.1 5.7 %shard_map.137 = (bf16[2304,256]{1,0:T(8,128)(2,1)}, bf16[2304,256]{1,0:T(8,128)(2,1)}, bf16[2304,256]{1,0:T(8,128)(2,1)}, bf16[2304,256]{1,0:T(8,128)(2,1)}) custom-call(s32[1]{0:T(128)} %bitcast.5.mine_ref, bf16[1024,1024]{1,0:T(8,128)(2,1)} %key_ref.1, bf16[1024,1024]{1,0:T(8,128)(2,1)} %value_ref.1, bf16[128,1024]{1,0:T(8,128)(2,1)} %get-tuple-element.60.glob_key_ref, ...), custom_call_target="tpu_custom_call" | custom-call | bytes 9437184 | tf_op jit(solution)/shard_map/pallas_call | solution.py:343
  27.1 3.1 shard_map.138
  30.3 2.3 collective-permute-start.1
  32.6 118.7 %collective-permute-done.3.refs_4_ = bf16[2304,256]{1,0:T(8,128)(2,1)} collective-permute-done((bf16[2304,256]{1,0:T(8,128)(2,1)}, bf16[2304,256]{1,0:T(8,128)(2,1)}, u32[]{:S(2)}, u32[]{:S(2)}) %collective-permute-start.3) | collective-permute-done | bytes 1179680 | tf_op jit(solution)/shard_map/ppermute | solution.py:642
  151.3 17.6 %all-to-all-done.pair_ref = bf16[16,784,256]{2,1,0:T(8,128)(2,1)} async-done(((bf16[16,784,256]{2,1,0:T(8,128)(2,1)}), bf16[16,784,256]{2,1,0:T(8,128)(2,1)}, u32[]{:S(2)}, u32[]{:S(2)}) %all-to-all-start) | async-done | bytes 6422560 | tf_op jit(solution)/shard_map/all_to_all | solution.py:174
  169.0 4.0 %all-to-all-start.1 = ((bf16[16,264,256]{2,1,0:T(8,128)(2,1)}), bf16[16,264,256]{2,1,0:T(8,128)(2,1)S(1)}, u32[]{:S(2)}, u32[]{:S(2)}) async-start(bf16[16,264,256]{2,1,0:T(8,128)(2,1)} %bitcast.51), calls=%async_computation.1 | async-start | bytes 4325376 | tf_op jit(solution)/shard_map/all_to_all | solution.py:174
  173.4 11.0 %collective-permute-done.5.refs_6_ = bf16[2304,256]{1,0:T(8,128)(2,1)} collective-permute-done((bf16[2304,256]{1,0:T(8,128)(2,1)}, bf16[2304,256]{1,0:T(8,128)(2,1)}, u32[]{:S(2)}, u32[]{:S(2)}) %collective-permute-start.5) | collective-permute-done | bytes 1179680 | tf_op jit(solution)/shard_map/ppermute | solution.py:642
  188.0 1.7 collective-permute-done.2.refs_3_
  189.7 1.7 collective-permute-done.4.refs_5_
  191.3 1.7 add_convert_fusion.glob_ref
  193.1 50.0 %shard_map.140 = (bf16[16,768,128]{2,1,0:T(8,128)(2,1)}, f32[64,128,256]{2,1,0:T(8,128)}, f32[128,256]{1,0:T(8,128)}) custom-call(s32[435]{0:T(512)} %pad_add_fusion.table_ref, bf16[128,256]{1,0:T(8,128)(2,1)} %add_convert_fusion.glob_ref, bf16[16,784,256]{2,1,0:T(8,128)(2,1)} %all-to-all-done.pair_ref, bf16[2304,256]{1,0:T(8,128)(2,1)} %get-tuple-element.29.refs_0_, ...), custom_call_target="tpu_custom_call" | custom-call | flops 17716740096 | bytes 16777216 | tf_op jit(solution)/shard_map/pallas_call | solution.py:535
  243.1 1.4 copy-done.1
  244.5 7.0 %all-to-all-start.2 = ((bf16[16,768,128]{2,1,0:T(8,128)(2,1)}), bf16[16,768,128]{2,1,0:T(8,128)(2,1)S(1)}, u32[]{:S(2)}, u32[]{:S(2)}) async-start(bf16[16,768,128]{2,1,0:T(8,128)(2,1)} %get-tuple-element.41), calls=%async_computation.2 | async-start | bytes 6291456 | tf_op jit(solution)/shard_map/all_to_all | solution.py:174
  252.6 22.6 %shard_map.141 = (bf16[16,256,128]{2,1,0:T(8,128)(2,1)}, bf16[2048,256]{1,0:T(8,128)(2,1)}, bf16[2048,256]{1,0:T(8,128)(2,1)}, bf16[2048,256]{1,0:T(8,128)(2,1)}...) custom-call(s32[147]{0:T(256)} %pad_add_fusion.1.table_ref, bf16[128,256]{1,0:T(8,128)(2,1)} %add_convert_fusion.glob_ref, ...), custom_call_target="tpu_custom_call" | custom-call | flops 5905580032 | bytes 16777216 | tf_op jit(solution)/shard_map/pallas_call | solution.py:535
  275.5 1.6 select_convert_fusion
  277.3 2.3 collective-permute-start.12
  279.6 45.6 %all-to-all-done.2.in_ref = bf16[16,768,128]{2,1,0:T(8,128)(2,1)S(1)} async-done(((bf16[16,768,128]{2,1,0:T(8,128)(2,1)}), bf16[16,768,128]{2,1,0:T(8,128)(2,1)S(1)}, u32[]{:S(2)}, u32[]{:S(2)}) %all-to-all-start.2) | async-done | bytes 3145760 | tf_op jit(solution)/shard_map/all_to_all | solution.py:174
  325.2 8.2 %collective-permute-done.7.refs_4_ = bf16[2048,256]{1,0:T(8,128)(2,1)} collective-permute-done((bf16[2048,256]{1,0:T(8,128)(2,1)}, bf16[2048,256]{1,0:T(8,128)(2,1)}, u32[]{:S(2)}, u32[]{:S(2)}) %collective-permute-start.7) | collective-permute-done | bytes 1048608 | tf_op jit(solution)/shard_map/ppermute | solution.py:642
  333.3 6.2 %all-to-all-start.3 = ((bf16[16,256,128]{2,1,0:T(8,128)(2,1)}), bf16[16,256,128]{2,1,0:T(8,128)(2,1)}, u32[]{:S(2)}, u32[]{:S(2)}) async-start(bf16[16,256,128]{2,1,0:T(8,128)(2,1)} %get-tuple-element.44), calls=%async_computation.3 | async-start | bytes 2097152 | tf_op jit(solution)/shard_map/all_to_all | solution.py:174
  339.9 17.9 %collective-permute-done.9.refs_2_ = bf16[2048,256]{1,0:T(8,128)(2,1)} collective-permute-done((bf16[2048,256]{1,0:T(8,128)(2,1)}, bf16[2048,256]{1,0:T(8,128)(2,1)}, u32[]{:S(2)}, u32[]{:S(2)}) %collective-permute-start.9) | collective-permute-done | bytes 1048608 | tf_op jit(solution)/shard_map/ppermute | solution.py:642
  357.8 0.8 collective-permute-start.10
  358.6 1.2 collective-permute-done.12.refs_6_
  359.8 2.4 collective-permute-start.13
  362.2 3.5 shard_map.142.refs_0_
  365.7 1.4 convert_element_type.57
  367.4 0.9 fusion.34
  368.9 0.9 copy_bitcast_fusion
  369.8 4.2 %shard_map.144 = (bf16[1024,1024]{1,0:T(8,128)(2,1)}, bf16[1024,1024]{1,0:T(8,128)(2,1)}) custom-call(s32[1]{0:T(128)} %bitcast.5.mine_ref, bf16[2048,256]{1,0:T(8,128)(2,1)} %get-tuple-element.46.refs_0_, bf16[2048,256]{1,0:T(8,128)(2,1)} %collective-permute-done.8.refs_1_, bf16[2048,256]{1,0:T(8,128)(2,1)} %collective-permute-done.9.refs_2_, ...), custom_call_target="tpu_custom_call" | custom-call | bytes 8388608 | tf_op jit(solution)/shard_map/pallas_call | solution.py:601
  374.3 2.2 shard_map.143
  (56 shorter events, 7.5 us)
Async XLA Ops:
  13.5 6.7 %copy-start.5 = (s32[128]{0:T(128)S(1)}, s32[128]{0:T(128)}, u32[]{:S(2)}) copy-start(s32[128]{0:T(128)} %param.19) | copy-start | bytes 1540
  13.5 6.7 %copy-start.2 = (bf16[1,128,1024]{2,1,0:T(8,128)(2,1)S(1)}, bf16[1,128,1024]{2,1,0:T(8,128)(2,1)}, u32[]{:S(2)}) copy-start(bf16[1,128,1024]{2,1,0:T(8,128)(2,1)} %param.17) | copy-start | bytes 786436
  13.5 6.7 %copy-start.3 = (bf16[1,128,1024]{2,1,0:T(8,128)(2,1)S(1)}, bf16[1,128,1024]{2,1,0:T(8,128)(2,1)}, u32[]{:S(2)}) copy-start(bf16[1,128,1024]{2,1,0:T(8,128)(2,1)} %param.16) | copy-start | bytes 786436
  13.5 155.5 %all-to-all-start = ((bf16[16,784,256]{2,1,0:T(8,128)(2,1)}), bf16[16,784,256]{2,1,0:T(8,128)(2,1)}, u32[]{:S(2)}, u32[]{:S(2)}) async-start(bf16[16,784,256]{2,1,0:T(8,128)(2,1)} %bitcast.50), calls=%async_computation | async-start | bytes 12845056 | tf_op jit(solution)/shard_map/all_to_all | solution.py:174
  26.8 124.5 %collective-permute-start.3 = (bf16[2304,256]{1,0:T(8,128)(2,1)}, bf16[2304,256]{1,0:T(8,128)(2,1)}, u32[]{:S(2)}, u32[]{:S(2)}) collective-permute-start(bf16[2304,256]{1,0:T(8,128)(2,1)} %get-tuple-element.33), channel_id=1, source_target_pairs={{0,8},{2,10},{4,12},{6,14},{8,0},{10,2},{12,4},{14,6},{16,24},{18,... | collective-permute-start | bytes 3538952 | tf_op jit(solution)/shard_map/ppermute | solution.py:642
  30.2 154.1 %collective-permute-start.5 = (bf16[2304,256]{1,0:T(8,128)(2,1)}, bf16[2304,256]{1,0:T(8,128)(2,1)}, u32[]{:S(2)}, u32[]{:S(2)}) collective-permute-start(bf16[2304,256]{1,0:T(8,128)(2,1)} %get-tuple-element.35), channel_id=1, source_target_pairs={{0,12},{2,14},{4,0},{6,2},{8,4},{10,6},{12,8},{14,10},{16,28},{18,... | collective-permute-start | bytes 3538952 | tf_op jit(solution)/shard_map/ppermute | solution.py:642
  30.3 155.4 %copy-start.4 = (s32[128,3]{0,1:T(4,128)S(1)}, s32[128,3]{0,1:T(4,128)}, u32[]{:S(2)}) copy-start(s32[128,3]{0,1:T(4,128)} %param.18) | copy-start | bytes 4612
  30.3 154.8 %collective-permute-start.1 = (bf16[2304,256]{1,0:T(8,128)(2,1)}, bf16[2304,256]{1,0:T(8,128)(2,1)}, u32[]{:S(2)}, u32[]{:S(2)}) collective-permute-start(bf16[2304,256]{1,0:T(8,128)(2,1)} %get-tuple-element.30), channel_id=1, source_target_pairs={{0,4},{2,6},{4,8},{6,10},{8,12},{10,14},{12,0},{14,2},{16,20},{18,... | collective-permute-start | bytes 3538952 | tf_op jit(solution)/shard_map/ppermute | solution.py:642
  169.0 74.1 %all-to-all-start.1 = ((bf16[16,264,256]{2,1,0:T(8,128)(2,1)}), bf16[16,264,256]{2,1,0:T(8,128)(2,1)S(1)}, u32[]{:S(2)}, u32[]{:S(2)}) async-start(bf16[16,264,256]{2,1,0:T(8,128)(2,1)} %bitcast.51), calls=%async_computation.1 | async-start | bytes 4325376 | tf_op jit(solution)/shard_map/all_to_all | solution.py:174
  172.9 14.4 %collective-permute-start = (bf16[2304,256]{1,0:T(8,128)(2,1)}, bf16[2304,256]{1,0:T(8,128)(2,1)}, u32[]{:S(2)}, u32[]{:S(2)}) collective-permute-start(bf16[2304,256]{1,0:T(8,128)(2,1)} %get-tuple-element.29.refs_0_), channel_id=1, source_target_pairs={{0,2},{2,0},{4,6},{6,4},{8,10},{10,8},{12,14},{14,12},{16,18},{18,... | collective-permute-start | bytes 3538952 | tf_op jit(solution)/shard_map/ppermute | solution.py:645
  184.4 3.6 collective-permute-start.6
  185.2 4.5 %collective-permute-start.2 = (bf16[2304,256]{1,0:T(8,128)(2,1)}, bf16[2304,256]{1,0:T(8,128)(2,1)}, u32[]{:S(2)}, u32[]{:S(2)}) collective-permute-start(bf16[2304,256]{1,0:T(8,128)(2,1)} %collective-permute-done.1.refs_2_), channel_id=1, source_target_pairs={{0,2},{2,0},{4,6},{6,4},{8,10},{10,8},{12,14},{14,12},{16,18},{18,... | collective-permute-start | bytes 3538952 | tf_op jit(solution)/shard_map/ppermute | solution.py:645
  185.2 6.2 %collective-permute-start.4 = (bf16[2304,256]{1,0:T(8,128)(2,1)}, bf16[2304,256]{1,0:T(8,128)(2,1)}, u32[]{:S(2)}, u32[]{:S(2)}) collective-permute-start(bf16[2304,256]{1,0:T(8,128)(2,1)} %collective-permute-done.3.refs_4_), channel_id=1, source_target_pairs={{0,2},{2,0},{4,6},{6,4},{8,10},{10,8},{12,14},{14,12},{16,18},{18,... | collective-permute-start | bytes 3538952 | tf_op jit(solution)/shard_map/ppermute | solution.py:645
  243.1 1.4 copy-start.1
  244.5 80.7 %all-to-all-start.2 = ((bf16[16,768,128]{2,1,0:T(8,128)(2,1)}), bf16[16,768,128]{2,1,0:T(8,128)(2,1)S(1)}, u32[]{:S(2)}, u32[]{:S(2)}) async-start(bf16[16,768,128]{2,1,0:T(8,128)(2,1)} %get-tuple-element.41), calls=%async_computation.2 | async-start | bytes 6291456 | tf_op jit(solution)/shard_map/all_to_all | solution.py:174
  251.4 114.3 %all-gather.3.cloned.1.call-start = ((), (), s32[]{:S(2)}) async-start(), calls=%async_computation.4 | async-start | bytes 1114112 | tf_op jit(solution)/shard_map/all_gather | solution.py:705
  275.1 58.2 %collective-permute-start.7 = (bf16[2048,256]{1,0:T(8,128)(2,1)}, bf16[2048,256]{1,0:T(8,128)(2,1)}, u32[]{:S(2)}, u32[]{:S(2)}) collective-permute-start(bf16[2048,256]{1,0:T(8,128)(2,1)} %get-tuple-element.43), channel_id=1, source_target_pairs={{0,8},{2,10},{4,12},{6,14},{8,0},{10,2},{12,4},{14,6},{16,24},{18,... | collective-permute-start | bytes 3145736 | tf_op jit(solution)/shard_map/ppermute | solution.py:642
  277.1 80.7 %collective-permute-start.9 = (bf16[2048,256]{1,0:T(8,128)(2,1)}, bf16[2048,256]{1,0:T(8,128)(2,1)}, u32[]{:S(2)}, u32[]{:S(2)}) collective-permute-start(bf16[2048,256]{1,0:T(8,128)(2,1)} %get-tuple-element.47), channel_id=1, source_target_pairs={{0,12},{2,14},{4,0},{6,2},{8,4},{10,6},{12,8},{14,10},{16,28},{18,... | collective-permute-start | bytes 3145736 | tf_op jit(solution)/shard_map/ppermute | solution.py:642
  277.3 82.5 %collective-permute-start.12 = (bf16[2048,256]{1,0:T(8,128)(2,1)}, bf16[2048,256]{1,0:T(8,128)(2,1)}, u32[]{:S(2)}, u32[]{:S(2)}) collective-permute-start(bf16[2048,256]{1,0:T(8,128)(2,1)} %get-tuple-element.49), channel_id=1, source_target_pairs={{0,4},{2,6},{4,8},{6,10},{8,12},{10,14},{12,0},{14,2},{16,20},{18,... | collective-permute-start | bytes 3145736 | tf_op jit(solution)/shard_map/ppermute | solution.py:642
  325.2 37.0 %copy-start = (bf16[16,768,128]{2,1,0:T(8,128)(2,1)}, bf16[16,768,128]{2,1,0:T(8,128)(2,1)S(1)}, u32[]{:S(2)}) copy-start(bf16[16,768,128]{2,1,0:T(8,128)(2,1)S(1)} %all-to-all-done.2.in_ref) | copy-start | bytes 9437188
  333.3 40.9 %all-to-all-start.3 = ((bf16[16,256,128]{2,1,0:T(8,128)(2,1)}), bf16[16,256,128]{2,1,0:T(8,128)(2,1)}, u32[]{:S(2)}, u32[]{:S(2)}) async-start(bf16[16,256,128]{2,1,0:T(8,128)(2,1)} %get-tuple-element.44), calls=%async_computation.3 | async-start | bytes 2097152 | tf_op jit(solution)/shard_map/all_to_all | solution.py:174
  339.5 30.3 %collective-permute-start.8 = (bf16[2048,256]{1,0:T(8,128)(2,1)}, bf16[2048,256]{1,0:T(8,128)(2,1)}, u32[]{:S(2)}, u32[]{:S(2)}) collective-permute-start(bf16[2048,256]{1,0:T(8,128)(2,1)} %get-tuple-element.46.refs_0_), channel_id=1, source_target_pairs={{0,2},{2,0},{4,6},{6,4},{8,10},{10,8},{12,14},{14,12},{16,18},{18,... | collective-permute-start | bytes 3145736 | tf_op jit(solution)/shard_map/ppermute | solution.py:645
  357.8 12.0 %collective-permute-start.10 = (bf16[2048,256]{1,0:T(8,128)(2,1)}, bf16[2048,256]{1,0:T(8,128)(2,1)}, u32[]{:S(2)}, u32[]{:S(2)}) collective-permute-start(bf16[2048,256]{1,0:T(8,128)(2,1)} %collective-permute-done.9.refs_2_), channel_id=1, source_target_pairs={{0,2},{2,0},{4,6},{6,4},{8,10},{10,8},{12,14},{14,12},{16,18},{18,... | collective-permute-start | bytes 3145736 | tf_op jit(solution)/shard_map/ppermute | solution.py:645
  359.8 10.1 %collective-permute-start.13 = (bf16[2048,256]{1,0:T(8,128)(2,1)}, bf16[2048,256]{1,0:T(8,128)(2,1)}, u32[]{:S(2)}, u32[]{:S(2)}) collective-permute-start(bf16[2048,256]{1,0:T(8,128)(2,1)} %collective-permute-done.12.refs_6_), channel_id=1, source_target_pairs={{0,2},{2,0},{4,6},{6,4},{8,10},{10,8},{12,14},{14,12},{16,18},{18,... | collective-permute-start | bytes 3145736 | tf_op jit(solution)/shard_map/ppermute | solution.py:645
  362.2 7.6 %collective-permute-start.11 = (bf16[2048,256]{1,0:T(8,128)(2,1)}, bf16[2048,256]{1,0:T(8,128)(2,1)}, u32[]{:S(2)}, u32[]{:S(2)}) collective-permute-start(bf16[2048,256]{1,0:T(8,128)(2,1)} %collective-permute-done.7.refs_4_), channel_id=1, source_target_pairs={{0,2},{2,0},{4,6},{6,4},{8,10},{10,8},{12,14},{14,12},{16,18},{18,... | collective-permute-start | bytes 3145736 | tf_op jit(solution)/shard_map/ppermute | solution.py:645
Sparse Core Ops, SparseCore 0:
  277.3 57.4 all-gather.2
